TPU v7x, 512 devices: a whole 4x4x16 slice. The times are simulated.
512 devices in a mesh: wide: 256 (over x, z, y), narrow: 2 (over core).
Axes of the slice: x: 4, y: 4, z: 16, core: 2. Of those that a mesh axis runs over, the one named last changes fastest.
Arguments:
- loads: bfloat16 [256, 2, 64, 1024], P('wide', 'narrow'), may hold values from -30 to 30
- flexibility: bfloat16 [256, 2, 1024, 1024], P('wide', 'narrow'), may hold values from -1 to 6
- dirichlet: bfloat16 [256, 2, 1024, 1024], P('wide', 'narrow'), may hold values from -1 to 6
- modes: bfloat16 [256, 2, 32, 1024], P('wide', 'narrow'), may hold values from -0.75 to 0.75
- coarse_inverse: bfloat16 [8192, 8192], P('wide', 'narrow'), may hold values from -1 to 4
- mode_counts: int32 [2, 256], replicated, may hold values from 1 to 32, 4096 in all within a row
Outputs:
- multipliers: bfloat16 [256, 2, 64, 1024], P('wide', 'narrow')
- residual: bfloat16 [256, 2, 64, 1024], P('wide', 'narrow')
Inputs may be any that keep to these rules, and one draw needn't show every extreme that they name: `mode_counts`: each row of this array is one grid column; the counts of each grid column sum to exactly 4096 in all, and the largest count of each grid column is exactly 32.
All inputs are finite; a program needn't handle non-finite values.
Results may differ from a plain program's by a relative error of at most 0.0087.
The roundings to bfloat16 on the way count: a program that leaves them out, or rounds other values in their place, can miss the bound.
Values may be sent and summed in bfloat16 or wider, within the bound.
No kernel may reach another device: no remote copies, remote signals or barrier semaphores. Data moves between devices by JAX's collectives and lax.ppermute only.
A program may use at most 64 MiB of HBM per device.

v0:
```python
import jax
import jax.numpy as jnp
from jax import lax
from jax.sharding import PartitionSpec as P

ITERS = 2


def extended(block, sides, width):
    for axis, dim in sides:
        count = lax.axis_size(axis)
        forward = [(i, i + 1) for i in range(count - 1)]
        backward = [(target, source) for source, target in forward]
        low = lax.ppermute(
            lax.slice_in_dim(block, block.shape[dim] - width, None, axis=dim), axis, forward
        )
        high = lax.ppermute(lax.slice_in_dim(block, 0, width, axis=dim), axis, backward)
        block = jnp.concatenate([low, block, high], axis=dim)
    return block


def jump_faces(values):
    load_count, width = values.shape
    face_len = width // 4
    face_parts = values.reshape(load_count, 4, face_len)
    north_face = face_parts[:, 0]
    south_face = face_parts[:, 1]
    west_face = face_parts[:, 2]
    east_face = face_parts[:, 3]
    layout = jnp.stack([jnp.stack([west_face, north_face]), jnp.stack([south_face, east_face])])
    padded = extended(layout, (("wide", 0), ("narrow", 1)), 1)
    from_above = padded[0, 1]
    from_below = padded[3, 2]
    from_west = padded[2, 0]
    from_east = padded[1, 3]
    nearby = jnp.stack([from_above, from_below, from_west, from_east], axis=1)
    return (face_parts.astype(jnp.float32) - nearby.astype(jnp.float32)).reshape(load_count, width)


def load_sums(left, right):
    return lax.psum(jnp.sum(left * right, axis=1), ("wide", "narrow"))


def shards(loads, flexibility, dirichlet, modes, coarse_inverse, mode_counts):
    local_loads = loads[0, 0]
    flex_block = flexibility[0, 0]
    precond_block = dirichlet[0, 0]
    mode_block = modes[0, 0]
    mode_slots = mode_block.shape[0]
    column_width = coarse_inverse.shape[1]
    row_total = lax.axis_size("wide")
    coarse_order = coarse_inverse.shape[0] * row_total
    row_index = lax.axis_index("wide")
    column = lax.axis_index("narrow")
    counts = lax.dynamic_index_in_dim(mode_counts, column, 0, keepdims=False)
    end_points = jnp.cumsum(counts)
    starts = end_points - counts
    position = jnp.arange(column_width, dtype=jnp.int32)
    owner_row = jnp.sum((end_points[None, :] <= position[:, None]).astype(jnp.int32), axis=1)
    slot_index = owner_row * mode_slots + position - jnp.take(starts, owner_row)
    rank_list = jnp.arange(mode_slots, dtype=jnp.int32)
    own_index = jnp.minimum(
        column * column_width + jnp.take(starts, row_index) + rank_list, coarse_order - 1
    )
    is_valid = rank_list < jnp.take(counts, row_index)

    def coarse_term(rounded):
        weights = lax.dot_general(
            rounded, mode_block, (((1,), (1,)), ((), ())), preferred_element_type=jnp.float32
        ).astype(jnp.bfloat16)
        padded = lax.all_gather(weights, "wide", axis=1, tiled=True)
        column_values = jnp.take(padded, slot_index, axis=1)
        partial_values = lax.dot_general(
            column_values,
            coarse_inverse,
            (((1,), (1,)), ((), ())),
            preferred_element_type=jnp.float32,
        )
        block_values = lax.psum(partial_values, "narrow").astype(jnp.bfloat16)
        coarse_values = lax.all_gather(block_values, "wide", axis=1, tiled=True)
        picked = jnp.take(coarse_values, own_index, axis=1)
        picked = jnp.where(is_valid[None, :], picked, jnp.zeros_like(picked))
        return jnp.dot(picked, mode_block, preferred_element_type=jnp.float32)

    def precondition(values):
        rounded = values.astype(jnp.bfloat16)
        inner = jump_faces(rounded).astype(jnp.bfloat16)
        smoothed = jnp.dot(inner, precond_block, preferred_element_type=jnp.float32).astype(
            jnp.bfloat16
        )
        return jump_faces(smoothed) + coarse_term(rounded)

    disp = jnp.dot(local_loads, flex_block, preferred_element_type=jnp.float32).astype(jnp.bfloat16)
    residual = jump_faces(disp)
    multipliers = jnp.zeros_like(residual)
    direction = precondition(residual)
    energy = load_sums(residual, direction)
    for step_number in range(ITERS):
        moved = jump_faces(direction.astype(jnp.bfloat16)).astype(jnp.bfloat16)
        image = jump_faces(
            jnp.dot(moved, flex_block, preferred_element_type=jnp.float32).astype(jnp.bfloat16)
        )
        step_size = energy / load_sums(direction, image)
        multipliers = multipliers + step_size[:, None] * direction
        residual = residual - step_size[:, None] * image
        if step_number + 1 < ITERS:
            fresh_z = precondition(residual)
            fresh = load_sums(residual, fresh_z)
            direction = fresh_z + (fresh / energy)[:, None] * direction
            energy = fresh
    return (multipliers.astype(jnp.bfloat16)[None, None], residual.astype(jnp.bfloat16)[None, None])


def solution(mesh):
    return jax.shard_map(
        shards,
        mesh=mesh,
        in_specs=(
            P("wide", "narrow", None, None),
            P("wide", "narrow", None, None),
            P("wide", "narrow", None, None),
            P("wide", "narrow", None, None),
            P("wide", "narrow"),
            P(),
        ),
        out_specs=(P("wide", "narrow", None, None), P("wide", "narrow", None, None)),
        check_vma=False,
    )
```

profile of v0, /device:TPU:1, one launch (start us, length us, event | category | flops | bytes accessed | tf_op | source)
XLA Modules:
  0.0 1263.8 jit_solution(416215307938295492)
XLA Ops:
  11.8 4.7 collective-permute-start
  17.8 25.7 %gather_fusion = s32[4096]{0:T(1024)S(1)} fusion(s32[256]{0:T(256)S(1)} %get-tuple-element.32, s32[4096]{0:T(1024)S(1)} %broadcast_clamp_fusion.1), kind=kCustom, calls=%fused_computation.4 | custom fusion | bytes 49152 | tf_op jit(solution)/shard_map/jit(_take)/gather | solution.py:60
  45.0 8.7 collective-permute-start.3
  59.7 4.0 collective-permute-start.4
  70.9 171.3 %all-gather.5.cloned.1.call-done = bf16[64,8192]{0,1:T(8,128)(2,1)} async-done(((bf16[64,32]{0,1:T(8,128)(2,1)}), bf16[64,8192]{0,1:T(8,128)(2,1)}) %all-gather.5.cloned.1.call-update) | async-done | bytes 1048592 | tf_op jit(solution)/shard_map/all_gather | solution.py:71
  242.2 16.2 %gather_fusion.1 = bf16[4096,64]{1,0:T(8,128)(2,1)} fusion(bf16[64,8192]{0,1:T(8,128)(2,1)} %all-gather.5.cloned.1.call-done, s32[4096]{0:T(1024)S(1)} %broadcast_clamp_fusion), kind=kCustom, calls=%fused_computation.clone | custom fusion | bytes 1064960 | tf_op jit(solution)/shard_map/jit(_take)/gather | solution.py:72
  260.4 15.1 %psum.42 = bf16[64,32]{0,1:T(8,128)(2,1)} all-reduce(f32[64,32]{0,1:T(8,128)S(1)} %fusion.27), channel_id=1, replica_groups=mesh['wide'=256,'narrow'=2] {'narrow'}, use_global_device_ids=true, to_apply=%region_3.5 | all-reduce | flops 2048 | bytes 12288 | tf_op jit(solution)/shard_map/psum | solution.py:79
  279.3 4.0 collective-permute-start.8
  290.2 166.6 %all-gather.7.cloned.1.call-done = bf16[64,8192]{0,1:T(8,128)(2,1)} async-done(((bf16[64,32]{0,1:T(8,128)(2,1)}), bf16[64,8192]{0,1:T(8,128)(2,1)}) %all-gather.7.cloned.1.call-update) | async-done | bytes 1048592 | tf_op jit(solution)/shard_map/all_gather | solution.py:80
  461.3 4.0 collective-permute-start.12
  467.9 14.6 %collective-permute-start.15 = (bf16[4,1,64,256]{3,2,1,0:T(8,128)(2,1)S(1)}, bf16[4,1,64,256]{3,2,1,0:T(8,128)(2,1)S(1)}, u32[]{:S(2)}, u32[]{:S(2)}) collective-permute-start(bf16[4,1,64,256]{3,2,1,0:T(8,128)(2,1)S(1)} %get-tuple-element.45), channel_id=1, source_target_pairs={{1,0},{3,2},{5,4},{7,6},{9,8},{11,10},{13,12},{15,14},{17,16},{19,... | collective-permute-start | bytes 393224 | tf_op jit(solution)/shard_map/ppermute | solution.py:17
  485.7 4.6 collective-permute-start.16
  497.3 112.4 %all-reduce = (f32[64]{0:T(128)S(1)}, f32[64]{0:T(128)S(1)}) all-reduce(f32[64]{0:T(128)S(1)} %get-tuple-element.27, f32[64]{0:T(128)S(1)} %get-tuple-element.26), channel_id=1, replica_groups=mesh['wide'=256,'narrow'=2] {'wide','narrow'}, use_global_device_ids=true, to_apply=%region_5.8 | all-reduce | flops 128 | bytes 1024 | tf_op jit(solution)/shard_map/psum | solution.py:41
  614.2 4.0 collective-permute-start.20
  620.8 3.7 collective-permute-start.23
  625.6 164.7 %all-gather.9.cloned.1.call-done = bf16[64,8192]{0,1:T(8,128)(2,1)} async-done(((bf16[64,32]{0,1:T(8,128)(2,1)}), bf16[64,8192]{0,1:T(8,128)(2,1)}) %all-gather.9.cloned.1.call-update) | async-done | bytes 1048592 | tf_op jit(solution)/shard_map/all_gather | solution.py:71
  790.3 16.2 %gather_fusion.3 = bf16[4096,64]{1,0:T(8,128)(2,1)} fusion(bf16[64,8192]{0,1:T(8,128)(2,1)} %all-gather.9.cloned.1.call-done, s32[4096]{0:T(1024)S(1)} %broadcast_clamp_fusion), kind=kCustom, calls=%fused_computation.2.clone | custom fusion | bytes 1064960 | tf_op jit(solution)/shard_map/jit(_take)/gather | solution.py:72
  808.5 15.1 %psum.45 = bf16[64,32]{0,1:T(8,128)(2,1)} all-reduce(f32[64,32]{0,1:T(8,128)S(1)} %fusion.25), channel_id=1, replica_groups=mesh['wide'=256,'narrow'=2] {'narrow'}, use_global_device_ids=true, to_apply=%region_8.11 | all-reduce | flops 2048 | bytes 12288 | tf_op jit(solution)/shard_map/psum | solution.py:79
  827.4 4.0 collective-permute-start.24
  838.5 166.5 %all-gather.11.cloned.1.call-done = bf16[64,8192]{0,1:T(8,128)(2,1)} async-done(((bf16[64,32]{0,1:T(8,128)(2,1)}), bf16[64,8192]{0,1:T(8,128)(2,1)}) %all-gather.11.cloned.1.call-update) | async-done | bytes 1048592 | tf_op jit(solution)/shard_map/all_gather | solution.py:80
  1008.0 111.3 %psum.46 = f32[64]{0:T(128)S(1)} all-reduce(f32[64]{0:T(128)S(1)} %get-tuple-element.92), channel_id=1, replica_groups=mesh['wide'=256,'narrow'=2] {'wide','narrow'}, use_global_device_ids=true, to_apply=%region_10.13 | all-reduce | flops 64 | bytes 512 | tf_op jit(solution)/shard_map/psum | solution.py:41
  1121.1 4.0 collective-permute-start.28
  1134.7 4.6 collective-permute-start.32
  1146.3 110.1 %psum.47 = f32[64]{0:T(128)S(1)} all-reduce(f32[64]{0:T(128)S(1)} %multiply_reduce_fusion), channel_id=1, replica_groups=mesh['wide'=256,'narrow'=2] {'wide','narrow'}, use_global_device_ids=true, to_apply=%region_12.15 | all-reduce | flops 64 | bytes 512 | tf_op jit(solution)/shard_map/psum | solution.py:41
  (282 shorter events, 91.1 us)
Async XLA Ops:
  7.2 235.0 %all-gather.5.cloned.1.call-start = ((), (), s32[]{:S(2)}) async-start(), calls=%async_computation | async-start | bytes 2105344 | tf_op jit(solution)/shard_map/all_gather | solution.py:71
  10.5 33.1 %collective-permute-start.1 = (bf16[1,2,64,256]{3,2,1,0:T(8,128)(2,1)S(1)}, bf16[1,2,64,256]{3,2,1,0:T(8,128)(2,1)S(1)}, u32[]{:S(2)}, u32[]{:S(2)}) collective-permute-start(bf16[1,2,64,256]{3,2,1,0:T(8,128)(2,1)S(1)} %maximum_bitcast_fusion.1), channel_id=1, source_target_pairs={{2,0},{4,2},{6,4},{8,6},{10,8},{12,10},{14,12},{16,14},{18,16},{20... | collective-permute-start | bytes 196616 | tf_op jit(solution)/shard_map/ppermute | solution.py:17
  11.8 31.8 %collective-permute-start = (bf16[1,2,64,256]{3,2,1,0:T(8,128)(2,1)S(1)}, bf16[1,2,64,256]{3,2,1,0:T(8,128)(2,1)S(1)}, u32[]{:S(2)}, u32[]{:S(2)}) collective-permute-start(bf16[1,2,64,256]{3,2,1,0:T(8,128)(2,1)S(1)} %maximum_bitcast_fusion), channel_id=1, source_target_pairs={{0,2},{2,4},{4,6},{6,8},{8,10},{10,12},{12,14},{14,16},{16,18},{18... | collective-permute-start | bytes 196616 | tf_op jit(solution)/shard_map/ppermute | solution.py:14
  43.7 10.0 collective-permute-start.2
  45.0 9.6 collective-permute-start.3
  55.5 401.4 %all-gather.7.cloned.1.call-start = ((), (), s32[]{:S(2)}) async-start(), calls=%async_computation.1 | async-start | bytes 2105344 | tf_op jit(solution)/shard_map/all_gather | solution.py:80
  58.4 5.3 collective-permute-start.5
  59.7 5.3 collective-permute-start.4
  275.5 514.9 %all-gather.9.cloned.1.call-start = ((), (), s32[]{:S(2)}) async-start(), calls=%async_computation.2 | async-start | bytes 2105344 | tf_op jit(solution)/shard_map/all_gather | solution.py:71
  277.9 5.4 collective-permute-start.9
  279.3 5.3 collective-permute-start.8
  459.9 5.3 collective-permute-start.13
  461.3 5.3 collective-permute-start.12
  466.6 15.9 %collective-permute-start.14 = (bf16[4,1,64,256]{3,2,1,0:T(8,128)(2,1)S(1)}, bf16[4,1,64,256]{3,2,1,0:T(8,128)(2,1)S(1)}, u32[]{:S(2)}, u32[]{:S(2)}) collective-permute-start(bf16[4,1,64,256]{3,2,1,0:T(8,128)(2,1)S(1)} %get-tuple-element.44), channel_id=1, source_target_pairs={{0,1},{2,3},{4,5},{6,7},{8,9},{10,11},{12,13},{14,15},{16,17},{18,... | collective-permute-start | bytes 393224 | tf_op jit(solution)/shard_map/ppermute | solution.py:14
  467.9 15.6 %collective-permute-start.15 = (bf16[4,1,64,256]{3,2,1,0:T(8,128)(2,1)S(1)}, bf16[4,1,64,256]{3,2,1,0:T(8,128)(2,1)S(1)}, u32[]{:S(2)}, u32[]{:S(2)}) collective-permute-start(bf16[4,1,64,256]{3,2,1,0:T(8,128)(2,1)S(1)} %get-tuple-element.45), channel_id=1, source_target_pairs={{1,0},{3,2},{5,4},{7,6},{9,8},{11,10},{13,12},{15,14},{17,16},{19,... | collective-permute-start | bytes 393224 | tf_op jit(solution)/shard_map/ppermute | solution.py:17
  484.4 6.1 collective-permute-start.17
  485.7 5.9 collective-permute-start.16
  612.4 392.5 %all-gather.11.cloned.1.call-start = ((), (), s32[]{:S(2)}) async-start(), calls=%async_computation.3 | async-start | bytes 2105344 | tf_op jit(solution)/shard_map/all_gather | solution.py:80
  612.9 5.3 collective-permute-start.21
  614.2 5.3 collective-permute-start.20
  826.1 5.4 collective-permute-start.25
  1119.8 5.3 collective-permute-start.29
  1133.4 6.1 collective-permute-start.33
  1134.7 5.9 collective-permute-start.32
  (33 other events, 2557.9 us)
Sparse Core Ops, SparseCore 0:
  55.6 186.5 all-gather.4
  275.6 181.1 all-gather.6
  612.6 177.7 all-gather.8
  823.7 181.2 all-gather.10
where the time goes:
time: 1270 us; the launch traced here: 1260 us
  waiting for transfers between devices  688 us (54%)
  blocking collectives  364 us (29%)
  starting transfers between devices  108 us (9%)
  local copies, waits for them, and re-layouts  70.2 us (6%)
  between operations  16.7 us (1%)
  matrix products  13.5 us (1%)
    all_gather x2, waiting for transfers between devices, coarse_term(): padded = lax.all_gather(weights, 'wide', axis=1, tiled=True)  336 us
    psum x3, blocking collectives, load_sums(): return lax.psum(jnp.sum(left * right, axis=1), ('wide', 'narrow'))  334 us
    all_gather x2, waiting for transfers between devices, coarse_term(): coarse_values = lax.all_gather(block_values, 'wide', axis=1, tiled=True)  333 us
    ppermute x18, starting transfers between devices, extended(): lax.ppermute(lax.slice_in_dim(block, 0, width, axis=dim), axis, backward)  58.4 us
    ppermute x18, starting transfers between devices, extended(): lax.ppermute(lax.slice_in_dim(block, block.shape[dim] - width, None, axis...  49.6 us
    gather x2, local copies, waits for them, and re-layouts, coarse_term(): column_values = jnp.take(padded, slot_index, axis=1)  32.3 us
    psum x2, blocking collectives, coarse_term(): block_values = lax.psum(partial_values, 'narrow').astype(jnp.bfloat16)  30.1 us
    gather x1, local copies, waits for them, and re-layouts, shards(): slot_index = owner_row * mode_slots + position - jnp.take(starts, owner_row)  25.7 us
  transfers between devices with their start and end apart: 40, of which 24 were waited for; matrix products, arithmetic and copies ran while one was open for 3% of the time, Pallas kernels for 0%

commit v1 on v0

v1 whole, which is shorter than its diff:
```python
import jax
import jax.numpy as jnp
from jax import lax
from jax.experimental import pallas as pl
from jax.experimental.pallas import tpu as pltpu
from jax.sharding import Mesh, PartitionSpec as P

ITERS = 2
XYZ = (4, 16, 4)
WIDE = ("x", "z", "y")
INTERPRET = False


def spread(values, axes):
    count = lax.axis_size(axes)
    copies = jnp.broadcast_to(values[None], (count,) + values.shape)
    return lax.all_to_all(copies, axes, 0, 0, tiled=False)


def gather_blocks(block):
    stage = spread(block, "z")
    stage = spread(stage, ("x", "y"))
    return stage.reshape((-1,) + block.shape)


def total(partial):
    stage = jnp.sum(spread(partial, ("x", "y", "c")), axis=0)
    return jnp.sum(spread(stage, "z"), axis=0)


def neighbours(values):
    load_count, width = values.shape
    face = width // 4
    rows = lax.axis_size(WIDE)
    column = lax.axis_index("c")
    down = [(i, i + 1) for i in range(rows - 1)]
    up = [(i + 1, i) for i in range(rows - 1)]
    north, south, west, east = (values[:, k * face : (k + 1) * face] for k in range(4))
    from_above = lax.ppermute(south, WIDE, down)
    from_below = lax.ppermute(north, WIDE, up)
    side = lax.ppermute(jnp.where(column == 0, east, west), "c", [(0, 1), (1, 0)])
    nothing = jnp.zeros_like(side)
    from_west = jnp.where(column == 1, side, nothing)
    from_east = jnp.where(column == 0, side, nothing)
    return jnp.concatenate([from_above, from_below, from_west, from_east], axis=1)


def jump(values):
    return values.astype(jnp.float32) - neighbours(values).astype(jnp.float32)


def pack(wide_rows):
    half = wide_rows.shape[0] // 2
    return jnp.concatenate([wide_rows[:half], wide_rows[half:]], axis=1)


def pad_kernel(first_ref, source_ref, block_ref, out_ref):
    rows, columns = block_ref.shape
    window = min(384, columns)
    chunks = out_ref.shape[1] // 128
    position = lax.broadcasted_iota(jnp.int32, (window, 128), 0)

    def step(chunk, carry):
        low = pl.multiple_of(first_ref[chunk] * 128, 128)
        part = block_ref[:, pl.ds(low, window)]
        target = pl.multiple_of(chunk * 128, 128)
        for half in range(2):
            hot = jnp.where(position == source_ref[half, chunk] - low, 1.0, 0.0).astype(jnp.bfloat16)
            chosen = jnp.dot(part, hot, preferred_element_type=jnp.float32)
            out_ref[half * rows : (half + 1) * rows, pl.ds(target, 128)] = chosen.astype(jnp.bfloat16)
        return carry

    lax.fori_loop(0, chunks, step, 0)


def padded_inverse(block, starts, counts):
    rows, columns = block.shape
    subdomains = counts.shape[0]
    slots = 32
    half_slots = slots // 2
    rank = jnp.arange(slots, dtype=jnp.int32)
    source = jnp.where(rank[None, :] < counts[:, None], starts[:, None] + rank[None, :], -1)
    chunks = subdomains * half_slots // 128
    source = source.reshape(subdomains, 2, half_slots).transpose(1, 0, 2).reshape(2, chunks, 1, 128)
    window = min(384, columns)
    first = jnp.minimum(starts.reshape(chunks, -1)[:, 0] // 128, (columns - window) // 128)
    return pl.pallas_call(
        pad_kernel,
        out_shape=jax.ShapeDtypeStruct((2 * rows, subdomains * half_slots), jnp.bfloat16),
        in_specs=[
            pl.BlockSpec(memory_space=pltpu.SMEM),
            pl.BlockSpec(memory_space=pltpu.VMEM),
            pl.BlockSpec(memory_space=pltpu.VMEM),
        ],
        out_specs=pl.BlockSpec(memory_space=pltpu.VMEM),
        interpret=INTERPRET,
        name="pad_inverse",
    )(first, source, block)


def product_kernel(padded_ref, blocks_ref, out_ref):
    nx, nz, ny = XYZ
    rows = padded_ref.shape[0] // 2
    length = nz * ny * blocks_ref.shape[1]
    result = jnp.zeros((2 * rows, 128), jnp.float32)
    for x in range(nx):
        order = [x * ny * nz + y * nz + z for z in range(nz) for y in range(ny)]
        part = jnp.concatenate([blocks_ref[p] for p in order], axis=0)
        result += jnp.dot(
            padded_ref[:, x * length : (x + 1) * length], part, preferred_element_type=jnp.float32
        )
    joined = result[:rows] + pltpu.roll(result[rows:], 64, 1)
    lane = lax.broadcasted_iota(jnp.int32, (rows // 2, 128), 1)
    out_ref[...] = jnp.where(lane < 64, joined[: rows // 2], pltpu.roll(joined[rows // 2 :], 64, 1))


def coarse_product(padded, blocks):
    return pl.pallas_call(
        product_kernel,
        out_shape=jax.ShapeDtypeStruct((padded.shape[0] // 4, 128), jnp.float32),
        interpret=INTERPRET,
        name="coarse_product",
    )(padded, blocks)


def lift_kernel(info_ref, low_ref, high_ref, modes_ref, out_ref):
    slots = modes_ref.shape[0]
    window = jnp.concatenate([low_ref[0], high_ref[0]], axis=0)
    rank = lax.broadcasted_iota(jnp.int32, (slots, slots), 0)
    column = lax.broadcasted_iota(jnp.int32, (slots, slots), 1)
    offset = info_ref[2] + rank
    row = (offset // 32) * 16 + offset % 16
    half = (offset // 16) % 2
    hit = jnp.logical_and(row == column, rank < info_ref[3])
    first = jnp.where(jnp.logical_and(hit, half == 0), 1.0, 0.0).astype(jnp.bfloat16)
    second = jnp.where(jnp.logical_and(hit, half == 1), 1.0, 0.0).astype(jnp.bfloat16)
    picked = jnp.dot(first, window, preferred_element_type=jnp.float32) + pltpu.roll(
        jnp.dot(second, window, preferred_element_type=jnp.float32), 64, 1
    )
    lifted = lax.dot_general(
        picked.astype(jnp.bfloat16),
        modes_ref[...],
        (((0,), (0,)), ((), ())),
        preferred_element_type=jnp.float32,
    )
    out_ref[...] = lifted[: out_ref.shape[0]]


def lift(info, blocks, modes):
    half_slots = blocks.shape[1]
    load_count = 64
    width = modes.shape[1]
    return pl.pallas_call(
        lift_kernel,
        out_shape=jax.ShapeDtypeStruct((load_count, width), jnp.float32),
        grid_spec=pltpu.PrefetchScalarGridSpec(
            num_scalar_prefetch=1,
            grid=(1,),
            in_specs=[
                pl.BlockSpec((1, half_slots, 128), lambda i, info: (info[0], 0, 0)),
                pl.BlockSpec((1, half_slots, 128), lambda i, info: (info[1], 0, 0)),
                pl.BlockSpec(modes.shape, lambda i, info: (0, 0)),
            ],
            out_specs=pl.BlockSpec((load_count, width), lambda i, info: (0, 0)),
        ),
        interpret=INTERPRET,
        name="lift",
    )(info, blocks, blocks, modes)


def shards(loads, flexibility, dirichlet, modes, coarse_inverse, mode_counts):
    local_loads = loads[0, 0]
    flex_block = flexibility[0, 0]
    precond_block = dirichlet[0, 0]
    mode_block = modes[0, 0]
    nx, nz, ny = XYZ
    rows = lax.axis_size(WIDE)
    row = lax.axis_index(WIDE)
    column = lax.axis_index("c")
    column_width = coarse_inverse.shape[1]
    width = local_loads.shape[1]
    face = width // 4

    counts = lax.dynamic_index_in_dim(mode_counts, column, 0, keepdims=False)
    ends = jnp.cumsum(counts)
    starts = ends - counts
    padded = padded_inverse(coarse_inverse, starts, counts)

    own_start = lax.dynamic_index_in_dim(starts, row, 0, keepdims=False)
    own_count = lax.dynamic_index_in_dim(counts, row, 0, keepdims=False)
    base = column * column_width + own_start
    owner = jnp.minimum(base // 32, rows - 2)

    def place(chip):
        return (chip // (ny * nz)) * (ny * nz) + (chip % ny) * nz + (chip // ny) % nz

    info = jnp.stack([place(owner), place(owner + 1), base - 32 * owner, own_count])

    doubled = jnp.stack([row > 0, row < rows - 1, column == 1, column == 0])
    factor = jnp.repeat(jnp.where(doubled, 2.0, 1.0), face)[None, :]

    def precondition(rounded):
        weights = lax.dot_general(
            mode_block, rounded, (((1,), (1,)), ((), ())), preferred_element_type=jnp.float32
        ).astype(jnp.bfloat16)
        inner = (rounded.astype(jnp.float32) * factor).astype(jnp.bfloat16)
        smoothed = jnp.dot(inner, precond_block, preferred_element_type=jnp.float32).astype(
            jnp.bfloat16
        )
        local = jump(smoothed)
        partial = coarse_product(padded, gather_blocks(pack(weights)))
        partner = lax.ppermute(partial, "c", [(0, 1), (1, 0)])
        values = gather_blocks((partial + partner).astype(jnp.bfloat16))
        return local + lift(info, values, mode_block)

    disp = jnp.dot(local_loads, flex_block, preferred_element_type=jnp.float32).astype(jnp.bfloat16)
    residual = jump(disp)
    direction = precondition(residual.astype(jnp.bfloat16))
    energy = None
    multipliers = None
    for step_number in range(ITERS):
        moved = jump(direction.astype(jnp.bfloat16)).astype(jnp.bfloat16)
        image = jump(
            jnp.dot(moved, flex_block, preferred_element_type=jnp.float32).astype(jnp.bfloat16)
        )
        curvature = jnp.sum(direction * image, axis=1)
        if energy is None:
            both = jnp.concatenate([jnp.sum(residual * direction, axis=1), curvature])
            both = total(both[None, :])[0]
            energy, curvature = both[:64], both[64:]
        else:
            curvature = total(curvature[None, :])[0]
        size = (energy / curvature)[:, None]
        multipliers = size * direction if multipliers is None else multipliers + size * direction
        residual = residual - size * image
        if step_number + 1 < ITERS:
            fresh_z = precondition(residual.astype(jnp.bfloat16))
            fresh = total(jnp.sum(residual * fresh_z, axis=1)[None, :])[0]
            direction = fresh_z + (fresh / energy)[:, None] * direction
            energy = fresh
    return (multipliers.astype(jnp.bfloat16)[None, None], residual.astype(jnp.bfloat16)[None, None])


def solution(mesh):
    split = Mesh(mesh.devices.reshape(XYZ + (2,)), WIDE + ("c",))
    blocks = P(WIDE, "c", None, None)
    return jax.shard_map(
        shards,
        mesh=split,
        in_specs=(blocks, blocks, blocks, blocks, P(WIDE, "c"), P()),
        out_specs=(blocks, blocks),
        check_vma=False,
    )
```

time: 1270 us -> 356 us (0.28)
  waiting for transfers between devices: 688 us -> 42.6 us
  blocking collectives: 364 us -> 152 us
  local copies, waits for them, and re-layouts: 70.2 us -> 16.4 us
  Pallas kernels: 0 us -> 17.2 us
  between operations: 16.7 us -> 2.15 us
    all_gather x4 -> x0, waiting for transfers between devices: 669 us -> none  [the longest x2 336 us: coarse_term(): padded = lax.all_gather(weights, 'wide', axis=1, tiled=True)]
    psum x5 -> x0, blocking collectives: 364 us -> none  [the longest x3 334 us: load_sums(): return lax.psum(jnp.sum(left * right, axis=1), ('wide', 'narrow'))]
    all_to_all x0 -> x9, blocking collectives: none -> 152 us  [spread(): return lax.all_to_all(copies, axes, 0, 0, tiled=False)]
    gather x5 -> x0, local copies, waits for them, and re-layouts: 63.1 us -> none  [the longest x2 32.3 us: coarse_term(): column_values = jnp.take(padded, slot_index, axis=1)]
    ppermute x36 -> x23, starting transfers between devices: 108 us -> 72.4 us  [the longest x7 32 us: neighbours(): lax.ppermute(jnp.where(column == 0, east, west), 'c', [(0, 1), (1, 0)])]
    all_to_all x0 -> x5, starting transfers between devices: none -> 31.4 us  [spread(): return lax.all_to_all(copies, axes, 0, 0, tiled=False)]
    all_to_all x0 -> x5, waiting for transfers between devices: none -> 23.9 us  [spread(): return lax.all_to_all(copies, axes, 0, 0, tiled=False)]
    pallas_call x0 -> x5, Pallas kernels: none -> 17.2 us  [the longest x1 6.95 us: padded_inverse(): pl.pallas_call(pad_kernel, out_shape=jax.ShapeDtypeStruct((2 * rows, subd...]
  transfers between devices with their start and end apart: 40 -> 28, of which waited for: 24 -> 11; matrix products, arithmetic and copies ran while one was open for 3% -> 5% of each run, Pallas kernels for 0% -> 3%
where the time goes in v1:
time: 356 us; the launch traced here: 354 us
  blocking collectives  152 us (43%)
  starting transfers between devices  104 us (29%)
  waiting for transfers between devices  42.6 us (12%)
  Pallas kernels  17.2 us (5%)
  local copies, waits for them, and re-layouts  16.4 us (5%)
  other arithmetic  12.9 us (4%)
  matrix products  6.78 us (2%)
    all_to_all x9, blocking collectives, spread(): return lax.all_to_all(copies, axes, 0, 0, tiled=False)  152 us
    ppermute x7, starting transfers between devices, neighbours(): lax.ppermute(jnp.where(column == 0, east, west), 'c', [(0, 1), (1, 0)])  32 us
    all_to_all x5, starting transfers between devices, spread(): return lax.all_to_all(copies, axes, 0, 0, tiled=False)  31.4 us
    all_to_all x5, waiting for transfers between devices, spread(): return lax.all_to_all(copies, axes, 0, 0, tiled=False)  23.9 us
    ppermute x7, starting transfers between devices, neighbours(): from_above = lax.ppermute(south, WIDE, down)  18.4 us
    ppermute x7, waiting for transfers between devices, neighbours(): from_below = lax.ppermute(north, WIDE, up)  16.7 us
    ppermute x2, starting transfers between devices, precondition(): partner = lax.ppermute(partial, 'c', [(0, 1), (1, 0)])  12.9 us
    ppermute x7, starting transfers between devices, neighbours(): from_below = lax.ppermute(north, WIDE, up)  9.02 us
  transfers between devices with their start and end apart: 28, of which 11 were waited for; matrix products, arithmetic and copies ran while one was open for 5% of the time, Pallas kernels for 3%

profile of v1, /device:TPU:1, one launch (start us, length us, event | category | flops | bytes accessed | tf_op | source)
XLA Modules:
  0.0 354.2 jit_solution(358968267117210957)
XLA Ops:
  3.6 8.7 %collective-permute-start.2 = (bf16[64,256]{1,0:T(8,128)(2,1)S(1)}, bf16[64,256]{1,0:T(8,128)(2,1)S(1)}, u32[]{:S(2)}, u32[]{:S(2)}) collective-permute-start(bf16[64,256]{1,0:T(8,128)(2,1)S(1)} %get-tuple-element.29), channel_id=1, source_target_pairs={{0,1},{1,0},{2,3},{3,2},{4,5},{5,4},{6,7},{7,6},{8,9},{9,8},{10,11... | collective-permute-start | bytes 98312 | tf_op jit(solution)/shard_map/ppermute | solution.py:41
  19.3 13.2 %all-to-all-start = ((bf16[16,16,128]{2,1,0:T(8,128)(2,1)}), bf16[16,16,128]{2,1,0:T(8,128)(2,1)S(1)}, u32[]{:S(2)}, u32[]{:S(2)}) async-start(bf16[16,16,128]{2,1,0:T(8,128)(2,1)} %broadcast_in_dim.50), calls=%async_computation | async-start | bytes 131072 | tf_op jit(solution)/shard_map/all_to_all | solution.py:17
  34.3 9.8 %all-to-all-done = bf16[16,16,128]{2,1,0:T(8,128)(2,1)S(1)} async-done(((bf16[16,16,128]{2,1,0:T(8,128)(2,1)}), bf16[16,16,128]{2,1,0:T(8,128)(2,1)S(1)}, u32[]{:S(2)}, u32[]{:S(2)}) %all-to-all-start) | async-done | bytes 65568 | tf_op jit(solution)/shard_map/all_to_all | solution.py:17
  45.3 6.8 %all-to-all-start.1 = ((bf16[16,16,16,128]{3,2,1,0:T(8,128)(2,1)}), bf16[16,16,16,128]{3,2,1,0:T(8,128)(2,1)S(1)}, u32[]{:S(2)}, u32[]{:S(2)}) async-start(bf16[16,16,16,128]{3,2,1,0:T(8,128)(2,1)} %broadcast_in_dim.51), calls=%async_computation.1 | async-start | bytes 2097152 | tf_op jit(solution)/shard_map/all_to_all | solution.py:17
  57.3 6.9 %pad_inverse.1.padded_ref = bf16[64,4096]{1,0:T(8,128)(2,1)} custom-call(s32[32]{0:T(128)} %fusion.51.first_ref, s32[2,32,1,128]{3,2,1,0:T(1,128)} %compare_select_fusion.source_ref, bf16[32,4096]{1,0:T(8,128)(2,1)} %block_ref.1), custom_call_target="tpu_custom_call" | custom-call | tf_op jit(solution)/shard_map/pad_inverse/pallas_call | solution.py:87
  69.4 6.4 %collective-permute-start.6 = (f32[16,128]{1,0:T(8,128)}, f32[16,128]{1,0:T(8,128)S(1)}, u32[]{:S(2)}, u32[]{:S(2)}) collective-permute-start(f32[16,128]{1,0:T(8,128)} %coarse_product.2), channel_id=1, source_target_pairs={{0,1},{1,0},{2,3},{3,2},{4,5},{5,4},{6,7},{7,6},{8,9},{9,8},{10,11... | collective-permute-start | bytes 24584 | tf_op jit(solution)/shard_map/ppermute | solution.py:212
  83.3 10.0 %all-to-all-done.2 = bf16[16,16,128]{2,1,0:T(8,128)(2,1)S(1)} async-done(((bf16[16,16,128]{2,1,0:T(8,128)(2,1)}), bf16[16,16,128]{2,1,0:T(8,128)(2,1)S(1)}, u32[]{:S(2)}, u32[]{:S(2)}) %all-to-all-start.2) | async-done | bytes 65568 | tf_op jit(solution)/shard_map/all_to_all | solution.py:17
  94.5 4.3 %all-to-all-start.3 = ((bf16[16,16,16,128]{3,2,1,0:T(8,128)(2,1)}), bf16[16,16,16,128]{3,2,1,0:T(8,128)(2,1)S(1)}, u32[]{:S(2)}, u32[]{:S(2)}) async-start(bf16[16,16,16,128]{3,2,1,0:T(8,128)(2,1)} %broadcast_in_dim.53), calls=%async_computation.3 | async-start | bytes 2097152 | tf_op jit(solution)/shard_map/all_to_all | solution.py:17
  102.9 4.1 %collective-permute-start.5 = (bf16[64,256]{1,0:T(8,128)(2,1)S(1)}, bf16[64,256]{1,0:T(8,128)(2,1)S(1)}, u32[]{:S(2)}, u32[]{:S(2)}) collective-permute-start(bf16[64,256]{1,0:T(8,128)(2,1)S(1)} %get-tuple-element.26), channel_id=1, source_target_pairs={{0,1},{1,0},{2,3},{3,2},{4,5},{5,4},{6,7},{7,6},{8,9},{9,8},{10,11... | collective-permute-start | bytes 98312 | tf_op jit(solution)/shard_map/ppermute | solution.py:41
  108.4 4.2 %collective-permute-start.3 = (bf16[64,256]{1,0:T(8,128)(2,1)}, bf16[64,256]{1,0:T(8,128)(2,1)}, u32[]{:S(2)}, u32[]{:S(2)}) collective-permute-start(bf16[64,256]{1,0:T(8,128)(2,1)} %get-tuple-element.25), channel_id=1, source_target_pairs={{0,2},{2,4},{4,6},{6,8},{8,10},{10,12},{12,14},{14,16},{16,18},{18... | collective-permute-start | bytes 98312 | tf_op jit(solution)/shard_map/ppermute | solution.py:39
  119.2 4.4 %collective-permute-start.9 = (bf16[64,256]{1,0:T(8,128)(2,1)S(1)}, bf16[64,256]{1,0:T(8,128)(2,1)S(1)}, u32[]{:S(2)}, u32[]{:S(2)}) collective-permute-start(bf16[64,256]{1,0:T(8,128)(2,1)S(1)} %get-tuple-element.23), channel_id=1, source_target_pairs={{0,1},{1,0},{2,3},{3,2},{4,5},{5,4},{6,7},{7,6},{8,9},{9,8},{10,11... | collective-permute-start | bytes 98312 | tf_op jit(solution)/shard_map/ppermute | solution.py:41
  141.8 21.9 %all_to_all.70 = f32[32,1,128]{2,1,0:T(1,128)S(1)} all-to-all(f32[32,1,128]{2,1,0:T(1,128)S(1)} %broadcast_in_dim.54), channel_id=1, replica_groups=mesh['x'=4,'z'=16,'y'=4,'c'=2] {'x','y','c'}, dimensions={0} | all-to-all | bytes 32768 | tf_op jit(solution)/shard_map/all_to_all | solution.py:17
  163.7 18.5 %all_to_all.71 = f32[16,1,128]{2,1,0:T(1,128)S(1)} all-to-all(f32[16,1,128]{2,1,0:T(1,128)S(1)} %broadcast_in_dim.55), channel_id=1, replica_groups=mesh['x'=4,'z'=16,'y'=4,'c'=2] {'z'}, dimensions={0} | all-to-all | bytes 16384 | tf_op jit(solution)/shard_map/all_to_all | solution.py:17
  182.7 14.2 %all_to_all.72 = bf16[16,16,128]{2,1,0:T(8,128)(2,1)S(1)} all-to-all(bf16[16,16,128]{2,1,0:T(8,128)(2,1)S(1)} %broadcast_in_dim.56), channel_id=1, replica_groups=mesh['x'=4,'z'=16,'y'=4,'c'=2] {'z'}, dimensions={0} | all-to-all | bytes 131072 | tf_op jit(solution)/shard_map/all_to_all | solution.py:17
  197.1 16.7 %all_to_all.73 = bf16[16,16,16,128]{3,2,1,0:T(8,128)(2,1)} all-to-all(bf16[16,16,16,128]{3,2,1,0:T(8,128)(2,1)S(1)} %broadcast_in_dim.57), channel_id=1, replica_groups=mesh['x'=4,'z'=16,'y'=4,'c'=2] {'x','y'}, dimensions={0} | all-to-all | bytes 2097152 | tf_op jit(solution)/shard_map/all_to_all | solution.py:17
  216.3 6.5 %collective-permute-start.16 = (f32[16,128]{1,0:T(8,128)}, f32[16,128]{1,0:T(8,128)S(1)}, u32[]{:S(2)}, u32[]{:S(2)}) collective-permute-start(f32[16,128]{1,0:T(8,128)} %coarse_product.3), channel_id=1, source_target_pairs={{0,1},{1,0},{2,3},{3,2},{4,5},{5,4},{6,7},{7,6},{8,9},{9,8},{10,11... | collective-permute-start | bytes 24584 | tf_op jit(solution)/shard_map/ppermute | solution.py:212
  224.6 14.4 %all_to_all.74 = bf16[16,16,128]{2,1,0:T(8,128)(2,1)S(1)} all-to-all(bf16[16,16,128]{2,1,0:T(8,128)(2,1)S(1)} %broadcast_in_dim.58), channel_id=1, replica_groups=mesh['x'=4,'z'=16,'y'=4,'c'=2] {'z'}, dimensions={0} | all-to-all | bytes 131072 | tf_op jit(solution)/shard_map/all_to_all | solution.py:17
  246.5 3.9 %collective-permute-start.15 = (bf16[64,256]{1,0:T(8,128)(2,1)S(1)}, bf16[64,256]{1,0:T(8,128)(2,1)S(1)}, u32[]{:S(2)}, u32[]{:S(2)}) collective-permute-start(bf16[64,256]{1,0:T(8,128)(2,1)S(1)} %get-tuple-element.17), channel_id=1, source_target_pairs={{0,1},{1,0},{2,3},{3,2},{4,5},{5,4},{6,7},{7,6},{8,9},{9,8},{10,11... | collective-permute-start | bytes 98312 | tf_op jit(solution)/shard_map/ppermute | solution.py:41
  250.5 4.0 %collective-permute-start.13 = (bf16[64,256]{1,0:T(8,128)(2,1)}, bf16[64,256]{1,0:T(8,128)(2,1)}, u32[]{:S(2)}, u32[]{:S(2)}) collective-permute-start(bf16[64,256]{1,0:T(8,128)(2,1)} %get-tuple-element.16), channel_id=1, source_target_pairs={{0,2},{2,4},{4,6},{6,8},{8,10},{10,12},{12,14},{14,16},{16,18},{18... | collective-permute-start | bytes 98312 | tf_op jit(solution)/shard_map/ppermute | solution.py:39
  263.6 13.9 %all_to_all.75 = f32[32,1,64]{2,1,0:T(1,128)S(1)} all-to-all(f32[32,1,64]{2,1,0:T(1,128)S(1)} %broadcast_in_dim.60), channel_id=1, replica_groups=mesh['x'=4,'z'=16,'y'=4,'c'=2] {'x','y','c'}, dimensions={0} | all-to-all | bytes 16384 | tf_op jit(solution)/shard_map/all_to_all | solution.py:17
  277.6 16.1 %all_to_all.76 = f32[16,1,64]{2,1,0:T(1,128)S(1)} all-to-all(f32[16,1,64]{2,1,0:T(1,128)S(1)} %broadcast_in_dim.61), channel_id=1, replica_groups=mesh['x'=4,'z'=16,'y'=4,'c'=2] {'z'}, dimensions={0} | all-to-all | bytes 8192 | tf_op jit(solution)/shard_map/all_to_all | solution.py:17
  294.9 4.1 %collective-permute-start.19 = (bf16[64,256]{1,0:T(8,128)(2,1)S(1)}, bf16[64,256]{1,0:T(8,128)(2,1)S(1)}, u32[]{:S(2)}, u32[]{:S(2)}) collective-permute-start(bf16[64,256]{1,0:T(8,128)(2,1)S(1)} %get-tuple-element.14), channel_id=1, source_target_pairs={{0,1},{1,0},{2,3},{3,2},{4,5},{5,4},{6,7},{7,6},{8,9},{9,8},{10,11... | collective-permute-start | bytes 98312 | tf_op jit(solution)/shard_map/ppermute | solution.py:41
  316.7 17.9 %all_to_all.77 = f32[32,1,64]{2,1,0:T(1,128)S(1)} all-to-all(f32[32,1,64]{2,1,0:T(1,128)S(1)} %broadcast_in_dim.62), channel_id=1, replica_groups=mesh['x'=4,'z'=16,'y'=4,'c'=2] {'x','y','c'}, dimensions={0} | all-to-all | bytes 16384 | tf_op jit(solution)/shard_map/all_to_all | solution.py:17
  334.7 18.7 %all_to_all.78 = f32[16,1,64]{2,1,0:T(1,128)S(1)} all-to-all(f32[16,1,64]{2,1,0:T(1,128)S(1)} %broadcast_in_dim.63), channel_id=1, replica_groups=mesh['x'=4,'z'=16,'y'=4,'c'=2] {'z'}, dimensions={0} | all-to-all | bytes 8192 | tf_op jit(solution)/shard_map/all_to_all | solution.py:17
  (180 shorter events, 102.1 us)
Async XLA Ops:
  3.6 11.4 %collective-permute-start.2 = (bf16[64,256]{1,0:T(8,128)(2,1)S(1)}, bf16[64,256]{1,0:T(8,128)(2,1)S(1)}, u32[]{:S(2)}, u32[]{:S(2)}) collective-permute-start(bf16[64,256]{1,0:T(8,128)(2,1)S(1)} %get-tuple-element.29), channel_id=1, source_target_pairs={{0,1},{1,0},{2,3},{3,2},{4,5},{5,4},{6,7},{7,6},{8,9},{9,8},{10,11... | collective-permute-start | bytes 98312 | tf_op jit(solution)/shard_map/ppermute | solution.py:41
  13.7 4.7 %collective-permute-start.1 = (bf16[64,256]{1,0:T(8,128)(2,1)S(1)}, bf16[64,256]{1,0:T(8,128)(2,1)S(1)}, u32[]{:S(2)}, u32[]{:S(2)}) collective-permute-start(bf16[64,256]{1,0:T(8,128)(2,1)S(1)} %get-tuple-element.30), channel_id=1, source_target_pairs={{2,0},{4,2},{6,4},{8,6},{10,8},{12,10},{14,12},{16,14},{18,16},{20... | collective-permute-start | bytes 98312 | tf_op jit(solution)/shard_map/ppermute | solution.py:40
  19.3 24.8 %all-to-all-start = ((bf16[16,16,128]{2,1,0:T(8,128)(2,1)}), bf16[16,16,128]{2,1,0:T(8,128)(2,1)S(1)}, u32[]{:S(2)}, u32[]{:S(2)}) async-start(bf16[16,16,128]{2,1,0:T(8,128)(2,1)} %broadcast_in_dim.50), calls=%async_computation | async-start | bytes 131072 | tf_op jit(solution)/shard_map/all_to_all | solution.py:17
  45.3 20.7 %all-to-all-start.1 = ((bf16[16,16,16,128]{3,2,1,0:T(8,128)(2,1)}), bf16[16,16,16,128]{3,2,1,0:T(8,128)(2,1)S(1)}, u32[]{:S(2)}, u32[]{:S(2)}) async-start(bf16[16,16,16,128]{3,2,1,0:T(8,128)(2,1)} %broadcast_in_dim.51), calls=%async_computation.1 | async-start | bytes 2097152 | tf_op jit(solution)/shard_map/all_to_all | solution.py:17
  69.4 7.4 %collective-permute-start.6 = (f32[16,128]{1,0:T(8,128)}, f32[16,128]{1,0:T(8,128)S(1)}, u32[]{:S(2)}, u32[]{:S(2)}) collective-permute-start(f32[16,128]{1,0:T(8,128)} %coarse_product.2), channel_id=1, source_target_pairs={{0,1},{1,0},{2,3},{3,2},{4,5},{5,4},{6,7},{7,6},{8,9},{9,8},{10,11... | collective-permute-start | bytes 24584 | tf_op jit(solution)/shard_map/ppermute | solution.py:212
  78.1 15.2 %all-to-all-start.2 = ((bf16[16,16,128]{2,1,0:T(8,128)(2,1)}), bf16[16,16,128]{2,1,0:T(8,128)(2,1)S(1)}, u32[]{:S(2)}, u32[]{:S(2)}) async-start(bf16[16,16,128]{2,1,0:T(8,128)(2,1)} %broadcast_in_dim.52), calls=%async_computation.2 | async-start | bytes 131072 | tf_op jit(solution)/shard_map/all_to_all | solution.py:17
  94.5 19.9 %all-to-all-start.3 = ((bf16[16,16,16,128]{3,2,1,0:T(8,128)(2,1)}), bf16[16,16,16,128]{3,2,1,0:T(8,128)(2,1)S(1)}, u32[]{:S(2)}, u32[]{:S(2)}) async-start(bf16[16,16,16,128]{3,2,1,0:T(8,128)(2,1)} %broadcast_in_dim.53), calls=%async_computation.3 | async-start | bytes 2097152 | tf_op jit(solution)/shard_map/all_to_all | solution.py:17
  102.9 10.9 %collective-permute-start.5 = (bf16[64,256]{1,0:T(8,128)(2,1)S(1)}, bf16[64,256]{1,0:T(8,128)(2,1)S(1)}, u32[]{:S(2)}, u32[]{:S(2)}) collective-permute-start(bf16[64,256]{1,0:T(8,128)(2,1)S(1)} %get-tuple-element.26), channel_id=1, source_target_pairs={{0,1},{1,0},{2,3},{3,2},{4,5},{5,4},{6,7},{7,6},{8,9},{9,8},{10,11... | collective-permute-start | bytes 98312 | tf_op jit(solution)/shard_map/ppermute | solution.py:41
  108.4 9.8 %collective-permute-start.3 = (bf16[64,256]{1,0:T(8,128)(2,1)}, bf16[64,256]{1,0:T(8,128)(2,1)}, u32[]{:S(2)}, u32[]{:S(2)}) collective-permute-start(bf16[64,256]{1,0:T(8,128)(2,1)} %get-tuple-element.25), channel_id=1, source_target_pairs={{0,2},{2,4},{4,6},{6,8},{8,10},{10,12},{12,14},{14,16},{16,18},{18... | collective-permute-start | bytes 98312 | tf_op jit(solution)/shard_map/ppermute | solution.py:39
  112.5 5.6 %collective-permute-start.4 = (bf16[64,256]{1,0:T(8,128)(2,1)}, bf16[64,256]{1,0:T(8,128)(2,1)}, u32[]{:S(2)}, u32[]{:S(2)}) collective-permute-start(bf16[64,256]{1,0:T(8,128)(2,1)} %get-tuple-element.27), channel_id=1, source_target_pairs={{2,0},{4,2},{6,4},{8,6},{10,8},{12,10},{14,12},{16,14},{18,16},{20... | collective-permute-start | bytes 98312 | tf_op jit(solution)/shard_map/ppermute | solution.py:40
  119.2 7.8 %collective-permute-start.9 = (bf16[64,256]{1,0:T(8,128)(2,1)S(1)}, bf16[64,256]{1,0:T(8,128)(2,1)S(1)}, u32[]{:S(2)}, u32[]{:S(2)}) collective-permute-start(bf16[64,256]{1,0:T(8,128)(2,1)S(1)} %get-tuple-element.23), channel_id=1, source_target_pairs={{0,1},{1,0},{2,3},{3,2},{4,5},{5,4},{6,7},{7,6},{8,9},{9,8},{10,11... | collective-permute-start | bytes 98312 | tf_op jit(solution)/shard_map/ppermute | solution.py:41
  125.7 4.7 %collective-permute-start.8 = (bf16[64,256]{1,0:T(8,128)(2,1)S(1)}, bf16[64,256]{1,0:T(8,128)(2,1)S(1)}, u32[]{:S(2)}, u32[]{:S(2)}) collective-permute-start(bf16[64,256]{1,0:T(8,128)(2,1)S(1)} %get-tuple-element.24), channel_id=1, source_target_pairs={{2,0},{4,2},{6,4},{8,6},{10,8},{12,10},{14,12},{16,14},{18,16},{20... | collective-permute-start | bytes 98312 | tf_op jit(solution)/shard_map/ppermute | solution.py:40
  130.9 7.1 %collective-permute-start.12 = (bf16[64,256]{1,0:T(8,128)(2,1)S(1)}, bf16[64,256]{1,0:T(8,128)(2,1)S(1)}, u32[]{:S(2)}, u32[]{:S(2)}) collective-permute-start(bf16[64,256]{1,0:T(8,128)(2,1)S(1)} %get-tuple-element.20), channel_id=1, source_target_pairs={{0,1},{1,0},{2,3},{3,2},{4,5},{5,4},{6,7},{7,6},{8,9},{9,8},{10,11... | collective-permute-start | bytes 98312 | tf_op jit(solution)/shard_map/ppermute | solution.py:41
  134.2 3.8 %collective-permute-start.10 = (bf16[64,256]{1,0:T(8,128)(2,1)S(1)}, bf16[64,256]{1,0:T(8,128)(2,1)S(1)}, u32[]{:S(2)}, u32[]{:S(2)}) collective-permute-start(bf16[64,256]{1,0:T(8,128)(2,1)S(1)} %get-tuple-element.19), channel_id=1, source_target_pairs={{0,2},{2,4},{4,6},{6,8},{8,10},{10,12},{12,14},{14,16},{16,18},{18... | collective-permute-start | bytes 98312 | tf_op jit(solution)/shard_map/ppermute | solution.py:39
  136.7 4.8 %collective-permute-start.11 = (bf16[64,256]{1,0:T(8,128)(2,1)S(1)}, bf16[64,256]{1,0:T(8,128)(2,1)S(1)}, u32[]{:S(2)}, u32[]{:S(2)}) collective-permute-start(bf16[64,256]{1,0:T(8,128)(2,1)S(1)} %get-tuple-element.21), channel_id=1, source_target_pairs={{2,0},{4,2},{6,4},{8,6},{10,8},{12,10},{14,12},{16,14},{18,16},{20... | collective-permute-start | bytes 98312 | tf_op jit(solution)/shard_map/ppermute | solution.py:40
  216.3 7.6 %collective-permute-start.16 = (f32[16,128]{1,0:T(8,128)}, f32[16,128]{1,0:T(8,128)S(1)}, u32[]{:S(2)}, u32[]{:S(2)}) collective-permute-start(f32[16,128]{1,0:T(8,128)} %coarse_product.3), channel_id=1, source_target_pairs={{0,1},{1,0},{2,3},{3,2},{4,5},{5,4},{6,7},{7,6},{8,9},{9,8},{10,11... | collective-permute-start | bytes 24584 | tf_op jit(solution)/shard_map/ppermute | solution.py:212
  240.1 18.7 %all-to-all-start.9 = ((bf16[16,16,16,128]{3,2,1,0:T(8,128)(2,1)}), bf16[16,16,16,128]{3,2,1,0:T(8,128)(2,1)S(1)}, u32[]{:S(2)}, u32[]{:S(2)}) async-start(bf16[16,16,16,128]{3,2,1,0:T(8,128)(2,1)} %broadcast_in_dim.59), calls=%async_computation.9 | async-start | bytes 2097152 | tf_op jit(solution)/shard_map/all_to_all | solution.py:17
  246.5 9.3 %collective-permute-start.15 = (bf16[64,256]{1,0:T(8,128)(2,1)S(1)}, bf16[64,256]{1,0:T(8,128)(2,1)S(1)}, u32[]{:S(2)}, u32[]{:S(2)}) collective-permute-start(bf16[64,256]{1,0:T(8,128)(2,1)S(1)} %get-tuple-element.17), channel_id=1, source_target_pairs={{0,1},{1,0},{2,3},{3,2},{4,5},{5,4},{6,7},{7,6},{8,9},{9,8},{10,11... | collective-permute-start | bytes 98312 | tf_op jit(solution)/shard_map/ppermute | solution.py:41
  250.5 12.0 %collective-permute-start.13 = (bf16[64,256]{1,0:T(8,128)(2,1)}, bf16[64,256]{1,0:T(8,128)(2,1)}, u32[]{:S(2)}, u32[]{:S(2)}) collective-permute-start(bf16[64,256]{1,0:T(8,128)(2,1)} %get-tuple-element.16), channel_id=1, source_target_pairs={{0,2},{2,4},{4,6},{6,8},{8,10},{10,12},{12,14},{14,16},{16,18},{18... | collective-permute-start | bytes 98312 | tf_op jit(solution)/shard_map/ppermute | solution.py:39
  254.5 8.0 %collective-permute-start.14 = (bf16[64,256]{1,0:T(8,128)(2,1)}, bf16[64,256]{1,0:T(8,128)(2,1)}, u32[]{:S(2)}, u32[]{:S(2)}) collective-permute-start(bf16[64,256]{1,0:T(8,128)(2,1)} %get-tuple-element.18), channel_id=1, source_target_pairs={{2,0},{4,2},{6,4},{8,6},{10,8},{12,10},{14,12},{16,14},{18,16},{20... | collective-permute-start | bytes 98312 | tf_op jit(solution)/shard_map/ppermute | solution.py:40
  294.9 7.6 %collective-permute-start.19 = (bf16[64,256]{1,0:T(8,128)(2,1)S(1)}, bf16[64,256]{1,0:T(8,128)(2,1)S(1)}, u32[]{:S(2)}, u32[]{:S(2)}) collective-permute-start(bf16[64,256]{1,0:T(8,128)(2,1)S(1)} %get-tuple-element.14), channel_id=1, source_target_pairs={{0,1},{1,0},{2,3},{3,2},{4,5},{5,4},{6,7},{7,6},{8,9},{9,8},{10,11... | collective-permute-start | bytes 98312 | tf_op jit(solution)/shard_map/ppermute | solution.py:41
  301.2 4.7 %collective-permute-start.18 = (bf16[64,256]{1,0:T(8,128)(2,1)S(1)}, bf16[64,256]{1,0:T(8,128)(2,1)S(1)}, u32[]{:S(2)}, u32[]{:S(2)}) collective-permute-start(bf16[64,256]{1,0:T(8,128)(2,1)S(1)} %get-tuple-element.15), channel_id=1, source_target_pairs={{2,0},{4,2},{6,4},{8,6},{10,8},{12,10},{14,12},{16,14},{18,16},{20... | collective-permute-start | bytes 98312 | tf_op jit(solution)/shard_map/ppermute | solution.py:40
  306.3 6.8 %collective-permute-start.22 = (bf16[64,256]{1,0:T(8,128)(2,1)S(1)}, bf16[64,256]{1,0:T(8,128)(2,1)S(1)}, u32[]{:S(2)}, u32[]{:S(2)}) collective-permute-start(bf16[64,256]{1,0:T(8,128)(2,1)S(1)} %get-tuple-element.11), channel_id=1, source_target_pairs={{0,1},{1,0},{2,3},{3,2},{4,5},{5,4},{6,7},{7,6},{8,9},{9,8},{10,11... | collective-permute-start | bytes 98312 | tf_op jit(solution)/shard_map/ppermute | solution.py:41
  311.9 4.7 %collective-permute-start.21 = (bf16[64,256]{1,0:T(8,128)(2,1)S(1)}, bf16[64,256]{1,0:T(8,128)(2,1)S(1)}, u32[]{:S(2)}, u32[]{:S(2)}) collective-permute-start(bf16[64,256]{1,0:T(8,128)(2,1)S(1)} %get-tuple-element.12), channel_id=1, source_target_pairs={{2,0},{4,2},{6,4},{8,6},{10,8},{12,10},{14,12},{16,14},{18,16},{20... | collective-permute-start | bytes 98312 | tf_op jit(solution)/shard_map/ppermute | solution.py:40
  (27 other events, 551.3 us)

commit v2 on v1

--- a/solution.py
+++ b/solution.py
@@ -5,7 +5,6 @@
 from jax.experimental.pallas import tpu as pltpu
 from jax.sharding import Mesh, PartitionSpec as P
 
-ITERS = 2
 XYZ = (4, 16, 4)
 WIDE = ("x", "z", "y")
 INTERPRET = False
@@ -59,21 +58,26 @@
     window = min(384, columns)
     chunks = out_ref.shape[1] // 128
     position = lax.broadcasted_iota(jnp.int32, (window, 128), 0)
+    own_row = lax.broadcasted_iota(jnp.int32, (rows, window), 0) + first_ref[chunks]
+    own_column = lax.broadcasted_iota(jnp.int32, (rows, window), 1)
 
     def step(chunk, carry):
         low = pl.multiple_of(first_ref[chunk] * 128, 128)
-        part = block_ref[:, pl.ds(low, window)]
+        unit = jnp.where(own_column + low == own_row, 1.0, 0.0).astype(jnp.bfloat16)
+        part = jnp.concatenate([block_ref[:, pl.ds(low, window)], unit], axis=0)
         target = pl.multiple_of(chunk * 128, 128)
         for half in range(2):
             hot = jnp.where(position == source_ref[half, chunk] - low, 1.0, 0.0).astype(jnp.bfloat16)
             chosen = jnp.dot(part, hot, preferred_element_type=jnp.float32)
-            out_ref[half * rows : (half + 1) * rows, pl.ds(target, 128)] = chosen.astype(jnp.bfloat16)
+            out_ref[2 * half * rows : 2 * (half + 1) * rows, pl.ds(target, 128)] = chosen.astype(
+                jnp.bfloat16
+            )
         return carry
 
     lax.fori_loop(0, chunks, step, 0)
 
 
-def padded_inverse(block, starts, counts):
+def padded_inverse(block, starts, counts, own_first):
     rows, columns = block.shape
     subdomains = counts.shape[0]
     slots = 32
@@ -84,9 +88,10 @@
     source = source.reshape(subdomains, 2, half_slots).transpose(1, 0, 2).reshape(2, chunks, 1, 128)
     window = min(384, columns)
     first = jnp.minimum(starts.reshape(chunks, -1)[:, 0] // 128, (columns - window) // 128)
+    first = jnp.concatenate([first, own_first[None]])
     return pl.pallas_call(
         pad_kernel,
-        out_shape=jax.ShapeDtypeStruct((2 * rows, subdomains * half_slots), jnp.bfloat16),
+        out_shape=jax.ShapeDtypeStruct((4 * rows, subdomains * half_slots), jnp.bfloat16),
         in_specs=[
             pl.BlockSpec(memory_space=pltpu.SMEM),
             pl.BlockSpec(memory_space=pltpu.VMEM),
@@ -100,32 +105,58 @@
 
 def product_kernel(padded_ref, blocks_ref, out_ref):
     nx, nz, ny = XYZ
-    rows = padded_ref.shape[0] // 2
-    length = nz * ny * blocks_ref.shape[1]
-    result = jnp.zeros((2 * rows, 128), jnp.float32)
+    rows = padded_ref.shape[0] // 4
+    half = rows // 2
+    length = nz * ny * half
+    result = jnp.zeros((4 * rows, 128), jnp.float32)
     for x in range(nx):
         order = [x * ny * nz + y * nz + z for z in range(nz) for y in range(ny)]
-        part = jnp.concatenate([blocks_ref[p] for p in order], axis=0)
+        part = jnp.concatenate([blocks_ref[p, 0:half, :] for p in order], axis=0)
         result += jnp.dot(
             padded_ref[:, x * length : (x + 1) * length], part, preferred_element_type=jnp.float32
         )
-    joined = result[:rows] + pltpu.roll(result[rows:], 64, 1)
-    lane = lax.broadcasted_iota(jnp.int32, (rows // 2, 128), 1)
-    out_ref[...] = jnp.where(lane < 64, joined[: rows // 2], pltpu.roll(joined[rows // 2 :], 64, 1))
+    joined = result[: 2 * rows] + pltpu.roll(result[2 * rows :], 64, 1)
+    lane = lax.broadcasted_iota(jnp.int32, (half, 128), 1)
+    for k in range(2):
+        low = joined[2 * k * half : (2 * k + 1) * half]
+        high = joined[(2 * k + 1) * half : (2 * k + 2) * half]
+        out_ref[k * half : (k + 1) * half, :] = jnp.where(lane < 64, low, pltpu.roll(high, 64, 1))
+    if out_ref.shape[0] > rows:
+        sums = jnp.zeros((8, 128), jnp.float32)
+        for p in range(blocks_ref.shape[0]):
+            sums += blocks_ref[p, half : half + 8, :].astype(jnp.float32)
+        out_ref[rows : rows + 8, :] = sums
 
 
 def coarse_product(padded, blocks):
+    rows = padded.shape[0] // 4
     return pl.pallas_call(
         product_kernel,
-        out_shape=jax.ShapeDtypeStruct((padded.shape[0] // 4, 128), jnp.float32),
+        out_shape=jax.ShapeDtypeStruct((rows + blocks.shape[1] - rows // 2, 128), jnp.float32),
         interpret=INTERPRET,
         name="coarse_product",
     )(padded, blocks)
 
 
+def in_pieces(values):
+    rest = values
+    pieces = []
+    for _ in range(3):
+        piece = lax.reduce_precision(rest, 8, 7)
+        pieces.append(piece)
+        rest = rest - piece
+    pieces.append(jnp.zeros((8 - len(pieces), values.shape[1]), jnp.float32))
+    return jnp.concatenate(pieces, axis=0).astype(jnp.bfloat16)
+
+
+def swapped_sum(partial):
+    return partial + lax.ppermute(partial, "c", [(0, 1), (1, 0)])
+
+
 def lift_kernel(info_ref, low_ref, high_ref, modes_ref, out_ref):
     slots = modes_ref.shape[0]
-    window = jnp.concatenate([low_ref[0], high_ref[0]], axis=0)
+    half_slots = slots // 2
+    window = jnp.concatenate([low_ref[0, 0:half_slots, :], high_ref[0, 0:half_slots, :]], axis=0)
     rank = lax.broadcasted_iota(jnp.int32, (slots, slots), 0)
     column = lax.broadcasted_iota(jnp.int32, (slots, slots), 1)
     offset = info_ref[2] + rank
@@ -147,7 +178,7 @@
 
 
 def lift(info, blocks, modes):
-    half_slots = blocks.shape[1]
+    block_rows = blocks.shape[1]
     load_count = 64
     width = modes.shape[1]
     return pl.pallas_call(
@@ -157,8 +188,8 @@
             num_scalar_prefetch=1,
             grid=(1,),
             in_specs=[
-                pl.BlockSpec((1, half_slots, 128), lambda i, info: (info[0], 0, 0)),
-                pl.BlockSpec((1, half_slots, 128), lambda i, info: (info[1], 0, 0)),
+                pl.BlockSpec((1, block_rows, 128), lambda i, info: (info[0], 0, 0)),
+                pl.BlockSpec((1, block_rows, 128), lambda i, info: (info[1], 0, 0)),
                 pl.BlockSpec(modes.shape, lambda i, info: (0, 0)),
             ],
             out_specs=pl.BlockSpec((load_count, width), lambda i, info: (0, 0)),
@@ -178,13 +209,12 @@
     row = lax.axis_index(WIDE)
     column = lax.axis_index("c")
     column_width = coarse_inverse.shape[1]
-    width = local_loads.shape[1]
-    face = width // 4
+    face = local_loads.shape[1] // 4
 
     counts = lax.dynamic_index_in_dim(mode_counts, column, 0, keepdims=False)
     ends = jnp.cumsum(counts)
     starts = ends - counts
-    padded = padded_inverse(coarse_inverse, starts, counts)
+    padded = padded_inverse(coarse_inverse, starts, counts, 32 * row - column * column_width)
 
     own_start = lax.dynamic_index_in_dim(starts, row, 0, keepdims=False)
     own_count = lax.dynamic_index_in_dim(counts, row, 0, keepdims=False)
@@ -199,45 +229,76 @@
     doubled = jnp.stack([row > 0, row < rows - 1, column == 1, column == 0])
     factor = jnp.repeat(jnp.where(doubled, 2.0, 1.0), face)[None, :]
 
-    def precondition(rounded):
-        weights = lax.dot_general(
+    def weigh(rounded):
+        return lax.dot_general(
             mode_block, rounded, (((1,), (1,)), ((), ())), preferred_element_type=jnp.float32
-        ).astype(jnp.bfloat16)
+        )
+
+    def smooth(rounded):
         inner = (rounded.astype(jnp.float32) * factor).astype(jnp.bfloat16)
-        smoothed = jnp.dot(inner, precond_block, preferred_element_type=jnp.float32).astype(
+        return jnp.dot(inner, precond_block, preferred_element_type=jnp.float32).astype(
             jnp.bfloat16
         )
-        local = jump(smoothed)
-        partial = coarse_product(padded, gather_blocks(pack(weights)))
-        partner = lax.ppermute(partial, "c", [(0, 1), (1, 0)])
-        values = gather_blocks((partial + partner).astype(jnp.bfloat16))
-        return local + lift(info, values, mode_block)
-
-    disp = jnp.dot(local_loads, flex_block, preferred_element_type=jnp.float32).astype(jnp.bfloat16)
-    residual = jump(disp)
-    direction = precondition(residual.astype(jnp.bfloat16))
-    energy = None
-    multipliers = None
-    for step_number in range(ITERS):
-        moved = jump(direction.astype(jnp.bfloat16)).astype(jnp.bfloat16)
-        image = jump(
-            jnp.dot(moved, flex_block, preferred_element_type=jnp.float32).astype(jnp.bfloat16)
-        )
-        curvature = jnp.sum(direction * image, axis=1)
-        if energy is None:
-            both = jnp.concatenate([jnp.sum(residual * direction, axis=1), curvature])
-            both = total(both[None, :])[0]
-            energy, curvature = both[:64], both[64:]
-        else:
-            curvature = total(curvature[None, :])[0]
-        size = (energy / curvature)[:, None]
-        multipliers = size * direction if multipliers is None else multipliers + size * direction
-        residual = residual - size * image
-        if step_number + 1 < ITERS:
-            fresh_z = precondition(residual.astype(jnp.bfloat16))
-            fresh = total(jnp.sum(residual * fresh_z, axis=1)[None, :])[0]
-            direction = fresh_z + (fresh / energy)[:, None] * direction
-            energy = fresh
+
+    def apply_flex(values):
+        return jnp.dot(values, flex_block, preferred_element_type=jnp.float32).astype(jnp.bfloat16)
+
+    def operator_input(direction):
+        return jump(direction.astype(jnp.bfloat16)).astype(jnp.bfloat16)
+
+    def load_dot(left, right):
+        return jnp.sum(left.astype(jnp.float32) * right.astype(jnp.float32), axis=1)
+
+    residual = jump(apply_flex(local_loads))
+    rounded = residual.astype(jnp.bfloat16)
+    smoothed = smooth(rounded)
+    first_sums = swapped_sum(
+        coarse_product(padded, gather_blocks(pack(weigh(rounded).astype(jnp.bfloat16))))
+    )
+    half_slots = first_sums.shape[0] // 2
+    values = gather_blocks(first_sums[:half_slots].astype(jnp.bfloat16))
+    direction = jump(smoothed) + lift(info, values, mode_block)
+
+    moved = operator_input(direction)
+    pushed = apply_flex(moved)
+    partials = jnp.concatenate([load_dot(residual, direction), load_dot(moved, pushed)])[None, :]
+    image = jump(pushed)
+    image_high = lax.reduce_precision(image, 8, 7)
+    image_low = (image - image_high).astype(jnp.bfloat16)
+    image_weights = weigh(image_high.astype(jnp.bfloat16)) + weigh(image_low)
+    block = jnp.concatenate([pack(image_weights.astype(jnp.bfloat16)), in_pieces(partials)], axis=0)
+    second_sums = swapped_sum(coarse_product(padded, gather_blocks(block)))
+    totals = jnp.sum(second_sums[2 * half_slots :], axis=0)
+    energy = totals[:64]
+    size = energy / totals[64:]
+    multipliers = size[:, None] * direction
+    residual = residual - size[:, None] * image
+
+    packed = first_sums - jnp.tile(size, 2)[None, :] * second_sums[: 2 * half_slots]
+    rounded = residual.astype(jnp.bfloat16)
+    smoothed = smooth(rounded)
+    coarse_values = lax.reduce_precision(packed[:half_slots], 8, 7)
+    coarse_energy = jnp.sum(coarse_values * packed[half_slots:], axis=0)
+    local_energy = load_dot(residual * factor, smoothed)
+    partial = local_energy + 0.5 * (coarse_energy[:64] + coarse_energy[64:])
+    partial = jnp.concatenate([partial, jnp.zeros_like(partial)])[None, :]
+    block = jnp.concatenate([coarse_values.astype(jnp.bfloat16), in_pieces(partial)], axis=0)
+    values = gather_blocks(block)
+    sums = jnp.sum(values[:, half_slots:, :].astype(jnp.float32), axis=(0, 1))[None, :]
+    fresh = swapped_sum(sums)[0, :64]
+    direction = (
+        jump(smoothed)
+        + lift(info, values, mode_block)
+        + (fresh / energy)[:, None] * direction
+    )
+
+    moved = operator_input(direction)
+    pushed = apply_flex(moved)
+    curvature = total(load_dot(moved, pushed)[None, :])[0]
+    image = jump(pushed)
+    size = (fresh / curvature)[:, None]
+    multipliers = multipliers + size * direction
+    residual = residual - size * image
     return (multipliers.astype(jnp.bfloat16)[None, None], residual.astype(jnp.bfloat16)[None, None])
 
 

time: 356 us -> 313 us (0.88)
  blocking collectives: 152 us -> 84.1 us
  starting transfers between devices: 104 us -> 116 us
  waiting for transfers between devices: 42.6 us -> 51.4 us
    all_to_all x9 -> x4, blocking collectives: 152 us -> 84.1 us  [spread(): return lax.all_to_all(copies, axes, 0, 0, tiled=False)]
    all_to_all x5 -> x6, waiting for transfers between devices: 23.9 us -> 35.9 us  [spread(): return lax.all_to_all(copies, axes, 0, 0, tiled=False)]
    all_to_all x5 -> x6, starting transfers between devices: 31.4 us -> 39.8 us  [spread(): return lax.all_to_all(copies, axes, 0, 0, tiled=False)]
    ppermute x2 -> x3, starting transfers between devices: 12.9 us -> 19 us  [swapped_sum(): return partial + lax.ppermute(partial, 'c', [(0, 1), (1, 0)])]
    dot_general x7 -> x8, matrix products: 6.78 us -> 7.3 us  [the longest x2 4.26 us: smooth(): jnp.dot(inner, precond_block, preferred_element_type=jnp.float32)]
  transfers between devices with their start and end apart: 28 -> 30, of which waited for: 11 -> 11; matrix products, arithmetic and copies ran while one was open for 5% -> 5% of each run, Pallas kernels for 3% -> 4%
where the time goes in v2:
time: 313 us; the launch traced here: 309 us
  starting transfers between devices  116 us (37%)
  blocking collectives  84.1 us (27%)
  waiting for transfers between devices  51.4 us (16%)
  Pallas kernels  18.8 us (6%)
  local copies, waits for them, and re-layouts  17 us (5%)
  other arithmetic  11.9 us (4%)
  matrix products  7.3 us (2%)
    all_to_all x4, blocking collectives, spread(): return lax.all_to_all(copies, axes, 0, 0, tiled=False)  84.1 us
    all_to_all x6, starting transfers between devices, spread(): return lax.all_to_all(copies, axes, 0, 0, tiled=False)  39.8 us
    all_to_all x6, waiting for transfers between devices, spread(): return lax.all_to_all(copies, axes, 0, 0, tiled=False)  35.9 us
    ppermute x7, starting transfers between devices, neighbours(): lax.ppermute(jnp.where(column == 0, east, west), 'c', [(0, 1), (1, 0)])  30.1 us
    ppermute x3, starting transfers between devices, swapped_sum(): return partial + lax.ppermute(partial, 'c', [(0, 1), (1, 0)])  19 us
    ppermute x7, starting transfers between devices, neighbours(): from_above = lax.ppermute(south, WIDE, down)  18.4 us
    ppermute x7, waiting for transfers between devices, neighbours(): from_below = lax.ppermute(north, WIDE, up)  13.4 us
    ppermute x7, starting transfers between devices, neighbours(): from_below = lax.ppermute(north, WIDE, up)  9.03 us
  transfers between devices with their start and end apart: 30, of which 11 were waited for; matrix products, arithmetic and copies ran while one was open for 5% of the time, Pallas kernels for 4%

profile of v2, /device:TPU:1, one launch (start us, length us, event | category | flops | bytes accessed | tf_op | source)
XLA Modules:
  0.0 308.9 jit_solution(11665687174656346760)
XLA Ops:
  3.6 8.7 %collective-permute-start.2 = (bf16[64,256]{1,0:T(8,128)(2,1)S(1)}, bf16[64,256]{1,0:T(8,128)(2,1)S(1)}, u32[]{:S(2)}, u32[]{:S(2)}) collective-permute-start(bf16[64,256]{1,0:T(8,128)(2,1)S(1)} %get-tuple-element.27), channel_id=1, source_target_pairs={{0,1},{1,0},{2,3},{3,2},{4,5},{5,4},{6,7},{7,6},{8,9},{9,8},{10,11... | collective-permute-start | bytes 98312 | tf_op jit(solution)/shard_map/ppermute | solution.py:40
  19.3 13.2 %all-to-all-start = ((bf16[16,16,128]{2,1,0:T(8,128)(2,1)}), bf16[16,16,128]{2,1,0:T(8,128)(2,1)S(1)}, u32[]{:S(2)}, u32[]{:S(2)}) async-start(bf16[16,16,128]{2,1,0:T(8,128)(2,1)} %broadcast_in_dim.47), calls=%async_computation | async-start | bytes 131072 | tf_op jit(solution)/shard_map/all_to_all | solution.py:16
  35.0 9.1 %all-to-all-done = bf16[16,16,128]{2,1,0:T(8,128)(2,1)S(1)} async-done(((bf16[16,16,128]{2,1,0:T(8,128)(2,1)}), bf16[16,16,128]{2,1,0:T(8,128)(2,1)S(1)}, u32[]{:S(2)}, u32[]{:S(2)}) %all-to-all-start) | async-done | bytes 65568 | tf_op jit(solution)/shard_map/all_to_all | solution.py:16
  45.3 6.8 %all-to-all-start.1 = ((bf16[16,16,16,128]{3,2,1,0:T(8,128)(2,1)}), bf16[16,16,16,128]{3,2,1,0:T(8,128)(2,1)S(1)}, u32[]{:S(2)}, u32[]{:S(2)}) async-start(bf16[16,16,16,128]{3,2,1,0:T(8,128)(2,1)} %broadcast_in_dim.48), calls=%async_computation.1 | async-start | bytes 2097152 | tf_op jit(solution)/shard_map/all_to_all | solution.py:16
  56.5 7.9 %pad_inverse.1.padded_ref = bf16[128,4096]{1,0:T(8,128)(2,1)} custom-call(s32[33]{0:T(128)} %pad_add_fusion.first_ref, s32[2,32,1,128]{3,2,1,0:T(1,128)} %compare_select_fusion.source_ref, bf16[32,4096]{1,0:T(8,128)(2,1)} %block_ref.1), custom_call_target="tpu_custom_call" | custom-call | tf_op jit(solution)/shard_map/pad_inverse/pallas_call | solution.py:92
  69.7 6.4 %collective-permute-start.6 = (f32[32,128]{1,0:T(8,128)}, f32[32,128]{1,0:T(8,128)S(1)}, u32[]{:S(2)}, u32[]{:S(2)}) collective-permute-start(f32[32,128]{1,0:T(8,128)} %coarse_product.2), channel_id=1, source_target_pairs={{0,1},{1,0},{2,3},{3,2},{4,5},{5,4},{6,7},{7,6},{8,9},{9,8},{10,11... | collective-permute-start | bytes 49160 | tf_op jit(solution)/shard_map/ppermute | solution.py:153
  78.4 3.5 %all-to-all-start.2 = ((bf16[16,16,128]{2,1,0:T(8,128)(2,1)}), bf16[16,16,128]{2,1,0:T(8,128)(2,1)S(1)}, u32[]{:S(2)}, u32[]{:S(2)}) async-start(bf16[16,16,128]{2,1,0:T(8,128)(2,1)} %broadcast_in_dim.49), calls=%async_computation.2 | async-start | bytes 131072 | tf_op jit(solution)/shard_map/all_to_all | solution.py:16
  83.5 10.1 %all-to-all-done.2 = bf16[16,16,128]{2,1,0:T(8,128)(2,1)S(1)} async-done(((bf16[16,16,128]{2,1,0:T(8,128)(2,1)}), bf16[16,16,128]{2,1,0:T(8,128)(2,1)S(1)}, u32[]{:S(2)}, u32[]{:S(2)}) %all-to-all-start.2) | async-done | bytes 65568 | tf_op jit(solution)/shard_map/all_to_all | solution.py:16
  94.8 4.4 %all-to-all-start.3 = ((bf16[16,16,16,128]{3,2,1,0:T(8,128)(2,1)}), bf16[16,16,16,128]{3,2,1,0:T(8,128)(2,1)S(1)}, u32[]{:S(2)}, u32[]{:S(2)}) async-start(bf16[16,16,16,128]{3,2,1,0:T(8,128)(2,1)} %broadcast_in_dim.50), calls=%async_computation.3 | async-start | bytes 2097152 | tf_op jit(solution)/shard_map/all_to_all | solution.py:16
  104.0 4.1 %collective-permute-start.5 = (bf16[64,256]{1,0:T(8,128)(2,1)S(1)}, bf16[64,256]{1,0:T(8,128)(2,1)S(1)}, u32[]{:S(2)}, u32[]{:S(2)}) collective-permute-start(bf16[64,256]{1,0:T(8,128)(2,1)S(1)} %get-tuple-element.24), channel_id=1, source_target_pairs={{0,1},{1,0},{2,3},{3,2},{4,5},{5,4},{6,7},{7,6},{8,9},{9,8},{10,11... | collective-permute-start | bytes 98312 | tf_op jit(solution)/shard_map/ppermute | solution.py:40
  109.5 4.2 %collective-permute-start.3 = (bf16[64,256]{1,0:T(8,128)(2,1)}, bf16[64,256]{1,0:T(8,128)(2,1)}, u32[]{:S(2)}, u32[]{:S(2)}) collective-permute-start(bf16[64,256]{1,0:T(8,128)(2,1)} %get-tuple-element.23), channel_id=1, source_target_pairs={{0,2},{2,4},{4,6},{6,8},{8,10},{10,12},{12,14},{14,16},{16,18},{18... | collective-permute-start | bytes 98312 | tf_op jit(solution)/shard_map/ppermute | solution.py:38
  120.4 3.7 %collective-permute-start.9 = (bf16[64,256]{1,0:T(8,128)(2,1)S(1)}, bf16[64,256]{1,0:T(8,128)(2,1)S(1)}, u32[]{:S(2)}, u32[]{:S(2)}) collective-permute-start(bf16[64,256]{1,0:T(8,128)(2,1)S(1)} %get-tuple-element.21), channel_id=1, source_target_pairs={{0,1},{1,0},{2,3},{3,2},{4,5},{5,4},{6,7},{7,6},{8,9},{9,8},{10,11... | collective-permute-start | bytes 98312 | tf_op jit(solution)/shard_map/ppermute | solution.py:40
  139.4 3.4 %collective-permute-done.11 = bf16[64,256]{1,0:T(8,128)(2,1)S(1)} collective-permute-done((bf16[64,256]{1,0:T(8,128)(2,1)S(1)}, bf16[64,256]{1,0:T(8,128)(2,1)S(1)}, u32[]{:S(2)}, u32[]{:S(2)}) %collective-permute-start.11) | collective-permute-done | bytes 32800 | tf_op jit(solution)/shard_map/ppermute | solution.py:39
  143.4 21.2 %all_to_all.50 = bf16[16,24,128]{2,1,0:T(8,128)(2,1)S(1)} all-to-all(bf16[16,24,128]{2,1,0:T(8,128)(2,1)S(1)} %broadcast_in_dim.51), channel_id=1, replica_groups=mesh['x'=4,'z'=16,'y'=4,'c'=2] {'z'}, dimensions={0} | all-to-all | bytes 196608 | tf_op jit(solution)/shard_map/all_to_all | solution.py:16
  164.9 30.4 %all_to_all.51 = bf16[16,16,24,128]{3,2,1,0:T(8,128)(2,1)} all-to-all(bf16[16,16,24,128]{3,2,1,0:T(8,128)(2,1)S(1)} %broadcast_in_dim.52), channel_id=1, replica_groups=mesh['x'=4,'z'=16,'y'=4,'c'=2] {'x','y'}, dimensions={0} | all-to-all | bytes 3145728 | tf_op jit(solution)/shard_map/all_to_all | solution.py:16
  198.2 6.6 %collective-permute-start.13 = (f32[40,128]{1,0:T(8,128)}, f32[40,128]{1,0:T(8,128)S(1)}, u32[]{:S(2)}, u32[]{:S(2)}) collective-permute-start(f32[40,128]{1,0:T(8,128)} %coarse_product.3), channel_id=1, source_target_pairs={{0,1},{1,0},{2,3},{3,2},{4,5},{5,4},{6,7},{7,6},{8,9},{9,8},{10,11... | collective-permute-start | bytes 61448 | tf_op jit(solution)/shard_map/ppermute | solution.py:153
  209.2 16.3 %all_to_all.52 = bf16[16,24,128]{2,1,0:T(8,128)(2,1)S(1)} all-to-all(bf16[16,24,128]{2,1,0:T(8,128)(2,1)S(1)} %broadcast_in_dim.53), channel_id=1, replica_groups=mesh['x'=4,'z'=16,'y'=4,'c'=2] {'z'}, dimensions={0} | all-to-all | bytes 196608 | tf_op jit(solution)/shard_map/all_to_all | solution.py:16
  226.9 4.4 %all-to-all-start.7 = ((bf16[16,16,24,128]{3,2,1,0:T(8,128)(2,1)}), bf16[16,16,24,128]{3,2,1,0:T(8,128)(2,1)}, u32[]{:S(2)}, u32[]{:S(2)}) async-start(bf16[16,16,24,128]{3,2,1,0:T(8,128)(2,1)} %broadcast_in_dim.54), calls=%async_computation.7 | async-start | bytes 3145728 | tf_op jit(solution)/shard_map/all_to_all | solution.py:16
  234.5 5.2 %collective-permute-start.17 = (bf16[64,256]{1,0:T(8,128)(2,1)S(1)}, bf16[64,256]{1,0:T(8,128)(2,1)S(1)}, u32[]{:S(2)}, u32[]{:S(2)}) collective-permute-start(bf16[64,256]{1,0:T(8,128)(2,1)S(1)} %get-tuple-element.15), channel_id=1, source_target_pairs={{0,1},{1,0},{2,3},{3,2},{4,5},{5,4},{6,7},{7,6},{8,9},{9,8},{10,11... | collective-permute-start | bytes 98312 | tf_op jit(solution)/shard_map/ppermute | solution.py:40
  240.9 10.6 %all-to-all-done.7 = bf16[16,16,24,128]{3,2,1,0:T(8,128)(2,1)} async-done(((bf16[16,16,24,128]{3,2,1,0:T(8,128)(2,1)}), bf16[16,16,24,128]{3,2,1,0:T(8,128)(2,1)}, u32[]{:S(2)}, u32[]{:S(2)}) %all-to-all-start.7) | async-done | bytes 1572896 | tf_op jit(solution)/shard_map/all_to_all | solution.py:16
  252.8 6.1 %collective-permute-start.14 = (f32[1,128]{1,0:T(1,128)S(1)}, f32[1,128]{1,0:T(1,128)S(1)}, u32[]{:S(2)}, u32[]{:S(2)}) collective-permute-start(f32[1,128]{1,0:T(1,128)S(1)} %bitcast.102), channel_id=1, source_target_pairs={{0,1},{1,0},{2,3},{3,2},{4,5},{5,4},{6,7},{7,6},{8,9},{9,8},{10,11... | collective-permute-start | bytes 1544 | tf_op jit(solution)/shard_map/ppermute | solution.py:153
  272.4 16.3 %all_to_all.53 = f32[32,1,64]{2,1,0:T(1,128)S(1)} all-to-all(f32[32,1,64]{2,1,0:T(1,128)S(1)} %broadcast_in_dim.56), channel_id=1, replica_groups=mesh['x'=4,'z'=16,'y'=4,'c'=2] {'x','y','c'}, dimensions={0} | all-to-all | bytes 16384 | tf_op jit(solution)/shard_map/all_to_all | solution.py:16
  289.3 7.5 %all-to-all-start.9 = ((f32[16,1,64]{2,1,0:T(1,128)}), f32[16,1,64]{2,1,0:T(1,128)S(1)}, u32[]{:S(2)}, u32[]{:S(2)}) async-start(f32[16,1,64]{2,1,0:T(1,128)} %broadcast_in_dim.57), calls=%async_computation.9 | async-start | bytes 16384 | tf_op jit(solution)/shard_map/all_to_all | solution.py:16
  303.4 4.6 %all-to-all-done.9 = f32[16,1,64]{2,1,0:T(1,128)S(1)} async-done(((f32[16,1,64]{2,1,0:T(1,128)}), f32[16,1,64]{2,1,0:T(1,128)S(1)}, u32[]{:S(2)}, u32[]{:S(2)}) %all-to-all-start.9) | async-done | bytes 4128 | tf_op jit(solution)/shard_map/all_to_all | solution.py:16
  (187 shorter events, 92.3 us)
Async XLA Ops:
  3.6 11.4 %collective-permute-start.2 = (bf16[64,256]{1,0:T(8,128)(2,1)S(1)}, bf16[64,256]{1,0:T(8,128)(2,1)S(1)}, u32[]{:S(2)}, u32[]{:S(2)}) collective-permute-start(bf16[64,256]{1,0:T(8,128)(2,1)S(1)} %get-tuple-element.27), channel_id=1, source_target_pairs={{0,1},{1,0},{2,3},{3,2},{4,5},{5,4},{6,7},{7,6},{8,9},{9,8},{10,11... | collective-permute-start | bytes 98312 | tf_op jit(solution)/shard_map/ppermute | solution.py:40
  13.7 4.7 %collective-permute-start.1 = (bf16[64,256]{1,0:T(8,128)(2,1)S(1)}, bf16[64,256]{1,0:T(8,128)(2,1)S(1)}, u32[]{:S(2)}, u32[]{:S(2)}) collective-permute-start(bf16[64,256]{1,0:T(8,128)(2,1)S(1)} %get-tuple-element.28), channel_id=1, source_target_pairs={{2,0},{4,2},{6,4},{8,6},{10,8},{12,10},{14,12},{16,14},{18,16},{20... | collective-permute-start | bytes 98312 | tf_op jit(solution)/shard_map/ppermute | solution.py:39
  19.3 24.8 %all-to-all-start = ((bf16[16,16,128]{2,1,0:T(8,128)(2,1)}), bf16[16,16,128]{2,1,0:T(8,128)(2,1)S(1)}, u32[]{:S(2)}, u32[]{:S(2)}) async-start(bf16[16,16,128]{2,1,0:T(8,128)(2,1)} %broadcast_in_dim.47), calls=%async_computation | async-start | bytes 131072 | tf_op jit(solution)/shard_map/all_to_all | solution.py:16
  45.3 20.7 %all-to-all-start.1 = ((bf16[16,16,16,128]{3,2,1,0:T(8,128)(2,1)}), bf16[16,16,16,128]{3,2,1,0:T(8,128)(2,1)S(1)}, u32[]{:S(2)}, u32[]{:S(2)}) async-start(bf16[16,16,16,128]{3,2,1,0:T(8,128)(2,1)} %broadcast_in_dim.48), calls=%async_computation.1 | async-start | bytes 2097152 | tf_op jit(solution)/shard_map/all_to_all | solution.py:16
  69.7 7.4 %collective-permute-start.6 = (f32[32,128]{1,0:T(8,128)}, f32[32,128]{1,0:T(8,128)S(1)}, u32[]{:S(2)}, u32[]{:S(2)}) collective-permute-start(f32[32,128]{1,0:T(8,128)} %coarse_product.2), channel_id=1, source_target_pairs={{0,1},{1,0},{2,3},{3,2},{4,5},{5,4},{6,7},{7,6},{8,9},{9,8},{10,11... | collective-permute-start | bytes 49160 | tf_op jit(solution)/shard_map/ppermute | solution.py:153
  78.4 15.2 %all-to-all-start.2 = ((bf16[16,16,128]{2,1,0:T(8,128)(2,1)}), bf16[16,16,128]{2,1,0:T(8,128)(2,1)S(1)}, u32[]{:S(2)}, u32[]{:S(2)}) async-start(bf16[16,16,128]{2,1,0:T(8,128)(2,1)} %broadcast_in_dim.49), calls=%async_computation.2 | async-start | bytes 131072 | tf_op jit(solution)/shard_map/all_to_all | solution.py:16
  94.8 20.7 %all-to-all-start.3 = ((bf16[16,16,16,128]{3,2,1,0:T(8,128)(2,1)}), bf16[16,16,16,128]{3,2,1,0:T(8,128)(2,1)S(1)}, u32[]{:S(2)}, u32[]{:S(2)}) async-start(bf16[16,16,16,128]{3,2,1,0:T(8,128)(2,1)} %broadcast_in_dim.50), calls=%async_computation.3 | async-start | bytes 2097152 | tf_op jit(solution)/shard_map/all_to_all | solution.py:16
  104.0 10.9 %collective-permute-start.5 = (bf16[64,256]{1,0:T(8,128)(2,1)S(1)}, bf16[64,256]{1,0:T(8,128)(2,1)S(1)}, u32[]{:S(2)}, u32[]{:S(2)}) collective-permute-start(bf16[64,256]{1,0:T(8,128)(2,1)S(1)} %get-tuple-element.24), channel_id=1, source_target_pairs={{0,1},{1,0},{2,3},{3,2},{4,5},{5,4},{6,7},{7,6},{8,9},{9,8},{10,11... | collective-permute-start | bytes 98312 | tf_op jit(solution)/shard_map/ppermute | solution.py:40
  109.5 9.8 %collective-permute-start.3 = (bf16[64,256]{1,0:T(8,128)(2,1)}, bf16[64,256]{1,0:T(8,128)(2,1)}, u32[]{:S(2)}, u32[]{:S(2)}) collective-permute-start(bf16[64,256]{1,0:T(8,128)(2,1)} %get-tuple-element.23), channel_id=1, source_target_pairs={{0,2},{2,4},{4,6},{6,8},{8,10},{10,12},{12,14},{14,16},{16,18},{18... | collective-permute-start | bytes 98312 | tf_op jit(solution)/shard_map/ppermute | solution.py:38
  113.6 5.6 %collective-permute-start.4 = (bf16[64,256]{1,0:T(8,128)(2,1)}, bf16[64,256]{1,0:T(8,128)(2,1)}, u32[]{:S(2)}, u32[]{:S(2)}) collective-permute-start(bf16[64,256]{1,0:T(8,128)(2,1)} %get-tuple-element.25), channel_id=1, source_target_pairs={{2,0},{4,2},{6,4},{8,6},{10,8},{12,10},{14,12},{16,14},{18,16},{20... | collective-permute-start | bytes 98312 | tf_op jit(solution)/shard_map/ppermute | solution.py:39
  120.4 7.8 %collective-permute-start.9 = (bf16[64,256]{1,0:T(8,128)(2,1)S(1)}, bf16[64,256]{1,0:T(8,128)(2,1)S(1)}, u32[]{:S(2)}, u32[]{:S(2)}) collective-permute-start(bf16[64,256]{1,0:T(8,128)(2,1)S(1)} %get-tuple-element.21), channel_id=1, source_target_pairs={{0,1},{1,0},{2,3},{3,2},{4,5},{5,4},{6,7},{7,6},{8,9},{9,8},{10,11... | collective-permute-start | bytes 98312 | tf_op jit(solution)/shard_map/ppermute | solution.py:40
  132.2 7.2 %collective-permute-start.12 = (bf16[64,256]{1,0:T(8,128)(2,1)S(1)}, bf16[64,256]{1,0:T(8,128)(2,1)S(1)}, u32[]{:S(2)}, u32[]{:S(2)}) collective-permute-start(bf16[64,256]{1,0:T(8,128)(2,1)S(1)} %get-tuple-element.18), channel_id=1, source_target_pairs={{0,1},{1,0},{2,3},{3,2},{4,5},{5,4},{6,7},{7,6},{8,9},{9,8},{10,11... | collective-permute-start | bytes 98312 | tf_op jit(solution)/shard_map/ppermute | solution.py:40
  138.1 4.8 %collective-permute-start.11 = (bf16[64,256]{1,0:T(8,128)(2,1)S(1)}, bf16[64,256]{1,0:T(8,128)(2,1)S(1)}, u32[]{:S(2)}, u32[]{:S(2)}) collective-permute-start(bf16[64,256]{1,0:T(8,128)(2,1)S(1)} %get-tuple-element.19), channel_id=1, source_target_pairs={{2,0},{4,2},{6,4},{8,6},{10,8},{12,10},{14,12},{16,14},{18,16},{20... | collective-permute-start | bytes 98312 | tf_op jit(solution)/shard_map/ppermute | solution.py:39
  198.2 7.6 %collective-permute-start.13 = (f32[40,128]{1,0:T(8,128)}, f32[40,128]{1,0:T(8,128)S(1)}, u32[]{:S(2)}, u32[]{:S(2)}) collective-permute-start(f32[40,128]{1,0:T(8,128)} %coarse_product.3), channel_id=1, source_target_pairs={{0,1},{1,0},{2,3},{3,2},{4,5},{5,4},{6,7},{7,6},{8,9},{9,8},{10,11... | collective-permute-start | bytes 61448 | tf_op jit(solution)/shard_map/ppermute | solution.py:153
  226.9 24.6 %all-to-all-start.7 = ((bf16[16,16,24,128]{3,2,1,0:T(8,128)(2,1)}), bf16[16,16,24,128]{3,2,1,0:T(8,128)(2,1)}, u32[]{:S(2)}, u32[]{:S(2)}) async-start(bf16[16,16,24,128]{3,2,1,0:T(8,128)(2,1)} %broadcast_in_dim.54), calls=%async_computation.7 | async-start | bytes 3145728 | tf_op jit(solution)/shard_map/all_to_all | solution.py:16
  231.4 30.3 %collective-permute-start.15 = (bf16[64,256]{1,0:T(8,128)(2,1)S(1)}, bf16[64,256]{1,0:T(8,128)(2,1)S(1)}, u32[]{:S(2)}, u32[]{:S(2)}) collective-permute-start(bf16[64,256]{1,0:T(8,128)(2,1)S(1)} %get-tuple-element.14), channel_id=1, source_target_pairs={{0,2},{2,4},{4,6},{6,8},{8,10},{10,12},{12,14},{14,16},{16,18},{18... | collective-permute-start | bytes 98312 | tf_op jit(solution)/shard_map/ppermute | solution.py:38
  234.5 24.5 %collective-permute-start.17 = (bf16[64,256]{1,0:T(8,128)(2,1)S(1)}, bf16[64,256]{1,0:T(8,128)(2,1)S(1)}, u32[]{:S(2)}, u32[]{:S(2)}) collective-permute-start(bf16[64,256]{1,0:T(8,128)(2,1)S(1)} %get-tuple-element.15), channel_id=1, source_target_pairs={{0,1},{1,0},{2,3},{3,2},{4,5},{5,4},{6,7},{7,6},{8,9},{9,8},{10,11... | collective-permute-start | bytes 98312 | tf_op jit(solution)/shard_map/ppermute | solution.py:40
  239.6 22.1 %collective-permute-start.16 = (bf16[64,256]{1,0:T(8,128)(2,1)S(1)}, bf16[64,256]{1,0:T(8,128)(2,1)S(1)}, u32[]{:S(2)}, u32[]{:S(2)}) collective-permute-start(bf16[64,256]{1,0:T(8,128)(2,1)S(1)} %get-tuple-element.16), channel_id=1, source_target_pairs={{2,0},{4,2},{6,4},{8,6},{10,8},{12,10},{14,12},{16,14},{18,16},{20... | collective-permute-start | bytes 98312 | tf_op jit(solution)/shard_map/ppermute | solution.py:39
  252.8 8.8 %collective-permute-start.14 = (f32[1,128]{1,0:T(1,128)S(1)}, f32[1,128]{1,0:T(1,128)S(1)}, u32[]{:S(2)}, u32[]{:S(2)}) collective-permute-start(f32[1,128]{1,0:T(1,128)S(1)} %bitcast.102), channel_id=1, source_target_pairs={{0,1},{1,0},{2,3},{3,2},{4,5},{5,4},{6,7},{7,6},{8,9},{9,8},{10,11... | collective-permute-start | bytes 1544 | tf_op jit(solution)/shard_map/ppermute | solution.py:153
  262.8 5.6 %collective-permute-start.20 = (bf16[64,256]{1,0:T(8,128)(2,1)S(1)}, bf16[64,256]{1,0:T(8,128)(2,1)S(1)}, u32[]{:S(2)}, u32[]{:S(2)}) collective-permute-start(bf16[64,256]{1,0:T(8,128)(2,1)S(1)} %get-tuple-element.12), channel_id=1, source_target_pairs={{0,1},{1,0},{2,3},{3,2},{4,5},{5,4},{6,7},{7,6},{8,9},{9,8},{10,11... | collective-permute-start | bytes 98312 | tf_op jit(solution)/shard_map/ppermute | solution.py:40
  289.3 18.7 %all-to-all-start.9 = ((f32[16,1,64]{2,1,0:T(1,128)}), f32[16,1,64]{2,1,0:T(1,128)S(1)}, u32[]{:S(2)}, u32[]{:S(2)}) async-start(f32[16,1,64]{2,1,0:T(1,128)} %broadcast_in_dim.57), calls=%async_computation.9 | async-start | bytes 16384 | tf_op jit(solution)/shard_map/all_to_all | solution.py:16
  296.8 11.3 %collective-permute-start.21 = (bf16[64,256]{1,0:T(8,128)(2,1)S(1)}, bf16[64,256]{1,0:T(8,128)(2,1)S(1)}, u32[]{:S(2)}, u32[]{:S(2)}) collective-permute-start(bf16[64,256]{1,0:T(8,128)(2,1)S(1)} %get-tuple-element.8), channel_id=1, source_target_pairs={{0,2},{2,4},{4,6},{6,8},{8,10},{10,12},{12,14},{14,16},{16,18},{18... | collective-permute-start | bytes 98312 | tf_op jit(solution)/shard_map/ppermute | solution.py:38
  299.0 9.1 %collective-permute-start.23 = (bf16[64,256]{1,0:T(8,128)(2,1)S(1)}, bf16[64,256]{1,0:T(8,128)(2,1)S(1)}, u32[]{:S(2)}, u32[]{:S(2)}) collective-permute-start(bf16[64,256]{1,0:T(8,128)(2,1)S(1)} %get-tuple-element.9), channel_id=1, source_target_pairs={{0,1},{1,0},{2,3},{3,2},{4,5},{5,4},{6,7},{7,6},{8,9},{9,8},{10,11... | collective-permute-start | bytes 98312 | tf_op jit(solution)/shard_map/ppermute | solution.py:40
  302.1 6.0 %collective-permute-start.22 = (bf16[64,256]{1,0:T(8,128)(2,1)S(1)}, bf16[64,256]{1,0:T(8,128)(2,1)S(1)}, u32[]{:S(2)}, u32[]{:S(2)}) collective-permute-start(bf16[64,256]{1,0:T(8,128)(2,1)S(1)} %get-tuple-element.10), channel_id=1, source_target_pairs={{2,0},{4,2},{6,4},{8,6},{10,8},{12,10},{14,12},{16,14},{18,16},{20... | collective-permute-start | bytes 98312 | tf_op jit(solution)/shard_map/ppermute | solution.py:39
  (30 other events, 492.6 us)

commit v3 on v2

--- a/solution.py
+++ b/solution.py
@@ -16,10 +16,20 @@
     return lax.all_to_all(copies, axes, 0, 0, tiled=False)
 
 
-def gather_blocks(block):
-    stage = spread(block, "z")
-    stage = spread(stage, ("x", "y"))
-    return stage.reshape((-1,) + block.shape)
+def along_z(block):
+    return spread(block, "z").reshape(-1, block.shape[1])
+
+
+def across(block):
+    return spread(block, ("x", "y"))
+
+
+def gather_with_sum(block, partial):
+    rows = block.shape[0]
+    stage = spread(jnp.concatenate([block, in_pieces(partial)], axis=0), "z")
+    sums = jnp.sum(stage[:, rows:, :].astype(jnp.float32), axis=(0, 1))[None, :]
+    rest = stage[:, :rows, :].reshape(-1, block.shape[1])
+    return across(jnp.concatenate([rest, in_pieces(sums)], axis=0))
 
 
 def total(partial):
@@ -110,8 +120,8 @@
     length = nz * ny * half
     result = jnp.zeros((4 * rows, 128), jnp.float32)
     for x in range(nx):
-        order = [x * ny * nz + y * nz + z for z in range(nz) for y in range(ny)]
-        part = jnp.concatenate([blocks_ref[p, 0:half, :] for p in order], axis=0)
+        order = [(x * ny + y, z * half) for z in range(nz) for y in range(ny)]
+        part = jnp.concatenate([blocks_ref[p, r : r + half, :] for p, r in order], axis=0)
         result += jnp.dot(
             padded_ref[:, x * length : (x + 1) * length], part, preferred_element_type=jnp.float32
         )
@@ -124,7 +134,7 @@
     if out_ref.shape[0] > rows:
         sums = jnp.zeros((8, 128), jnp.float32)
         for p in range(blocks_ref.shape[0]):
-            sums += blocks_ref[p, half : half + 8, :].astype(jnp.float32)
+            sums += blocks_ref[p, nz * half : nz * half + 8, :].astype(jnp.float32)
         out_ref[rows : rows + 8, :] = sums
 
 
@@ -132,7 +142,7 @@
     rows = padded.shape[0] // 4
     return pl.pallas_call(
         product_kernel,
-        out_shape=jax.ShapeDtypeStruct((rows + blocks.shape[1] - rows // 2, 128), jnp.float32),
+        out_shape=jax.ShapeDtypeStruct((rows + blocks.shape[1] - XYZ[1] * (rows // 2), 128), jnp.float32),
         interpret=INTERPRET,
         name="coarse_product",
     )(padded, blocks)
@@ -153,50 +163,92 @@
     return partial + lax.ppermute(partial, "c", [(0, 1), (1, 0)])
 
 
-def lift_kernel(info_ref, low_ref, high_ref, modes_ref, out_ref):
-    slots = modes_ref.shape[0]
+def direction_kernel(info_ref, *refs):
+    blocks = refs[:8]
+    modes_ref, near_modes_ref, smoothed_ref, near_smoothed_ref, exists_ref = refs[8:13]
+    out_ref, near_ref, moved_ref = refs[-3:]
+    slots, width = modes_ref.shape
+    load_count = out_ref.shape[0]
+    face = width // 4
     half_slots = slots // 2
-    window = jnp.concatenate([low_ref[0, 0:half_slots, :], high_ref[0, 0:half_slots, :]], axis=0)
     rank = lax.broadcasted_iota(jnp.int32, (slots, slots), 0)
     column = lax.broadcasted_iota(jnp.int32, (slots, slots), 1)
-    offset = info_ref[2] + rank
-    row = (offset // 32) * 16 + offset % 16
-    half = (offset // 16) % 2
-    hit = jnp.logical_and(row == column, rank < info_ref[3])
-    first = jnp.where(jnp.logical_and(hit, half == 0), 1.0, 0.0).astype(jnp.bfloat16)
-    second = jnp.where(jnp.logical_and(hit, half == 1), 1.0, 0.0).astype(jnp.bfloat16)
-    picked = jnp.dot(first, window, preferred_element_type=jnp.float32) + pltpu.roll(
-        jnp.dot(second, window, preferred_element_type=jnp.float32), 64, 1
-    )
-    lifted = lax.dot_general(
-        picked.astype(jnp.bfloat16),
-        modes_ref[...],
-        (((0,), (0,)), ((), ())),
-        preferred_element_type=jnp.float32,
-    )
-    out_ref[...] = lifted[: out_ref.shape[0]]
-
-
-def lift(info, blocks, modes):
-    block_rows = blocks.shape[1]
-    load_count = 64
-    width = modes.shape[1]
+
+    def lifted(which, rows):
+        window = jnp.concatenate([blocks[2 * which][0], blocks[2 * which + 1][0]], axis=0)
+        offset = info_ref[4 * which + 2] + rank
+        row = (offset // slots) * half_slots + offset % half_slots
+        second = (offset // half_slots) % 2 == 1
+        hit = jnp.logical_and(row == column, rank < info_ref[4 * which + 3])
+        low = jnp.where(jnp.logical_and(hit, jnp.logical_not(second)), 1.0, 0.0)
+        high = jnp.where(jnp.logical_and(hit, second), 1.0, 0.0)
+        picked = jnp.dot(
+            low.astype(jnp.bfloat16), window, preferred_element_type=jnp.float32
+        ) + pltpu.roll(
+            jnp.dot(high.astype(jnp.bfloat16), window, preferred_element_type=jnp.float32), 64, 1
+        )
+        result = lax.dot_general(
+            picked.astype(jnp.bfloat16),
+            rows,
+            (((0,), (0,)), ((), ())),
+            preferred_element_type=jnp.float32,
+        )
+        return result[:load_count]
+
+    local = smoothed_ref[...].astype(jnp.float32) - near_smoothed_ref[...].astype(jnp.float32)
+    direction = local + lifted(0, modes_ref[...])
+    near_lifted = jnp.concatenate(
+        [
+            lifted(1, near_modes_ref[:, :face]),
+            lifted(2, near_modes_ref[:, face : 2 * face]),
+            lifted(3, near_modes_ref[:, 2 * face :]),
+        ],
+        axis=1,
+    )
+    near = near_lifted - exists_ref[...] * local
+    if len(refs) > 16:
+        ratio_ref, previous_ref, near_previous_ref = refs[13:16]
+        ratio = ratio_ref[...]
+        direction += ratio * previous_ref[...]
+        near += ratio * near_previous_ref[...]
+    out_ref[...] = direction
+    near_ref[...] = near
+    moved_ref[...] = (
+        direction.astype(jnp.bfloat16).astype(jnp.float32)
+        - near.astype(jnp.bfloat16).astype(jnp.float32)
+    ).astype(jnp.bfloat16)
+
+
+def next_direction(info, blocks, modes, near_modes, smoothed, near_smoothed, exists, *previous):
+    half_slots = modes.shape[0] // 2
+    nz = XYZ[1]
+
+    def block_spec(k):
+        return pl.BlockSpec(
+            (1, half_slots, 128), lambda i, info: (info[k] // nz, info[k] % nz, 0)
+        )
+
+    def whole(array):
+        return pl.BlockSpec(array.shape, lambda i, info: (0, 0))
+
+    rest = (modes, near_modes, smoothed, near_smoothed, exists) + previous
+    shape = smoothed.shape
     return pl.pallas_call(
-        lift_kernel,
-        out_shape=jax.ShapeDtypeStruct((load_count, width), jnp.float32),
+        direction_kernel,
+        out_shape=(
+            jax.ShapeDtypeStruct(shape, jnp.float32),
+            jax.ShapeDtypeStruct(shape, jnp.float32),
+            jax.ShapeDtypeStruct(shape, jnp.bfloat16),
+        ),
         grid_spec=pltpu.PrefetchScalarGridSpec(
             num_scalar_prefetch=1,
             grid=(1,),
-            in_specs=[
-                pl.BlockSpec((1, block_rows, 128), lambda i, info: (info[0], 0, 0)),
-                pl.BlockSpec((1, block_rows, 128), lambda i, info: (info[1], 0, 0)),
-                pl.BlockSpec(modes.shape, lambda i, info: (0, 0)),
-            ],
-            out_specs=pl.BlockSpec((load_count, width), lambda i, info: (0, 0)),
+            in_specs=[block_spec(4 * (k // 2) + k % 2) for k in range(8)] + [whole(r) for r in rest],
+            out_specs=(whole(smoothed), whole(smoothed), whole(smoothed)),
         ),
         interpret=INTERPRET,
-        name="lift",
-    )(info, blocks, blocks, modes)
+        name="next_direction",
+    )(info, *([blocks] * 8), *rest)
 
 
 def shards(loads, flexibility, dirichlet, modes, coarse_inverse, mode_counts):
@@ -211,23 +263,34 @@
     column_width = coarse_inverse.shape[1]
     face = local_loads.shape[1] // 4
 
-    counts = lax.dynamic_index_in_dim(mode_counts, column, 0, keepdims=False)
-    ends = jnp.cumsum(counts)
-    starts = ends - counts
+    all_ends = jnp.cumsum(mode_counts, axis=1)
+    all_starts = all_ends - mode_counts
+    own_first = column == 0
+    counts = jnp.where(own_first, mode_counts[0], mode_counts[1])
+    starts = jnp.where(own_first, all_starts[0], all_starts[1])
     padded = padded_inverse(coarse_inverse, starts, counts, 32 * row - column * column_width)
 
-    own_start = lax.dynamic_index_in_dim(starts, row, 0, keepdims=False)
-    own_count = lax.dynamic_index_in_dim(counts, row, 0, keepdims=False)
-    base = column * column_width + own_start
+    column_of = jnp.stack([column, column, column, 1 - column])
+    row_of = jnp.stack([row, row - 1, row + 1, row])
+    chosen = jnp.logical_and(
+        jnp.arange(rows)[None, None, :] == row_of[:, None, None],
+        jnp.arange(2)[None, :, None] == column_of[:, None, None],
+    )
+    start_of = jnp.sum(jnp.where(chosen, all_starts[None], 0), axis=(1, 2))
+    count_of = jnp.sum(jnp.where(chosen, mode_counts[None], 0), axis=(1, 2))
+    base = column_of * column_width + start_of
     owner = jnp.minimum(base // 32, rows - 2)
 
     def place(chip):
         return (chip // (ny * nz)) * (ny * nz) + (chip % ny) * nz + (chip // ny) % nz
 
-    info = jnp.stack([place(owner), place(owner + 1), base - 32 * owner, own_count])
-
-    doubled = jnp.stack([row > 0, row < rows - 1, column == 1, column == 0])
-    factor = jnp.repeat(jnp.where(doubled, 2.0, 1.0), face)[None, :]
+    info = jnp.stack([place(owner), place(owner + 1), base - 32 * owner, count_of], axis=1)
+    info = info.reshape(-1).astype(jnp.int32)
+
+    has_neighbour = jnp.stack([row > 0, row < rows - 1, column == 1, column == 0])
+    exists = jnp.repeat(jnp.where(has_neighbour, 1.0, 0.0), face)[None, :]
+    factor = 1.0 + exists
+    near_modes = neighbours(mode_block)
 
     def weigh(rounded):
         return lax.dot_general(
@@ -243,31 +306,32 @@
     def apply_flex(values):
         return jnp.dot(values, flex_block, preferred_element_type=jnp.float32).astype(jnp.bfloat16)
 
-    def operator_input(direction):
-        return jump(direction.astype(jnp.bfloat16)).astype(jnp.bfloat16)
-
     def load_dot(left, right):
         return jnp.sum(left.astype(jnp.float32) * right.astype(jnp.float32), axis=1)
 
     residual = jump(apply_flex(local_loads))
     rounded = residual.astype(jnp.bfloat16)
     smoothed = smooth(rounded)
-    first_sums = swapped_sum(
-        coarse_product(padded, gather_blocks(pack(weigh(rounded).astype(jnp.bfloat16))))
-    )
+    near_smoothed = neighbours(smoothed)
+    stage = along_z(pack(weigh(rounded).astype(jnp.bfloat16)))
+    stage, padded, info, near_modes, near_smoothed = lax.optimization_barrier(
+        (stage, padded, info, near_modes, near_smoothed)
+    )
+    first_sums = swapped_sum(coarse_product(padded, across(stage)))
     half_slots = first_sums.shape[0] // 2
-    values = gather_blocks(first_sums[:half_slots].astype(jnp.bfloat16))
-    direction = jump(smoothed) + lift(info, values, mode_block)
-
-    moved = operator_input(direction)
+    values = across(along_z(first_sums[:half_slots].astype(jnp.bfloat16)))
+    direction, near_direction, moved = next_direction(
+        info, values, mode_block, near_modes, smoothed, near_smoothed, exists
+    )
+
     pushed = apply_flex(moved)
     partials = jnp.concatenate([load_dot(residual, direction), load_dot(moved, pushed)])[None, :]
     image = jump(pushed)
     image_high = lax.reduce_precision(image, 8, 7)
     image_low = (image - image_high).astype(jnp.bfloat16)
     image_weights = weigh(image_high.astype(jnp.bfloat16)) + weigh(image_low)
-    block = jnp.concatenate([pack(image_weights.astype(jnp.bfloat16)), in_pieces(partials)], axis=0)
-    second_sums = swapped_sum(coarse_product(padded, gather_blocks(block)))
+    blocks = gather_with_sum(pack(image_weights.astype(jnp.bfloat16)), partials)
+    second_sums = swapped_sum(coarse_product(padded, blocks))
     totals = jnp.sum(second_sums[2 * half_slots :], axis=0)
     energy = totals[:64]
     size = energy / totals[64:]
@@ -282,17 +346,23 @@
     local_energy = load_dot(residual * factor, smoothed)
     partial = local_energy + 0.5 * (coarse_energy[:64] + coarse_energy[64:])
     partial = jnp.concatenate([partial, jnp.zeros_like(partial)])[None, :]
-    block = jnp.concatenate([coarse_values.astype(jnp.bfloat16), in_pieces(partial)], axis=0)
-    values = gather_blocks(block)
-    sums = jnp.sum(values[:, half_slots:, :].astype(jnp.float32), axis=(0, 1))[None, :]
+    near_smoothed = neighbours(smoothed)
+    values = gather_with_sum(coarse_values.astype(jnp.bfloat16), partial)
+    sums = jnp.sum(values[:, nz * half_slots :, :].astype(jnp.float32), axis=(0, 1))[None, :]
     fresh = swapped_sum(sums)[0, :64]
-    direction = (
-        jump(smoothed)
-        + lift(info, values, mode_block)
-        + (fresh / energy)[:, None] * direction
-    )
-
-    moved = operator_input(direction)
+    direction, near_direction, moved = next_direction(
+        info,
+        values,
+        mode_block,
+        near_modes,
+        smoothed,
+        near_smoothed,
+        exists,
+        (fresh / energy)[:, None],
+        direction,
+        near_direction,
+    )
+
     pushed = apply_flex(moved)
     curvature = total(load_dot(moved, pushed)[None, :])[0]
     image = jump(pushed)

time: 313 us -> 299 us (0.955)
  blocking collectives: 84.1 us -> 108 us
  starting transfers between devices: 116 us -> 95.9 us
  waiting for transfers between devices: 51.4 us -> 38.9 us
  local copies, waits for them, and re-layouts: 17 us -> 8.94 us
    all_to_all x4 -> x6, blocking collectives: 84.1 us -> 108 us  [spread(): return lax.all_to_all(copies, axes, 0, 0, tiled=False)]
    all_to_all x6 -> x4, starting transfers between devices: 39.8 us -> 29.7 us  [spread(): return lax.all_to_all(copies, axes, 0, 0, tiled=False)]
    all_to_all x6 -> x4, waiting for transfers between devices: 35.9 us -> 27.2 us  [spread(): return lax.all_to_all(copies, axes, 0, 0, tiled=False)]
    ppermute x7 -> x6, starting transfers between devices: 30.1 us -> 24.2 us  [neighbours(): lax.ppermute(jnp.where(column == 0, east, west), 'c', [(0, 1), (1, 0)])]
    ppermute x7 -> x6, waiting for transfers between devices: 13.4 us -> 9.58 us  [neighbours(): from_below = lax.ppermute(north, WIDE, up)]
    ppermute x7 -> x6, starting transfers between devices: 9.03 us -> 7.73 us  [neighbours(): from_below = lax.ppermute(north, WIDE, up)]
    ppermute x7 -> x6, starting transfers between devices: 18.4 us -> 17.7 us  [neighbours(): from_above = lax.ppermute(south, WIDE, down)]
  transfers between devices with their start and end apart: 30 -> 25, of which waited for: 11 -> 9; matrix products, arithmetic and copies ran while one was open for 5% -> 4% of each run, Pallas kernels for 4% -> 3%
where the time goes in v3:
time: 299 us; the launch traced here: 295 us
  blocking collectives  108 us (36%)
  starting transfers between devices  95.9 us (32%)
  waiting for transfers between devices  38.9 us (13%)
  Pallas kernels  20.6 us (7%)
  other arithmetic  11.2 us (4%)
  matrix products  9.98 us (3%)
  local copies, waits for them, and re-layouts  8.94 us (3%)
    all_to_all x6, blocking collectives, spread(): return lax.all_to_all(copies, axes, 0, 0, tiled=False)  108 us
    all_to_all x4, starting transfers between devices, spread(): return lax.all_to_all(copies, axes, 0, 0, tiled=False)  29.7 us
    all_to_all x4, waiting for transfers between devices, spread(): return lax.all_to_all(copies, axes, 0, 0, tiled=False)  27.2 us
    ppermute x6, starting transfers between devices, neighbours(): lax.ppermute(jnp.where(column == 0, east, west), 'c', [(0, 1), (1, 0)])  24.2 us
    ppermute x6, starting transfers between devices, neighbours(): from_above = lax.ppermute(south, WIDE, down)  17.7 us
    ppermute x3, starting transfers between devices, swapped_sum(): return partial + lax.ppermute(partial, 'c', [(0, 1), (1, 0)])  16.6 us
    ppermute x6, waiting for transfers between devices, neighbours(): from_below = lax.ppermute(north, WIDE, up)  9.58 us
    pallas_call x1, Pallas kernels, padded_inverse(): pl.pallas_call(pad_kernel, out_shape=jax.ShapeDtypeStruct((4 * rows, subd...  7.85 us
  transfers between devices with their start and end apart: 25, of which 9 were waited for; matrix products, arithmetic and copies ran while one was open for 4% of the time, Pallas kernels for 3%

profile of v3, /device:TPU:1, one launch (start us, length us, event | category | flops | bytes accessed | tf_op | source)
XLA Modules:
  0.0 295.1 jit_solution(11174120774311606620)
XLA Ops:
  1.6 4.0 %collective-permute-start.3 = (bf16[32,256]{1,0:T(8,128)(2,1)S(1)}, bf16[32,256]{1,0:T(8,128)(2,1)S(1)}, u32[]{:S(2)}, u32[]{:S(2)}) collective-permute-start(bf16[32,256]{1,0:T(8,128)(2,1)S(1)} %get-tuple-element.46), channel_id=1, source_target_pairs={{0,2},{2,4},{4,6},{6,8},{8,10},{10,12},{12,14},{14,16},{16,18},{18... | collective-permute-start | bytes 49160 | tf_op jit(solution)/shard_map/ppermute | solution.py:48
  5.6 6.0 %collective-permute-start.5 = (bf16[32,256]{1,0:T(8,128)(2,1)S(1)}, bf16[32,256]{1,0:T(8,128)(2,1)S(1)}, u32[]{:S(2)}, u32[]{:S(2)}) collective-permute-start(bf16[32,256]{1,0:T(8,128)(2,1)S(1)} %get-tuple-element.47), channel_id=1, source_target_pairs={{0,1},{1,0},{2,3},{3,2},{4,5},{5,4},{6,7},{7,6},{8,9},{9,8},{10,11... | collective-permute-start | bytes 49160 | tf_op jit(solution)/shard_map/ppermute | solution.py:50
  14.4 4.0 %collective-permute-start = (bf16[64,256]{1,0:T(8,128)(2,1)S(1)}, bf16[64,256]{1,0:T(8,128)(2,1)S(1)}, u32[]{:S(2)}, u32[]{:S(2)}) collective-permute-start(bf16[64,256]{1,0:T(8,128)(2,1)S(1)} %get-tuple-element.43), channel_id=1, source_target_pairs={{0,2},{2,4},{4,6},{6,8},{8,10},{10,12},{12,14},{14,16},{16,18},{18... | collective-permute-start | bytes 98312 | tf_op jit(solution)/shard_map/ppermute | solution.py:48
  25.5 7.8 %pad_inverse.1.padded_ref = bf16[128,4096]{1,0:T(8,128)(2,1)} custom-call(s32[33]{0:T(128)} %pad_add_fusion.1.first_ref, s32[2,32,1,128]{3,2,1,0:T(1,128)} %compare_select_fusion.source_ref, bf16[32,4096]{1,0:T(8,128)(2,1)} %block_ref.1), custom_call_target="tpu_custom_call" | custom-call | tf_op jit(solution)/shard_map/pad_inverse/pallas_call | solution.py:102
  44.1 16.5 %all-to-all-start = ((bf16[16,16,128]{2,1,0:T(8,128)(2,1)}), bf16[16,16,128]{2,1,0:T(8,128)(2,1)S(1)}, u32[]{:S(2)}, u32[]{:S(2)}) async-start(bf16[16,16,128]{2,1,0:T(8,128)(2,1)} %broadcast_in_dim.68), calls=%async_computation | async-start | bytes 131072 | tf_op jit(solution)/shard_map/all_to_all | solution.py:16
  67.6 4.7 %all-to-all-done = bf16[16,16,128]{2,1,0:T(8,128)(2,1)S(1)} async-done(((bf16[16,16,128]{2,1,0:T(8,128)(2,1)}), bf16[16,16,128]{2,1,0:T(8,128)(2,1)S(1)}, u32[]{:S(2)}, u32[]{:S(2)}) %all-to-all-start) | async-done | bytes 65568 | tf_op jit(solution)/shard_map/all_to_all | solution.py:16
  72.5 22.0 %all_to_all.50.blocks_ref = bf16[16,256,128]{2,1,0:T(8,128)(2,1)} all-to-all(bf16[16,256,128]{2,1,0:T(8,128)(2,1)S(1)} %broadcast_in_dim.141), channel_id=1, replica_groups=mesh['x'=4,'z'=16,'y'=4,'c'=2] {'x','y'}, dimensions={0} | all-to-all | bytes 2097152 | tf_op jit(solution)/shard_map/all_to_all | solution.py:16
  97.2 5.0 %collective-permute-start.9 = (f32[32,128]{1,0:T(8,128)}, f32[32,128]{1,0:T(8,128)S(1)}, u32[]{:S(2)}, u32[]{:S(2)}) collective-permute-start(f32[32,128]{1,0:T(8,128)} %coarse_product.2), channel_id=1, source_target_pairs={{0,1},{1,0},{2,3},{3,2},{4,5},{5,4},{6,7},{7,6},{8,9},{9,8},{10,11... | collective-permute-start | bytes 49160 | tf_op jit(solution)/shard_map/ppermute | solution.py:163
  104.0 21.3 %all_to_all.51 = bf16[16,16,128]{2,1,0:T(8,128)(2,1)S(1)} all-to-all(bf16[16,16,128]{2,1,0:T(8,128)(2,1)S(1)} %broadcast_in_dim.142), channel_id=1, replica_groups=mesh['x'=4,'z'=16,'y'=4,'c'=2] {'z'}, dimensions={0} | all-to-all | bytes 131072 | tf_op jit(solution)/shard_map/all_to_all | solution.py:16
  126.5 3.7 %all-to-all-start.3 = ((bf16[16,256,128]{2,1,0:T(8,128)(2,1)}), bf16[16,256,128]{2,1,0:T(8,128)(2,1)S(1)}, u32[]{:S(2)}, u32[]{:S(2)}) async-start(bf16[16,256,128]{2,1,0:T(8,128)(2,1)} %broadcast_in_dim.144), calls=%async_computation.3 | async-start | bytes 2097152 | tf_op jit(solution)/shard_map/all_to_all | solution.py:16
  130.8 14.3 %all-to-all-done.3.refs_0_.refs_1_.refs_2_.refs_3_.refs_4_.refs_5_.refs_6_.refs_7_ = bf16[16,256,128]{2,1,0:T(8,128)(2,1)S(1)} async-done(((bf16[16,256,128]{2,1,0:T(8,128)(2,1)}), bf16[16,256,128]{2,1,0:T(8,128)(2,1)S(1)}, u32[]{:S(2)}, u32[]{:S(2)}) %all-to-all-start.3) | async-done | bytes 1048608 | tf_op jit(solution)/shard_map/all_to_all | solution.py:16
  151.3 4.9 %collective-permute-start.12 = (bf16[64,256]{1,0:T(8,128)(2,1)S(1)}, bf16[64,256]{1,0:T(8,128)(2,1)S(1)}, u32[]{:S(2)}, u32[]{:S(2)}) collective-permute-start(bf16[64,256]{1,0:T(8,128)(2,1)S(1)} %get-tuple-element.38), channel_id=1, source_target_pairs={{0,1},{1,0},{2,3},{3,2},{4,5},{5,4},{6,7},{7,6},{8,9},{9,8},{10,11... | collective-permute-start | bytes 98312 | tf_op jit(solution)/shard_map/ppermute | solution.py:50
  163.9 18.9 %all_to_all.52 = bf16[16,24,128]{2,1,0:T(8,128)(2,1)S(1)} all-to-all(bf16[16,24,128]{2,1,0:T(8,128)(2,1)S(1)} %broadcast_in_dim.146), channel_id=1, replica_groups=mesh['x'=4,'z'=16,'y'=4,'c'=2] {'z'}, dimensions={0} | all-to-all | bytes 196608 | tf_op jit(solution)/shard_map/all_to_all | solution.py:16
  183.1 20.2 %all_to_all.53.blocks_ref = bf16[16,264,128]{2,1,0:T(8,128)(2,1)} all-to-all(bf16[16,264,128]{2,1,0:T(8,128)(2,1)S(1)} %broadcast_in_dim.147), channel_id=1, replica_groups=mesh['x'=4,'z'=16,'y'=4,'c'=2] {'x','y'}, dimensions={0} | all-to-all | bytes 2162688 | tf_op jit(solution)/shard_map/all_to_all | solution.py:16
  206.1 6.2 %collective-permute-start.13 = (f32[40,128]{1,0:T(8,128)}, f32[40,128]{1,0:T(8,128)S(1)}, u32[]{:S(2)}, u32[]{:S(2)}) collective-permute-start(f32[40,128]{1,0:T(8,128)} %coarse_product.3), channel_id=1, source_target_pairs={{0,1},{1,0},{2,3},{3,2},{4,5},{5,4},{6,7},{7,6},{8,9},{9,8},{10,11... | collective-permute-start | bytes 61448 | tf_op jit(solution)/shard_map/ppermute | solution.py:163
  217.8 15.1 %all_to_all.54 = bf16[16,24,128]{2,1,0:T(8,128)(2,1)S(1)} all-to-all(bf16[16,24,128]{2,1,0:T(8,128)(2,1)S(1)} %broadcast_in_dim.148), channel_id=1, replica_groups=mesh['x'=4,'z'=16,'y'=4,'c'=2] {'z'}, dimensions={0} | all-to-all | bytes 196608 | tf_op jit(solution)/shard_map/all_to_all | solution.py:16
  234.2 3.7 %all-to-all-start.7 = ((bf16[16,264,128]{2,1,0:T(8,128)(2,1)}), bf16[16,264,128]{2,1,0:T(8,128)(2,1)S(1)}, u32[]{:S(2)}, u32[]{:S(2)}) async-start(bf16[16,264,128]{2,1,0:T(8,128)(2,1)} %broadcast_in_dim.149), calls=%async_computation.7 | async-start | bytes 2162688 | tf_op jit(solution)/shard_map/all_to_all | solution.py:16
  239.4 4.6 %collective-permute-start.17 = (bf16[64,256]{1,0:T(8,128)(2,1)S(1)}, bf16[64,256]{1,0:T(8,128)(2,1)S(1)}, u32[]{:S(2)}, u32[]{:S(2)}) collective-permute-start(bf16[64,256]{1,0:T(8,128)(2,1)S(1)} %get-tuple-element.35), channel_id=1, source_target_pairs={{0,1},{1,0},{2,3},{3,2},{4,5},{5,4},{6,7},{7,6},{8,9},{9,8},{10,11... | collective-permute-start | bytes 98312 | tf_op jit(solution)/shard_map/ppermute | solution.py:50
  244.0 4.0 %collective-permute-start.15 = (bf16[64,256]{1,0:T(8,128)(2,1)}, bf16[64,256]{1,0:T(8,128)(2,1)}, u32[]{:S(2)}, u32[]{:S(2)}) collective-permute-start(bf16[64,256]{1,0:T(8,128)(2,1)} %get-tuple-element.34), channel_id=1, source_target_pairs={{0,2},{2,4},{4,6},{6,8},{8,10},{10,12},{12,14},{14,16},{16,18},{18... | collective-permute-start | bytes 98312 | tf_op jit(solution)/shard_map/ppermute | solution.py:48
  252.9 5.4 %collective-permute-start.14 = (f32[1,128]{1,0:T(1,128)S(1)}, f32[1,128]{1,0:T(1,128)S(1)}, u32[]{:S(2)}, u32[]{:S(2)}) collective-permute-start(f32[1,128]{1,0:T(1,128)S(1)} %bitcast.137), channel_id=1, source_target_pairs={{0,1},{1,0},{2,3},{3,2},{4,5},{5,4},{6,7},{7,6},{8,9},{9,8},{10,11... | collective-permute-start | bytes 1544 | tf_op jit(solution)/shard_map/ppermute | solution.py:163
  260.4 3.9 %next_direction.3 = (f32[64,1024]{1,0:T(8,128)}, f32[64,1024]{1,0:T(8,128)}, bf16[64,1024]{1,0:T(8,128)(2,1)}) custom-call(s32[16]{0:T(128)} %reshape.836.info_ref, bf16[16,264,128]{2,1,0:T(8,128)(2,1)} %copy-done.1, bf16[16,264,128]{2,1,0:T(8,128)(2,1)} %copy-done.1, bf16[16,264,128]{2,1,0:T(8,128)(2,1)} %copy-done.1, bf16[16,264,128]{2,1,0:T(8,128)(2,1)} %copy-done.1, ...), custom_call_target="tpu_custom_call" | custom-call | tf_op jit(solution)/shard_map/next_direction/pallas_call | solution.py:236
  265.9 10.6 %all_to_all.55 = f32[32,1,64]{2,1,0:T(1,128)S(1)} all-to-all(f32[32,1,64]{2,1,0:T(1,128)S(1)} %broadcast_in_dim.152), channel_id=1, replica_groups=mesh['x'=4,'z'=16,'y'=4,'c'=2] {'x','y','c'}, dimensions={0} | all-to-all | bytes 16384 | tf_op jit(solution)/shard_map/all_to_all | solution.py:16
  277.1 5.8 %all-to-all-start.9 = ((f32[16,1,64]{2,1,0:T(1,128)}), f32[16,1,64]{2,1,0:T(1,128)S(1)}, u32[]{:S(2)}, u32[]{:S(2)}) async-start(f32[16,1,64]{2,1,0:T(1,128)} %broadcast_in_dim.153), calls=%async_computation.9 | async-start | bytes 16384 | tf_op jit(solution)/shard_map/all_to_all | solution.py:16
  289.6 4.6 %all-to-all-done.9 = f32[16,1,64]{2,1,0:T(1,128)S(1)} async-done(((f32[16,1,64]{2,1,0:T(1,128)}), f32[16,1,64]{2,1,0:T(1,128)S(1)}, u32[]{:S(2)}, u32[]{:S(2)}) %all-to-all-start.9) | async-done | bytes 4128 | tf_op jit(solution)/shard_map/all_to_all | solution.py:16
  (193 shorter events, 76.3 us)
Async XLA Ops:
  1.6 33.1 %collective-permute-start.3 = (bf16[32,256]{1,0:T(8,128)(2,1)S(1)}, bf16[32,256]{1,0:T(8,128)(2,1)S(1)}, u32[]{:S(2)}, u32[]{:S(2)}) collective-permute-start(bf16[32,256]{1,0:T(8,128)(2,1)S(1)} %get-tuple-element.46), channel_id=1, source_target_pairs={{0,2},{2,4},{4,6},{6,8},{8,10},{10,12},{12,14},{14,16},{16,18},{18... | collective-permute-start | bytes 49160 | tf_op jit(solution)/shard_map/ppermute | solution.py:48
  5.6 27.8 %collective-permute-start.5 = (bf16[32,256]{1,0:T(8,128)(2,1)S(1)}, bf16[32,256]{1,0:T(8,128)(2,1)S(1)}, u32[]{:S(2)}, u32[]{:S(2)}) collective-permute-start(bf16[32,256]{1,0:T(8,128)(2,1)S(1)} %get-tuple-element.47), channel_id=1, source_target_pairs={{0,1},{1,0},{2,3},{3,2},{4,5},{5,4},{6,7},{7,6},{8,9},{9,8},{10,11... | collective-permute-start | bytes 49160 | tf_op jit(solution)/shard_map/ppermute | solution.py:50
  11.6 23.1 %collective-permute-start.4 = (bf16[32,256]{1,0:T(8,128)(2,1)S(1)}, bf16[32,256]{1,0:T(8,128)(2,1)S(1)}, u32[]{:S(2)}, u32[]{:S(2)}) collective-permute-start(bf16[32,256]{1,0:T(8,128)(2,1)S(1)} %get-tuple-element.48), channel_id=1, source_target_pairs={{2,0},{4,2},{6,4},{8,6},{10,8},{12,10},{14,12},{16,14},{18,16},{20... | collective-permute-start | bytes 49160 | tf_op jit(solution)/shard_map/ppermute | solution.py:49
  14.4 21.0 %collective-permute-start = (bf16[64,256]{1,0:T(8,128)(2,1)S(1)}, bf16[64,256]{1,0:T(8,128)(2,1)S(1)}, u32[]{:S(2)}, u32[]{:S(2)}) collective-permute-start(bf16[64,256]{1,0:T(8,128)(2,1)S(1)} %get-tuple-element.43), channel_id=1, source_target_pairs={{0,2},{2,4},{4,6},{6,8},{8,10},{10,12},{12,14},{14,16},{16,18},{18... | collective-permute-start | bytes 98312 | tf_op jit(solution)/shard_map/ppermute | solution.py:48
  18.4 17.0 %collective-permute-start.2 = (bf16[64,256]{1,0:T(8,128)(2,1)S(1)}, bf16[64,256]{1,0:T(8,128)(2,1)S(1)}, u32[]{:S(2)}, u32[]{:S(2)}) collective-permute-start(bf16[64,256]{1,0:T(8,128)(2,1)S(1)} %get-tuple-element.44), channel_id=1, source_target_pairs={{0,1},{1,0},{2,3},{3,2},{4,5},{5,4},{6,7},{7,6},{8,9},{9,8},{10,11... | collective-permute-start | bytes 98312 | tf_op jit(solution)/shard_map/ppermute | solution.py:50
  33.4 4.6 %collective-permute-start.1 = (bf16[64,256]{1,0:T(8,128)(2,1)S(1)}, bf16[64,256]{1,0:T(8,128)(2,1)S(1)}, u32[]{:S(2)}, u32[]{:S(2)}) collective-permute-start(bf16[64,256]{1,0:T(8,128)(2,1)S(1)} %get-tuple-element.45), channel_id=1, source_target_pairs={{2,0},{4,2},{6,4},{8,6},{10,8},{12,10},{14,12},{16,14},{18,16},{20... | collective-permute-start | bytes 98312 | tf_op jit(solution)/shard_map/ppermute | solution.py:49
  40.3 22.9 %collective-permute-start.8 = (bf16[64,256]{1,0:T(8,128)(2,1)S(1)}, bf16[64,256]{1,0:T(8,128)(2,1)S(1)}, u32[]{:S(2)}, u32[]{:S(2)}) collective-permute-start(bf16[64,256]{1,0:T(8,128)(2,1)S(1)} %get-tuple-element.41), channel_id=1, source_target_pairs={{0,1},{1,0},{2,3},{3,2},{4,5},{5,4},{6,7},{7,6},{8,9},{9,8},{10,11... | collective-permute-start | bytes 98312 | tf_op jit(solution)/shard_map/ppermute | solution.py:50
  44.1 28.2 %all-to-all-start = ((bf16[16,16,128]{2,1,0:T(8,128)(2,1)}), bf16[16,16,128]{2,1,0:T(8,128)(2,1)S(1)}, u32[]{:S(2)}, u32[]{:S(2)}) async-start(bf16[16,16,128]{2,1,0:T(8,128)(2,1)} %broadcast_in_dim.68), calls=%async_computation | async-start | bytes 131072 | tf_op jit(solution)/shard_map/all_to_all | solution.py:16
  62.0 5.0 %collective-permute-start.7 = (bf16[64,256]{1,0:T(8,128)(2,1)S(1)}, bf16[64,256]{1,0:T(8,128)(2,1)S(1)}, u32[]{:S(2)}, u32[]{:S(2)}) collective-permute-start(bf16[64,256]{1,0:T(8,128)(2,1)S(1)} %get-tuple-element.42), channel_id=1, source_target_pairs={{2,0},{4,2},{6,4},{8,6},{10,8},{12,10},{14,12},{16,14},{18,16},{20... | collective-permute-start | bytes 98312 | tf_op jit(solution)/shard_map/ppermute | solution.py:49
  97.2 6.0 %collective-permute-start.9 = (f32[32,128]{1,0:T(8,128)}, f32[32,128]{1,0:T(8,128)S(1)}, u32[]{:S(2)}, u32[]{:S(2)}) collective-permute-start(f32[32,128]{1,0:T(8,128)} %coarse_product.2), channel_id=1, source_target_pairs={{0,1},{1,0},{2,3},{3,2},{4,5},{5,4},{6,7},{7,6},{8,9},{9,8},{10,11... | collective-permute-start | bytes 49160 | tf_op jit(solution)/shard_map/ppermute | solution.py:163
  126.5 18.7 %all-to-all-start.3 = ((bf16[16,256,128]{2,1,0:T(8,128)(2,1)}), bf16[16,256,128]{2,1,0:T(8,128)(2,1)S(1)}, u32[]{:S(2)}, u32[]{:S(2)}) async-start(bf16[16,256,128]{2,1,0:T(8,128)(2,1)} %broadcast_in_dim.144), calls=%async_computation.3 | async-start | bytes 2097152 | tf_op jit(solution)/shard_map/all_to_all | solution.py:16
  151.3 8.7 %collective-permute-start.12 = (bf16[64,256]{1,0:T(8,128)(2,1)S(1)}, bf16[64,256]{1,0:T(8,128)(2,1)S(1)}, u32[]{:S(2)}, u32[]{:S(2)}) collective-permute-start(bf16[64,256]{1,0:T(8,128)(2,1)S(1)} %get-tuple-element.38), channel_id=1, source_target_pairs={{0,1},{1,0},{2,3},{3,2},{4,5},{5,4},{6,7},{7,6},{8,9},{9,8},{10,11... | collective-permute-start | bytes 98312 | tf_op jit(solution)/shard_map/ppermute | solution.py:50
  156.6 3.5 %collective-permute-start.10 = (bf16[64,256]{1,0:T(8,128)(2,1)S(1)}, bf16[64,256]{1,0:T(8,128)(2,1)S(1)}, u32[]{:S(2)}, u32[]{:S(2)}) collective-permute-start(bf16[64,256]{1,0:T(8,128)(2,1)S(1)} %get-tuple-element.37), channel_id=1, source_target_pairs={{0,2},{2,4},{4,6},{6,8},{8,10},{10,12},{12,14},{14,16},{16,18},{18... | collective-permute-start | bytes 98312 | tf_op jit(solution)/shard_map/ppermute | solution.py:48
  158.8 4.7 %collective-permute-start.11 = (bf16[64,256]{1,0:T(8,128)(2,1)S(1)}, bf16[64,256]{1,0:T(8,128)(2,1)S(1)}, u32[]{:S(2)}, u32[]{:S(2)}) collective-permute-start(bf16[64,256]{1,0:T(8,128)(2,1)S(1)} %get-tuple-element.39), channel_id=1, source_target_pairs={{2,0},{4,2},{6,4},{8,6},{10,8},{12,10},{14,12},{16,14},{18,16},{20... | collective-permute-start | bytes 98312 | tf_op jit(solution)/shard_map/ppermute | solution.py:49
  206.1 7.3 %collective-permute-start.13 = (f32[40,128]{1,0:T(8,128)}, f32[40,128]{1,0:T(8,128)S(1)}, u32[]{:S(2)}, u32[]{:S(2)}) collective-permute-start(f32[40,128]{1,0:T(8,128)} %coarse_product.3), channel_id=1, source_target_pairs={{0,1},{1,0},{2,3},{3,2},{4,5},{5,4},{6,7},{7,6},{8,9},{9,8},{10,11... | collective-permute-start | bytes 61448 | tf_op jit(solution)/shard_map/ppermute | solution.py:163
  234.2 18.6 %all-to-all-start.7 = ((bf16[16,264,128]{2,1,0:T(8,128)(2,1)}), bf16[16,264,128]{2,1,0:T(8,128)(2,1)S(1)}, u32[]{:S(2)}, u32[]{:S(2)}) async-start(bf16[16,264,128]{2,1,0:T(8,128)(2,1)} %broadcast_in_dim.149), calls=%async_computation.7 | async-start | bytes 2162688 | tf_op jit(solution)/shard_map/all_to_all | solution.py:16
  239.4 9.9 %collective-permute-start.17 = (bf16[64,256]{1,0:T(8,128)(2,1)S(1)}, bf16[64,256]{1,0:T(8,128)(2,1)S(1)}, u32[]{:S(2)}, u32[]{:S(2)}) collective-permute-start(bf16[64,256]{1,0:T(8,128)(2,1)S(1)} %get-tuple-element.35), channel_id=1, source_target_pairs={{0,1},{1,0},{2,3},{3,2},{4,5},{5,4},{6,7},{7,6},{8,9},{9,8},{10,11... | collective-permute-start | bytes 98312 | tf_op jit(solution)/shard_map/ppermute | solution.py:50
  244.0 14.3 %collective-permute-start.15 = (bf16[64,256]{1,0:T(8,128)(2,1)}, bf16[64,256]{1,0:T(8,128)(2,1)}, u32[]{:S(2)}, u32[]{:S(2)}) collective-permute-start(bf16[64,256]{1,0:T(8,128)(2,1)} %get-tuple-element.34), channel_id=1, source_target_pairs={{0,2},{2,4},{4,6},{6,8},{8,10},{10,12},{12,14},{14,16},{16,18},{18... | collective-permute-start | bytes 98312 | tf_op jit(solution)/shard_map/ppermute | solution.py:48
  248.0 10.3 %collective-permute-start.16 = (bf16[64,256]{1,0:T(8,128)(2,1)S(1)}, bf16[64,256]{1,0:T(8,128)(2,1)}, u32[]{:S(2)}, u32[]{:S(2)}) collective-permute-start(bf16[64,256]{1,0:T(8,128)(2,1)S(1)} %get-tuple-element.36), channel_id=1, source_target_pairs={{2,0},{4,2},{6,4},{8,6},{10,8},{12,10},{14,12},{16,14},{18,16},{20... | collective-permute-start | bytes 98312 | tf_op jit(solution)/shard_map/ppermute | solution.py:49
  252.9 6.9 %collective-permute-start.14 = (f32[1,128]{1,0:T(1,128)S(1)}, f32[1,128]{1,0:T(1,128)S(1)}, u32[]{:S(2)}, u32[]{:S(2)}) collective-permute-start(f32[1,128]{1,0:T(1,128)S(1)} %bitcast.137), channel_id=1, source_target_pairs={{0,1},{1,0},{2,3},{3,2},{4,5},{5,4},{6,7},{7,6},{8,9},{9,8},{10,11... | collective-permute-start | bytes 1544 | tf_op jit(solution)/shard_map/ppermute | solution.py:163
  277.1 17.1 %all-to-all-start.9 = ((f32[16,1,64]{2,1,0:T(1,128)}), f32[16,1,64]{2,1,0:T(1,128)S(1)}, u32[]{:S(2)}, u32[]{:S(2)}) async-start(f32[16,1,64]{2,1,0:T(1,128)} %broadcast_in_dim.153), calls=%async_computation.9 | async-start | bytes 16384 | tf_op jit(solution)/shard_map/all_to_all | solution.py:16
  283.0 11.3 %collective-permute-start.18 = (bf16[64,256]{1,0:T(8,128)(2,1)S(1)}, bf16[64,256]{1,0:T(8,128)(2,1)S(1)}, u32[]{:S(2)}, u32[]{:S(2)}) collective-permute-start(bf16[64,256]{1,0:T(8,128)(2,1)S(1)} %get-tuple-element.31), channel_id=1, source_target_pairs={{0,2},{2,4},{4,6},{6,8},{8,10},{10,12},{12,14},{14,16},{16,18},{18... | collective-permute-start | bytes 98312 | tf_op jit(solution)/shard_map/ppermute | solution.py:48
  285.2 9.1 %collective-permute-start.20 = (bf16[64,256]{1,0:T(8,128)(2,1)S(1)}, bf16[64,256]{1,0:T(8,128)(2,1)S(1)}, u32[]{:S(2)}, u32[]{:S(2)}) collective-permute-start(bf16[64,256]{1,0:T(8,128)(2,1)S(1)} %get-tuple-element.32), channel_id=1, source_target_pairs={{0,1},{1,0},{2,3},{3,2},{4,5},{5,4},{6,7},{7,6},{8,9},{9,8},{10,11... | collective-permute-start | bytes 98312 | tf_op jit(solution)/shard_map/ppermute | solution.py:50
  288.3 6.0 %collective-permute-start.19 = (bf16[64,256]{1,0:T(8,128)(2,1)S(1)}, bf16[64,256]{1,0:T(8,128)(2,1)S(1)}, u32[]{:S(2)}, u32[]{:S(2)}) collective-permute-start(bf16[64,256]{1,0:T(8,128)(2,1)S(1)} %get-tuple-element.33), channel_id=1, source_target_pairs={{2,0},{4,2},{6,4},{8,6},{10,8},{12,10},{14,12},{16,14},{18,16},{20... | collective-permute-start | bytes 98312 | tf_op jit(solution)/shard_map/ppermute | solution.py:49
  (25 other events, 434.4 us)

commit v4 on v3

--- a/solution.py
+++ b/solution.py
@@ -109,6 +109,7 @@
         ],
         out_specs=pl.BlockSpec(memory_space=pltpu.VMEM),
         interpret=INTERPRET,
+        compiler_params=pltpu.CompilerParams(vmem_limit_bytes=8 << 20),
         name="pad_inverse",
     )(first, source, block)
 
@@ -143,7 +144,10 @@
     return pl.pallas_call(
         product_kernel,
         out_shape=jax.ShapeDtypeStruct((rows + blocks.shape[1] - XYZ[1] * (rows // 2), 128), jnp.float32),
+        in_specs=[pl.BlockSpec(memory_space=pltpu.VMEM)] * 2,
+        out_specs=pl.BlockSpec(memory_space=pltpu.VMEM),
         interpret=INTERPRET,
+        compiler_params=pltpu.CompilerParams(vmem_limit_bytes=8 << 20),
         name="coarse_product",
     )(padded, blocks)
 
@@ -163,9 +167,8 @@
     return partial + lax.ppermute(partial, "c", [(0, 1), (1, 0)])
 
 
-def direction_kernel(info_ref, *refs):
-    blocks = refs[:8]
-    modes_ref, near_modes_ref, smoothed_ref, near_smoothed_ref, exists_ref = refs[8:13]
+def direction_kernel(info_ref, blocks_ref, *refs):
+    modes_ref, near_modes_ref, smoothed_ref, near_smoothed_ref, exists_ref = refs[:5]
     out_ref, near_ref, moved_ref = refs[-3:]
     slots, width = modes_ref.shape
     load_count = out_ref.shape[0]
@@ -174,8 +177,14 @@
     rank = lax.broadcasted_iota(jnp.int32, (slots, slots), 0)
     column = lax.broadcasted_iota(jnp.int32, (slots, slots), 1)
 
+    def chip_block(chip):
+        start = pl.multiple_of((chip % XYZ[1]) * half_slots, half_slots)
+        return blocks_ref[chip // XYZ[1], pl.ds(start, half_slots), :]
+
     def lifted(which, rows):
-        window = jnp.concatenate([blocks[2 * which][0], blocks[2 * which + 1][0]], axis=0)
+        window = jnp.concatenate(
+            [chip_block(info_ref[4 * which]), chip_block(info_ref[4 * which + 1])], axis=0
+        )
         offset = info_ref[4 * which + 2] + rank
         row = (offset // slots) * half_slots + offset % half_slots
         second = (offset // half_slots) % 2 == 1
@@ -206,8 +215,8 @@
         axis=1,
     )
     near = near_lifted - exists_ref[...] * local
-    if len(refs) > 16:
-        ratio_ref, previous_ref, near_previous_ref = refs[13:16]
+    if len(refs) > 8:
+        ratio_ref, previous_ref, near_previous_ref = refs[5:8]
         ratio = ratio_ref[...]
         direction += ratio * previous_ref[...]
         near += ratio * near_previous_ref[...]
@@ -220,19 +229,9 @@
 
 
 def next_direction(info, blocks, modes, near_modes, smoothed, near_smoothed, exists, *previous):
-    half_slots = modes.shape[0] // 2
-    nz = XYZ[1]
-
-    def block_spec(k):
-        return pl.BlockSpec(
-            (1, half_slots, 128), lambda i, info: (info[k] // nz, info[k] % nz, 0)
-        )
-
-    def whole(array):
-        return pl.BlockSpec(array.shape, lambda i, info: (0, 0))
-
     rest = (modes, near_modes, smoothed, near_smoothed, exists) + previous
     shape = smoothed.shape
+    in_vmem = pl.BlockSpec(memory_space=pltpu.VMEM)
     return pl.pallas_call(
         direction_kernel,
         out_shape=(
@@ -240,15 +239,12 @@
             jax.ShapeDtypeStruct(shape, jnp.float32),
             jax.ShapeDtypeStruct(shape, jnp.bfloat16),
         ),
-        grid_spec=pltpu.PrefetchScalarGridSpec(
-            num_scalar_prefetch=1,
-            grid=(1,),
-            in_specs=[block_spec(4 * (k // 2) + k % 2) for k in range(8)] + [whole(r) for r in rest],
-            out_specs=(whole(smoothed), whole(smoothed), whole(smoothed)),
-        ),
+        in_specs=[pl.BlockSpec(memory_space=pltpu.SMEM)] + [in_vmem] * (1 + len(rest)),
+        out_specs=(in_vmem,) * 3,
         interpret=INTERPRET,
+        compiler_params=pltpu.CompilerParams(vmem_limit_bytes=8 << 20),
         name="next_direction",
-    )(info, *([blocks] * 8), *rest)
+    )(info, blocks, *rest)
 
 
 def shards(loads, flexibility, dirichlet, modes, coarse_inverse, mode_counts):
@@ -263,6 +259,33 @@
     column_width = coarse_inverse.shape[1]
     face = local_loads.shape[1] // 4
 
+    has_neighbour = jnp.stack([row > 0, row < rows - 1, column == 1, column == 0])
+    exists = jnp.repeat(jnp.where(has_neighbour, 1.0, 0.0), face)[None, :]
+    factor = 1.0 + exists
+
+    def weigh(rounded):
+        return lax.dot_general(
+            mode_block, rounded, (((1,), (1,)), ((), ())), preferred_element_type=jnp.float32
+        )
+
+    def smooth(rounded):
+        inner = (rounded.astype(jnp.float32) * factor).astype(jnp.bfloat16)
+        return jnp.dot(inner, precond_block, preferred_element_type=jnp.float32).astype(
+            jnp.bfloat16
+        )
+
+    def apply_flex(values):
+        return jnp.dot(values, flex_block, preferred_element_type=jnp.float32).astype(jnp.bfloat16)
+
+    def load_dot(left, right):
+        return jnp.sum(left.astype(jnp.float32) * right.astype(jnp.float32), axis=1)
+
+    residual = jump(apply_flex(local_loads))
+    rounded = residual.astype(jnp.bfloat16)
+    payload = pack(weigh(rounded).astype(jnp.bfloat16))
+    payload, mode_counts = lax.optimization_barrier((payload, mode_counts))
+    stage = along_z(payload)
+
     all_ends = jnp.cumsum(mode_counts, axis=1)
     all_starts = all_ends - mode_counts
     own_first = column == 0
@@ -287,37 +310,14 @@
     info = jnp.stack([place(owner), place(owner + 1), base - 32 * owner, count_of], axis=1)
     info = info.reshape(-1).astype(jnp.int32)
 
-    has_neighbour = jnp.stack([row > 0, row < rows - 1, column == 1, column == 0])
-    exists = jnp.repeat(jnp.where(has_neighbour, 1.0, 0.0), face)[None, :]
-    factor = 1.0 + exists
-    near_modes = neighbours(mode_block)
-
-    def weigh(rounded):
-        return lax.dot_general(
-            mode_block, rounded, (((1,), (1,)), ((), ())), preferred_element_type=jnp.float32
-        )
-
-    def smooth(rounded):
-        inner = (rounded.astype(jnp.float32) * factor).astype(jnp.bfloat16)
-        return jnp.dot(inner, precond_block, preferred_element_type=jnp.float32).astype(
-            jnp.bfloat16
-        )
-
-    def apply_flex(values):
-        return jnp.dot(values, flex_block, preferred_element_type=jnp.float32).astype(jnp.bfloat16)
-
-    def load_dot(left, right):
-        return jnp.sum(left.astype(jnp.float32) * right.astype(jnp.float32), axis=1)
-
-    residual = jump(apply_flex(local_loads))
-    rounded = residual.astype(jnp.bfloat16)
+    stage, padded, info, rounded = lax.optimization_barrier((stage, padded, info, rounded))
     smoothed = smooth(rounded)
     near_smoothed = neighbours(smoothed)
-    stage = along_z(pack(weigh(rounded).astype(jnp.bfloat16)))
-    stage, padded, info, near_modes, near_smoothed = lax.optimization_barrier(
-        (stage, padded, info, near_modes, near_smoothed)
-    )
-    first_sums = swapped_sum(coarse_product(padded, across(stage)))
+    blocks, near_smoothed, late_modes = lax.optimization_barrier(
+        (across(stage), near_smoothed, mode_block)
+    )
+    near_modes = neighbours(late_modes)
+    first_sums = swapped_sum(coarse_product(padded, blocks))
     half_slots = first_sums.shape[0] // 2
     values = across(along_z(first_sums[:half_slots].astype(jnp.bfloat16)))
     direction, near_direction, moved = next_direction(

time: 299 us -> 280 us (0.936)
  blocking collectives: 108 us -> 87.3 us
  local copies, waits for them, and re-layouts: 8.94 us -> 19.2 us
  waiting for transfers between devices: 38.9 us -> 29 us
  starting transfers between devices: 95.9 us -> 105 us
  Pallas kernels: 20.6 us -> 13.4 us
    all_to_all x6 -> x5, blocking collectives: 108 us -> 87.3 us  [spread(): return lax.all_to_all(copies, axes, 0, 0, tiled=False)]
    all_to_all x4 -> x5, waiting for transfers between devices: 27.2 us -> 10.6 us  [spread(): return lax.all_to_all(copies, axes, 0, 0, tiled=False)]
    unnamed x52 -> x78, local copies, waits for them, and re-layouts: 2.29 us -> 12.1 us
    all_to_all x4 -> x5, starting transfers between devices: 29.7 us -> 36.7 us  [spread(): return lax.all_to_all(copies, axes, 0, 0, tiled=False)]
    ppermute x6, waiting for transfers between devices: 9.58 us -> 14.5 us  [neighbours(): from_below = lax.ppermute(north, WIDE, up)]
    ppermute x6, starting transfers between devices: 24.2 us -> 27.3 us  [neighbours(): lax.ppermute(jnp.where(column == 0, east, west), 'c', [(0, 1), (1, 0)])]
    pallas_call x2, Pallas kernels: 5.43 us -> 2.36 us  [coarse_product(): pl.pallas_call(product_kernel, out_shape=jax.ShapeDtypeStruct((rows + blo...]
  transfers between devices with their start and end apart: 25 -> 26, of which waited for: 9 -> 10; matrix products, arithmetic and copies ran while one was open for 4% -> 4% of each run, Pallas kernels for 3% -> 2%
where the time goes in v4:
time: 280 us; the launch traced here: 276 us
  starting transfers between devices  105 us (38%)
  blocking collectives  87.3 us (31%)
  waiting for transfers between devices  29 us (10%)
  local copies, waits for them, and re-layouts  19.2 us (7%)
  Pallas kernels  13.4 us (5%)
  other arithmetic  12.1 us (4%)
  matrix products  8.06 us (3%)
    all_to_all x5, blocking collectives, spread(): return lax.all_to_all(copies, axes, 0, 0, tiled=False)  87.3 us
    all_to_all x5, starting transfers between devices, spread(): return lax.all_to_all(copies, axes, 0, 0, tiled=False)  36.7 us
    ppermute x6, starting transfers between devices, neighbours(): lax.ppermute(jnp.where(column == 0, east, west), 'c', [(0, 1), (1, 0)])  27.3 us
    ppermute x6, starting transfers between devices, neighbours(): from_above = lax.ppermute(south, WIDE, down)  18.8 us
    ppermute x6, waiting for transfers between devices, neighbours(): from_below = lax.ppermute(north, WIDE, up)  14.5 us
    ppermute x3, starting transfers between devices, swapped_sum(): return partial + lax.ppermute(partial, 'c', [(0, 1), (1, 0)])  14.5 us
    unnamed x78, local copies, waits for them, and re-layouts  12.1 us
    all_to_all x5, waiting for transfers between devices, spread(): return lax.all_to_all(copies, axes, 0, 0, tiled=False)  10.6 us
  transfers between devices with their start and end apart: 26, of which 10 were waited for; matrix products, arithmetic and copies ran while one was open for 4% of the time, Pallas kernels for 2%

profile of v4, /device:TPU:1, one launch (start us, length us, event | category | flops | bytes accessed | tf_op | source)
XLA Modules:
  0.0 275.6 jit_solution(11389016531601553914)
XLA Ops:
  3.6 4.0 %collective-permute-start = (bf16[64,256]{1,0:T(8,128)(2,1)S(1)}, bf16[64,256]{1,0:T(8,128)(2,1)S(1)}, u32[]{:S(2)}, u32[]{:S(2)}) collective-permute-start(bf16[64,256]{1,0:T(8,128)(2,1)S(1)} %get-tuple-element.51), channel_id=1, source_target_pairs={{0,2},{2,4},{4,6},{6,8},{8,10},{10,12},{12,14},{14,16},{16,18},{18... | collective-permute-start | bytes 98312 | tf_op jit(solution)/shard_map/ppermute | solution.py:48
  7.7 6.0 %collective-permute-start.2 = (bf16[64,256]{1,0:T(8,128)(2,1)S(1)}, bf16[64,256]{1,0:T(8,128)(2,1)S(1)}, u32[]{:S(2)}, u32[]{:S(2)}) collective-permute-start(bf16[64,256]{1,0:T(8,128)(2,1)S(1)} %get-tuple-element.52), channel_id=1, source_target_pairs={{0,1},{1,0},{2,3},{3,2},{4,5},{5,4},{6,7},{7,6},{8,9},{9,8},{10,11... | collective-permute-start | bytes 98312 | tf_op jit(solution)/shard_map/ppermute | solution.py:50
  21.4 13.5 %all-to-all-start = ((bf16[16,16,128]{2,1,0:T(8,128)(2,1)}), bf16[16,16,128]{2,1,0:T(8,128)(2,1)S(1)}, u32[]{:S(2)}, u32[]{:S(2)}) async-start(bf16[16,16,128]{2,1,0:T(8,128)(2,1)} %broadcast_in_dim.68), calls=%async_computation | async-start | bytes 131072 | tf_op jit(solution)/shard_map/all_to_all | solution.py:16
  36.9 6.5 %pad_inverse.1.padded_ref = bf16[128,4096]{1,0:T(8,128)(2,1)S(1)} custom-call(s32[33]{0:T(128)S(1)} %pad_add_fusion.1.first_ref, s32[2,32,1,128]{3,2,1,0:T(1,128)S(1)} %compare_select_fusion.source_ref, bf16[32,4096]{1,0:T(8,128)(2,1)S(1)} %copy-done.10), custom_call_target="tpu_custom_call" | custom-call | tf_op jit(solution)/shard_map/pad_inverse/pallas_call | solution.py:102
  47.6 6.8 %all-to-all-start.1 = ((bf16[16,256,128]{2,1,0:T(8,128)(2,1)}), bf16[16,256,128]{2,1,0:T(8,128)(2,1)}, u32[]{:S(2)}, u32[]{:S(2)}) async-start(bf16[16,256,128]{2,1,0:T(8,128)(2,1)} %broadcast_in_dim.74), calls=%async_computation.1 | async-start | bytes 2097152 | tf_op jit(solution)/shard_map/all_to_all | solution.py:16
  56.7 4.9 %collective-permute-start.5 = (bf16[64,256]{1,0:T(8,128)(2,1)S(1)}, bf16[64,256]{1,0:T(8,128)(2,1)S(1)}, u32[]{:S(2)}, u32[]{:S(2)}) collective-permute-start(bf16[64,256]{1,0:T(8,128)(2,1)S(1)} %get-tuple-element.49), channel_id=1, source_target_pairs={{0,1},{1,0},{2,3},{3,2},{4,5},{5,4},{6,7},{7,6},{8,9},{9,8},{10,11... | collective-permute-start | bytes 98312 | tf_op jit(solution)/shard_map/ppermute | solution.py:50
  61.6 3.5 %collective-permute-start.3 = (bf16[64,256]{1,0:T(8,128)(2,1)S(1)}, bf16[64,256]{1,0:T(8,128)(2,1)S(1)}, u32[]{:S(2)}, u32[]{:S(2)}) collective-permute-start(bf16[64,256]{1,0:T(8,128)(2,1)S(1)} %get-tuple-element.48), channel_id=1, source_target_pairs={{0,2},{2,4},{4,6},{6,8},{8,10},{10,12},{12,14},{14,16},{16,18},{18... | collective-permute-start | bytes 98312 | tf_op jit(solution)/shard_map/ppermute | solution.py:48
  77.8 19.9 %all_to_all.50 = bf16[16,16,128]{2,1,0:T(8,128)(2,1)S(1)} all-to-all(bf16[16,16,128]{2,1,0:T(8,128)(2,1)S(1)} %broadcast_in_dim.141), channel_id=1, replica_groups=mesh['x'=4,'z'=16,'y'=4,'c'=2] {'z'}, dimensions={0} | all-to-all | bytes 131072 | tf_op jit(solution)/shard_map/all_to_all | solution.py:16
  98.9 6.9 %all-to-all-start.3 = ((bf16[16,256,128]{2,1,0:T(8,128)(2,1)}), bf16[16,256,128]{2,1,0:T(8,128)(2,1)}, u32[]{:S(2)}, u32[]{:S(2)}) async-start(bf16[16,256,128]{2,1,0:T(8,128)(2,1)} %broadcast_in_dim.143), calls=%async_computation.3 | async-start | bytes 2097152 | tf_op jit(solution)/shard_map/all_to_all | solution.py:16
  105.7 4.2 %collective-permute-start.9 = (bf16[32,256]{1,0:T(8,128)(2,1)S(1)}, bf16[32,256]{1,0:T(8,128)(2,1)S(1)}, u32[]{:S(2)}, u32[]{:S(2)}) collective-permute-start(bf16[32,256]{1,0:T(8,128)(2,1)S(1)} %get-tuple-element.55), channel_id=1, source_target_pairs={{0,1},{1,0},{2,3},{3,2},{4,5},{5,4},{6,7},{7,6},{8,9},{9,8},{10,11... | collective-permute-start | bytes 49160 | tf_op jit(solution)/shard_map/ppermute | solution.py:50
  114.9 5.8 %collective-permute-done.8 = bf16[32,256]{1,0:T(8,128)(2,1)S(1)} collective-permute-done((bf16[32,256]{1,0:T(8,128)(2,1)S(1)}, bf16[32,256]{1,0:T(8,128)(2,1)S(1)}, u32[]{:S(2)}, u32[]{:S(2)}) %collective-permute-start.8) | collective-permute-done | bytes 16416 | tf_op jit(solution)/shard_map/ppermute | solution.py:49
  127.5 4.5 %collective-permute-start.12 = (bf16[64,256]{1,0:T(8,128)(2,1)S(1)}, bf16[64,256]{1,0:T(8,128)(2,1)S(1)}, u32[]{:S(2)}, u32[]{:S(2)}) collective-permute-start(bf16[64,256]{1,0:T(8,128)(2,1)S(1)} %get-tuple-element.46), channel_id=1, source_target_pairs={{0,1},{1,0},{2,3},{3,2},{4,5},{5,4},{6,7},{7,6},{8,9},{9,8},{10,11... | collective-permute-start | bytes 98312 | tf_op jit(solution)/shard_map/ppermute | solution.py:50
  136.0 3.6 %collective-permute-done.11 = bf16[64,256]{1,0:T(8,128)(2,1)S(1)} collective-permute-done((bf16[64,256]{1,0:T(8,128)(2,1)S(1)}, bf16[64,256]{1,0:T(8,128)(2,1)S(1)}, u32[]{:S(2)}, u32[]{:S(2)}) %collective-permute-start.11) | collective-permute-done | bytes 32800 | tf_op jit(solution)/shard_map/ppermute | solution.py:49
  140.3 19.2 %all_to_all.51 = bf16[16,24,128]{2,1,0:T(8,128)(2,1)S(1)} all-to-all(bf16[16,24,128]{2,1,0:T(8,128)(2,1)S(1)} %broadcast_in_dim.146), channel_id=1, replica_groups=mesh['x'=4,'z'=16,'y'=4,'c'=2] {'z'}, dimensions={0} | all-to-all | bytes 196608 | tf_op jit(solution)/shard_map/all_to_all | solution.py:16
  161.0 21.1 %all_to_all.52.blocks_ref = bf16[16,264,128]{2,1,0:T(8,128)(2,1)S(1)} all-to-all(bf16[16,264,128]{2,1,0:T(8,128)(2,1)S(1)} %broadcast_in_dim.147), channel_id=1, replica_groups=mesh['x'=4,'z'=16,'y'=4,'c'=2] {'x','y'}, dimensions={0} | all-to-all | bytes 2162688 | tf_op jit(solution)/shard_map/all_to_all | solution.py:16
  182.7 6.2 %collective-permute-start.13 = (f32[40,128]{1,0:T(8,128)S(1)}, f32[40,128]{1,0:T(8,128)S(1)}, u32[]{:S(2)}, u32[]{:S(2)}) collective-permute-start(f32[40,128]{1,0:T(8,128)S(1)} %coarse_product.3), channel_id=1, source_target_pairs={{0,1},{1,0},{2,3},{3,2},{4,5},{5,4},{6,7},{7,6},{8,9},{9,8},{10,11... | collective-permute-start | bytes 61448 | tf_op jit(solution)/shard_map/ppermute | solution.py:167
  195.2 16.3 %all_to_all.53 = bf16[16,24,128]{2,1,0:T(8,128)(2,1)S(1)} all-to-all(bf16[16,24,128]{2,1,0:T(8,128)(2,1)S(1)} %broadcast_in_dim.148), channel_id=1, replica_groups=mesh['x'=4,'z'=16,'y'=4,'c'=2] {'z'}, dimensions={0} | all-to-all | bytes 196608 | tf_op jit(solution)/shard_map/all_to_all | solution.py:16
  212.7 3.7 %all-to-all-start.7 = ((bf16[16,264,128]{2,1,0:T(8,128)(2,1)}), bf16[16,264,128]{2,1,0:T(8,128)(2,1)S(1)}, u32[]{:S(2)}, u32[]{:S(2)}) async-start(bf16[16,264,128]{2,1,0:T(8,128)(2,1)} %broadcast_in_dim.149), calls=%async_computation.7 | async-start | bytes 2162688 | tf_op jit(solution)/shard_map/all_to_all | solution.py:16
  217.9 4.6 %collective-permute-start.17 = (bf16[64,256]{1,0:T(8,128)(2,1)S(1)}, bf16[64,256]{1,0:T(8,128)(2,1)S(1)}, u32[]{:S(2)}, u32[]{:S(2)}) collective-permute-start(bf16[64,256]{1,0:T(8,128)(2,1)S(1)} %get-tuple-element.43), channel_id=1, source_target_pairs={{0,1},{1,0},{2,3},{3,2},{4,5},{5,4},{6,7},{7,6},{8,9},{9,8},{10,11... | collective-permute-start | bytes 98312 | tf_op jit(solution)/shard_map/ppermute | solution.py:50
  222.5 4.0 %collective-permute-start.15 = (bf16[64,256]{1,0:T(8,128)(2,1)}, bf16[64,256]{1,0:T(8,128)(2,1)}, u32[]{:S(2)}, u32[]{:S(2)}) collective-permute-start(bf16[64,256]{1,0:T(8,128)(2,1)} %get-tuple-element.42), channel_id=1, source_target_pairs={{0,2},{2,4},{4,6},{6,8},{8,10},{10,12},{12,14},{14,16},{16,18},{18... | collective-permute-start | bytes 98312 | tf_op jit(solution)/shard_map/ppermute | solution.py:48
  231.4 5.4 %collective-permute-start.14 = (f32[1,128]{1,0:T(1,128)S(1)}, f32[1,128]{1,0:T(1,128)S(1)}, u32[]{:S(2)}, u32[]{:S(2)}) collective-permute-start(f32[1,128]{1,0:T(1,128)S(1)} %bitcast.138), channel_id=1, source_target_pairs={{0,1},{1,0},{2,3},{3,2},{4,5},{5,4},{6,7},{7,6},{8,9},{9,8},{10,11... | collective-permute-start | bytes 1544 | tf_op jit(solution)/shard_map/ppermute | solution.py:167
  246.2 10.8 %all_to_all.54 = f32[32,1,64]{2,1,0:T(1,128)S(1)} all-to-all(f32[32,1,64]{2,1,0:T(1,128)S(1)} %broadcast_in_dim.152), channel_id=1, replica_groups=mesh['x'=4,'z'=16,'y'=4,'c'=2] {'x','y','c'}, dimensions={0} | all-to-all | bytes 16384 | tf_op jit(solution)/shard_map/all_to_all | solution.py:16
  257.6 5.8 %all-to-all-start.9 = ((f32[16,1,64]{2,1,0:T(1,128)}), f32[16,1,64]{2,1,0:T(1,128)S(1)}, u32[]{:S(2)}, u32[]{:S(2)}) async-start(f32[16,1,64]{2,1,0:T(1,128)} %broadcast_in_dim.153), calls=%async_computation.9 | async-start | bytes 16384 | tf_op jit(solution)/shard_map/all_to_all | solution.py:16
  270.0 4.6 %all-to-all-done.9 = f32[16,1,64]{2,1,0:T(1,128)S(1)} async-done(((f32[16,1,64]{2,1,0:T(1,128)}), f32[16,1,64]{2,1,0:T(1,128)S(1)}, u32[]{:S(2)}, u32[]{:S(2)}) %all-to-all-start.9) | async-done | bytes 4128 | tf_op jit(solution)/shard_map/all_to_all | solution.py:16
  (222 shorter events, 82.3 us)
Async XLA Ops:
  3.6 11.9 %collective-permute-start = (bf16[64,256]{1,0:T(8,128)(2,1)S(1)}, bf16[64,256]{1,0:T(8,128)(2,1)S(1)}, u32[]{:S(2)}, u32[]{:S(2)}) collective-permute-start(bf16[64,256]{1,0:T(8,128)(2,1)S(1)} %get-tuple-element.51), channel_id=1, source_target_pairs={{0,2},{2,4},{4,6},{6,8},{8,10},{10,12},{12,14},{14,16},{16,18},{18... | collective-permute-start | bytes 98312 | tf_op jit(solution)/shard_map/ppermute | solution.py:48
  7.7 7.8 %collective-permute-start.2 = (bf16[64,256]{1,0:T(8,128)(2,1)S(1)}, bf16[64,256]{1,0:T(8,128)(2,1)S(1)}, u32[]{:S(2)}, u32[]{:S(2)}) collective-permute-start(bf16[64,256]{1,0:T(8,128)(2,1)S(1)} %get-tuple-element.52), channel_id=1, source_target_pairs={{0,1},{1,0},{2,3},{3,2},{4,5},{5,4},{6,7},{7,6},{8,9},{9,8},{10,11... | collective-permute-start | bytes 98312 | tf_op jit(solution)/shard_map/ppermute | solution.py:50
  13.7 4.7 %collective-permute-start.1 = (bf16[64,256]{1,0:T(8,128)(2,1)S(1)}, bf16[64,256]{1,0:T(8,128)(2,1)S(1)}, u32[]{:S(2)}, u32[]{:S(2)}) collective-permute-start(bf16[64,256]{1,0:T(8,128)(2,1)S(1)} %get-tuple-element.53), channel_id=1, source_target_pairs={{2,0},{4,2},{6,4},{8,6},{10,8},{12,10},{14,12},{16,14},{18,16},{20... | collective-permute-start | bytes 98312 | tf_op jit(solution)/shard_map/ppermute | solution.py:49
  21.4 25.1 %all-to-all-start = ((bf16[16,16,128]{2,1,0:T(8,128)(2,1)}), bf16[16,16,128]{2,1,0:T(8,128)(2,1)S(1)}, u32[]{:S(2)}, u32[]{:S(2)}) async-start(bf16[16,16,128]{2,1,0:T(8,128)(2,1)} %broadcast_in_dim.68), calls=%async_computation | async-start | bytes 131072 | tf_op jit(solution)/shard_map/all_to_all | solution.py:16
  47.6 24.0 %all-to-all-start.1 = ((bf16[16,256,128]{2,1,0:T(8,128)(2,1)}), bf16[16,256,128]{2,1,0:T(8,128)(2,1)}, u32[]{:S(2)}, u32[]{:S(2)}) async-start(bf16[16,256,128]{2,1,0:T(8,128)(2,1)} %broadcast_in_dim.74), calls=%async_computation.1 | async-start | bytes 2097152 | tf_op jit(solution)/shard_map/all_to_all | solution.py:16
  56.7 9.7 %collective-permute-start.5 = (bf16[64,256]{1,0:T(8,128)(2,1)S(1)}, bf16[64,256]{1,0:T(8,128)(2,1)S(1)}, u32[]{:S(2)}, u32[]{:S(2)}) collective-permute-start(bf16[64,256]{1,0:T(8,128)(2,1)S(1)} %get-tuple-element.49), channel_id=1, source_target_pairs={{0,1},{1,0},{2,3},{3,2},{4,5},{5,4},{6,7},{7,6},{8,9},{9,8},{10,11... | collective-permute-start | bytes 98312 | tf_op jit(solution)/shard_map/ppermute | solution.py:50
  61.6 7.0 %collective-permute-start.3 = (bf16[64,256]{1,0:T(8,128)(2,1)S(1)}, bf16[64,256]{1,0:T(8,128)(2,1)S(1)}, u32[]{:S(2)}, u32[]{:S(2)}) collective-permute-start(bf16[64,256]{1,0:T(8,128)(2,1)S(1)} %get-tuple-element.48), channel_id=1, source_target_pairs={{0,2},{2,4},{4,6},{6,8},{8,10},{10,12},{12,14},{14,16},{16,18},{18... | collective-permute-start | bytes 98312 | tf_op jit(solution)/shard_map/ppermute | solution.py:48
  65.1 5.9 %collective-permute-start.4 = (bf16[64,256]{1,0:T(8,128)(2,1)S(1)}, bf16[64,256]{1,0:T(8,128)(2,1)S(1)}, u32[]{:S(2)}, u32[]{:S(2)}) collective-permute-start(bf16[64,256]{1,0:T(8,128)(2,1)S(1)} %get-tuple-element.50), channel_id=1, source_target_pairs={{2,0},{4,2},{6,4},{8,6},{10,8},{12,10},{14,12},{16,14},{18,16},{20... | collective-permute-start | bytes 98312 | tf_op jit(solution)/shard_map/ppermute | solution.py:49
  98.9 22.4 %all-to-all-start.3 = ((bf16[16,256,128]{2,1,0:T(8,128)(2,1)}), bf16[16,256,128]{2,1,0:T(8,128)(2,1)}, u32[]{:S(2)}, u32[]{:S(2)}) async-start(bf16[16,256,128]{2,1,0:T(8,128)(2,1)} %broadcast_in_dim.143), calls=%async_computation.3 | async-start | bytes 2097152 | tf_op jit(solution)/shard_map/all_to_all | solution.py:16
  105.7 9.1 %collective-permute-start.9 = (bf16[32,256]{1,0:T(8,128)(2,1)S(1)}, bf16[32,256]{1,0:T(8,128)(2,1)S(1)}, u32[]{:S(2)}, u32[]{:S(2)}) collective-permute-start(bf16[32,256]{1,0:T(8,128)(2,1)S(1)} %get-tuple-element.55), channel_id=1, source_target_pairs={{0,1},{1,0},{2,3},{3,2},{4,5},{5,4},{6,7},{7,6},{8,9},{9,8},{10,11... | collective-permute-start | bytes 49160 | tf_op jit(solution)/shard_map/ppermute | solution.py:50
  110.1 4.8 %collective-permute-start.7 = (bf16[32,256]{1,0:T(8,128)(2,1)S(1)}, bf16[32,256]{1,0:T(8,128)(2,1)S(1)}, u32[]{:S(2)}, u32[]{:S(2)}) collective-permute-start(bf16[32,256]{1,0:T(8,128)(2,1)S(1)} %get-tuple-element.54), channel_id=1, source_target_pairs={{0,2},{2,4},{4,6},{6,8},{8,10},{10,12},{12,14},{14,16},{16,18},{18... | collective-permute-start | bytes 49160 | tf_op jit(solution)/shard_map/ppermute | solution.py:48
  113.5 7.1 %collective-permute-start.8 = (bf16[32,256]{1,0:T(8,128)(2,1)S(1)}, bf16[32,256]{1,0:T(8,128)(2,1)S(1)}, u32[]{:S(2)}, u32[]{:S(2)}) collective-permute-start(bf16[32,256]{1,0:T(8,128)(2,1)S(1)} %get-tuple-element.56), channel_id=1, source_target_pairs={{2,0},{4,2},{6,4},{8,6},{10,8},{12,10},{14,12},{16,14},{18,16},{20... | collective-permute-start | bytes 49160 | tf_op jit(solution)/shard_map/ppermute | solution.py:49
  127.5 8.4 %collective-permute-start.12 = (bf16[64,256]{1,0:T(8,128)(2,1)S(1)}, bf16[64,256]{1,0:T(8,128)(2,1)S(1)}, u32[]{:S(2)}, u32[]{:S(2)}) collective-permute-start(bf16[64,256]{1,0:T(8,128)(2,1)S(1)} %get-tuple-element.46), channel_id=1, source_target_pairs={{0,1},{1,0},{2,3},{3,2},{4,5},{5,4},{6,7},{7,6},{8,9},{9,8},{10,11... | collective-permute-start | bytes 98312 | tf_op jit(solution)/shard_map/ppermute | solution.py:50
  134.6 5.0 %collective-permute-start.11 = (bf16[64,256]{1,0:T(8,128)(2,1)S(1)}, bf16[64,256]{1,0:T(8,128)(2,1)S(1)}, u32[]{:S(2)}, u32[]{:S(2)}) collective-permute-start(bf16[64,256]{1,0:T(8,128)(2,1)S(1)} %get-tuple-element.47), channel_id=1, source_target_pairs={{2,0},{4,2},{6,4},{8,6},{10,8},{12,10},{14,12},{16,14},{18,16},{20... | collective-permute-start | bytes 98312 | tf_op jit(solution)/shard_map/ppermute | solution.py:49
  182.7 7.0 %collective-permute-start.13 = (f32[40,128]{1,0:T(8,128)S(1)}, f32[40,128]{1,0:T(8,128)S(1)}, u32[]{:S(2)}, u32[]{:S(2)}) collective-permute-start(f32[40,128]{1,0:T(8,128)S(1)} %coarse_product.3), channel_id=1, source_target_pairs={{0,1},{1,0},{2,3},{3,2},{4,5},{5,4},{6,7},{7,6},{8,9},{9,8},{10,11... | collective-permute-start | bytes 61448 | tf_op jit(solution)/shard_map/ppermute | solution.py:167
  212.7 18.6 %all-to-all-start.7 = ((bf16[16,264,128]{2,1,0:T(8,128)(2,1)}), bf16[16,264,128]{2,1,0:T(8,128)(2,1)S(1)}, u32[]{:S(2)}, u32[]{:S(2)}) async-start(bf16[16,264,128]{2,1,0:T(8,128)(2,1)} %broadcast_in_dim.149), calls=%async_computation.7 | async-start | bytes 2162688 | tf_op jit(solution)/shard_map/all_to_all | solution.py:16
  217.9 9.9 %collective-permute-start.17 = (bf16[64,256]{1,0:T(8,128)(2,1)S(1)}, bf16[64,256]{1,0:T(8,128)(2,1)S(1)}, u32[]{:S(2)}, u32[]{:S(2)}) collective-permute-start(bf16[64,256]{1,0:T(8,128)(2,1)S(1)} %get-tuple-element.43), channel_id=1, source_target_pairs={{0,1},{1,0},{2,3},{3,2},{4,5},{5,4},{6,7},{7,6},{8,9},{9,8},{10,11... | collective-permute-start | bytes 98312 | tf_op jit(solution)/shard_map/ppermute | solution.py:50
  222.5 14.3 %collective-permute-start.15 = (bf16[64,256]{1,0:T(8,128)(2,1)}, bf16[64,256]{1,0:T(8,128)(2,1)}, u32[]{:S(2)}, u32[]{:S(2)}) collective-permute-start(bf16[64,256]{1,0:T(8,128)(2,1)} %get-tuple-element.42), channel_id=1, source_target_pairs={{0,2},{2,4},{4,6},{6,8},{8,10},{10,12},{12,14},{14,16},{16,18},{18... | collective-permute-start | bytes 98312 | tf_op jit(solution)/shard_map/ppermute | solution.py:48
  226.5 10.3 %collective-permute-start.16 = (bf16[64,256]{1,0:T(8,128)(2,1)}, bf16[64,256]{1,0:T(8,128)(2,1)}, u32[]{:S(2)}, u32[]{:S(2)}) collective-permute-start(bf16[64,256]{1,0:T(8,128)(2,1)} %get-tuple-element.44), channel_id=1, source_target_pairs={{2,0},{4,2},{6,4},{8,6},{10,8},{12,10},{14,12},{16,14},{18,16},{20... | collective-permute-start | bytes 98312 | tf_op jit(solution)/shard_map/ppermute | solution.py:49
  231.4 6.9 %collective-permute-start.14 = (f32[1,128]{1,0:T(1,128)S(1)}, f32[1,128]{1,0:T(1,128)S(1)}, u32[]{:S(2)}, u32[]{:S(2)}) collective-permute-start(f32[1,128]{1,0:T(1,128)S(1)} %bitcast.138), channel_id=1, source_target_pairs={{0,1},{1,0},{2,3},{3,2},{4,5},{5,4},{6,7},{7,6},{8,9},{9,8},{10,11... | collective-permute-start | bytes 1544 | tf_op jit(solution)/shard_map/ppermute | solution.py:167
  257.6 17.1 %all-to-all-start.9 = ((f32[16,1,64]{2,1,0:T(1,128)}), f32[16,1,64]{2,1,0:T(1,128)S(1)}, u32[]{:S(2)}, u32[]{:S(2)}) async-start(f32[16,1,64]{2,1,0:T(1,128)} %broadcast_in_dim.153), calls=%async_computation.9 | async-start | bytes 16384 | tf_op jit(solution)/shard_map/all_to_all | solution.py:16
  263.4 11.3 %collective-permute-start.18 = (bf16[64,256]{1,0:T(8,128)(2,1)S(1)}, bf16[64,256]{1,0:T(8,128)(2,1)S(1)}, u32[]{:S(2)}, u32[]{:S(2)}) collective-permute-start(bf16[64,256]{1,0:T(8,128)(2,1)S(1)} %get-tuple-element.39), channel_id=1, source_target_pairs={{0,2},{2,4},{4,6},{6,8},{8,10},{10,12},{12,14},{14,16},{16,18},{18... | collective-permute-start | bytes 98312 | tf_op jit(solution)/shard_map/ppermute | solution.py:48
  265.6 9.1 %collective-permute-start.20 = (bf16[64,256]{1,0:T(8,128)(2,1)S(1)}, bf16[64,256]{1,0:T(8,128)(2,1)S(1)}, u32[]{:S(2)}, u32[]{:S(2)}) collective-permute-start(bf16[64,256]{1,0:T(8,128)(2,1)S(1)} %get-tuple-element.40), channel_id=1, source_target_pairs={{0,1},{1,0},{2,3},{3,2},{4,5},{5,4},{6,7},{7,6},{8,9},{9,8},{10,11... | collective-permute-start | bytes 98312 | tf_op jit(solution)/shard_map/ppermute | solution.py:50
  268.7 6.0 %collective-permute-start.19 = (bf16[64,256]{1,0:T(8,128)(2,1)S(1)}, bf16[64,256]{1,0:T(8,128)(2,1)S(1)}, u32[]{:S(2)}, u32[]{:S(2)}) collective-permute-start(bf16[64,256]{1,0:T(8,128)(2,1)S(1)} %get-tuple-element.41), channel_id=1, source_target_pairs={{2,0},{4,2},{6,4},{8,6},{10,8},{12,10},{14,12},{16,14},{18,16},{20... | collective-permute-start | bytes 98312 | tf_op jit(solution)/shard_map/ppermute | solution.py:49
  (39 other events, 413.8 us)

commit v5 on v4

--- a/solution.py
+++ b/solution.py
@@ -5,6 +5,7 @@
 from jax.experimental.pallas import tpu as pltpu
 from jax.sharding import Mesh, PartitionSpec as P
 
+
 XYZ = (4, 16, 4)
 WIDE = ("x", "z", "y")
 INTERPRET = False
@@ -24,12 +25,15 @@
     return spread(block, ("x", "y"))
 
 
-def gather_with_sum(block, partial):
-    rows = block.shape[0]
-    stage = spread(jnp.concatenate([block, in_pieces(partial)], axis=0), "z")
+def with_sum(block, partial):
+    return jnp.concatenate([block, in_pieces(partial)], axis=0)
+
+
+def summed_along_z(payload):
+    stage = spread(payload, "z")
+    rows = payload.shape[0] - 8
     sums = jnp.sum(stage[:, rows:, :].astype(jnp.float32), axis=(0, 1))[None, :]
-    rest = stage[:, :rows, :].reshape(-1, block.shape[1])
-    return across(jnp.concatenate([rest, in_pieces(sums)], axis=0))
+    return with_sum(stage[:, :rows, :].reshape(-1, payload.shape[1]), sums)
 
 
 def total(partial):
@@ -38,7 +42,7 @@
 
 
 def neighbours(values):
-    load_count, width = values.shape
+    _, width = values.shape
     face = width // 4
     rows = lax.axis_size(WIDE)
     column = lax.axis_index("c")
@@ -167,9 +171,17 @@
     return partial + lax.ppermute(partial, "c", [(0, 1), (1, 0)])
 
 
-def direction_kernel(info_ref, blocks_ref, *refs):
-    modes_ref, near_modes_ref, smoothed_ref, near_smoothed_ref, exists_ref = refs[:5]
-    out_ref, near_ref, moved_ref = refs[-3:]
+def direction_kernel(info_ref, blocks_ref, exists_ref, *refs):
+    copied = (len(refs) - 4) // 2 if len(refs) % 2 == 0 else (len(refs) - 5) // 2
+    sources, buffers, semaphores = refs[:copied], refs[-1 - copied : -1], refs[-1]
+    out_ref, near_ref, moved_ref = refs[-4 - copied : -1 - copied]
+    copies = [
+        pltpu.make_async_copy(source, buffer, semaphores.at[k])
+        for k, (source, buffer) in enumerate(zip(sources, buffers))
+    ]
+    for copy in copies:
+        copy.start()
+    modes_ref, near_modes_ref, smoothed_ref, near_smoothed_ref = buffers[:4]
     slots, width = modes_ref.shape
     load_count = out_ref.shape[0]
     face = width // 4
@@ -181,7 +193,7 @@
         start = pl.multiple_of((chip % XYZ[1]) * half_slots, half_slots)
         return blocks_ref[chip // XYZ[1], pl.ds(start, half_slots), :]
 
-    def lifted(which, rows):
+    def picked(which):
         window = jnp.concatenate(
             [chip_block(info_ref[4 * which]), chip_block(info_ref[4 * which + 1])], axis=0
         )
@@ -191,33 +203,36 @@
         hit = jnp.logical_and(row == column, rank < info_ref[4 * which + 3])
         low = jnp.where(jnp.logical_and(hit, jnp.logical_not(second)), 1.0, 0.0)
         high = jnp.where(jnp.logical_and(hit, second), 1.0, 0.0)
-        picked = jnp.dot(
-            low.astype(jnp.bfloat16), window, preferred_element_type=jnp.float32
-        ) + pltpu.roll(
-            jnp.dot(high.astype(jnp.bfloat16), window, preferred_element_type=jnp.float32), 64, 1
-        )
+        return (
+            jnp.dot(low.astype(jnp.bfloat16), window, preferred_element_type=jnp.float32)
+            + pltpu.roll(
+                jnp.dot(high.astype(jnp.bfloat16), window, preferred_element_type=jnp.float32), 64, 1
+            )
+        ).astype(jnp.bfloat16)
+
+    def lifted(values, rows):
         result = lax.dot_general(
-            picked.astype(jnp.bfloat16),
-            rows,
-            (((0,), (0,)), ((), ())),
-            preferred_element_type=jnp.float32,
+            values, rows, (((0,), (0,)), ((), ())), preferred_element_type=jnp.float32
         )
         return result[:load_count]
 
+    chosen = [picked(which) for which in range(4)]
+    for copy in copies:
+        copy.wait()
     local = smoothed_ref[...].astype(jnp.float32) - near_smoothed_ref[...].astype(jnp.float32)
-    direction = local + lifted(0, modes_ref[...])
+    direction = local + lifted(chosen[0], modes_ref[...])
     near_lifted = jnp.concatenate(
         [
-            lifted(1, near_modes_ref[:, :face]),
-            lifted(2, near_modes_ref[:, face : 2 * face]),
-            lifted(3, near_modes_ref[:, 2 * face :]),
+            lifted(chosen[1], near_modes_ref[:, :face]),
+            lifted(chosen[2], near_modes_ref[:, face : 2 * face]),
+            lifted(chosen[3], near_modes_ref[:, 2 * face :]),
         ],
         axis=1,
     )
     near = near_lifted - exists_ref[...] * local
-    if len(refs) > 8:
-        ratio_ref, previous_ref, near_previous_ref = refs[5:8]
-        ratio = ratio_ref[...]
+    if copied > 4:
+        previous_ref, near_previous_ref = buffers[4:]
+        ratio = refs[copied][...]
         direction += ratio * previous_ref[...]
         near += ratio * near_previous_ref[...]
     out_ref[...] = direction
@@ -228,8 +243,11 @@
     ).astype(jnp.bfloat16)
 
 
-def next_direction(info, blocks, modes, near_modes, smoothed, near_smoothed, exists, *previous):
-    rest = (modes, near_modes, smoothed, near_smoothed, exists) + previous
+def next_direction(
+    info, blocks, exists, modes, near_modes, smoothed, near_smoothed, ratio=None, previous=()
+):
+    copied = (modes, near_modes, smoothed, near_smoothed) + previous
+    ratios = () if ratio is None else (ratio,)
     shape = smoothed.shape
     in_vmem = pl.BlockSpec(memory_space=pltpu.VMEM)
     return pl.pallas_call(
@@ -239,12 +257,16 @@
             jax.ShapeDtypeStruct(shape, jnp.float32),
             jax.ShapeDtypeStruct(shape, jnp.bfloat16),
         ),
-        in_specs=[pl.BlockSpec(memory_space=pltpu.SMEM)] + [in_vmem] * (1 + len(rest)),
+        in_specs=[pl.BlockSpec(memory_space=pltpu.SMEM), in_vmem, in_vmem]
+        + [pl.BlockSpec(memory_space=pltpu.HBM)] * len(copied)
+        + [in_vmem] * len(ratios),
         out_specs=(in_vmem,) * 3,
+        scratch_shapes=[pltpu.VMEM(array.shape, array.dtype) for array in copied]
+        + [pltpu.SemaphoreType.DMA((len(copied),))],
         interpret=INTERPRET,
         compiler_params=pltpu.CompilerParams(vmem_limit_bytes=8 << 20),
         name="next_direction",
-    )(info, blocks, *rest)
+    )(info, blocks, exists, *copied, *ratios)
 
 
 def shards(loads, flexibility, dirichlet, modes, coarse_inverse, mode_counts):
@@ -252,7 +274,7 @@
     flex_block = flexibility[0, 0]
     precond_block = dirichlet[0, 0]
     mode_block = modes[0, 0]
-    nx, nz, ny = XYZ
+    _, nz, ny = XYZ
     rows = lax.axis_size(WIDE)
     row = lax.axis_index(WIDE)
     column = lax.axis_index("c")
@@ -283,8 +305,9 @@
     residual = jump(apply_flex(local_loads))
     rounded = residual.astype(jnp.bfloat16)
     payload = pack(weigh(rounded).astype(jnp.bfloat16))
-    payload, mode_counts = lax.optimization_barrier((payload, mode_counts))
+    payload, mode_counts, late_modes = lax.optimization_barrier((payload, mode_counts, mode_block))
     stage = along_z(payload)
+    near_modes = neighbours(late_modes)
 
     all_ends = jnp.cumsum(mode_counts, axis=1)
     all_starts = all_ends - mode_counts
@@ -313,15 +336,15 @@
     stage, padded, info, rounded = lax.optimization_barrier((stage, padded, info, rounded))
     smoothed = smooth(rounded)
     near_smoothed = neighbours(smoothed)
-    blocks, near_smoothed, late_modes = lax.optimization_barrier(
-        (across(stage), near_smoothed, mode_block)
-    )
-    near_modes = neighbours(late_modes)
-    first_sums = swapped_sum(coarse_product(padded, blocks))
+    blocks = across(stage)
+    products = coarse_product(padded, blocks)
+    first_sums = swapped_sum(products)
     half_slots = first_sums.shape[0] // 2
-    values = across(along_z(first_sums[:half_slots].astype(jnp.bfloat16)))
+    stage = along_z(first_sums[:half_slots].astype(jnp.bfloat16))
+    stage, near_smoothed = lax.optimization_barrier((stage, near_smoothed))
+    values = across(stage)
     direction, near_direction, moved = next_direction(
-        info, values, mode_block, near_modes, smoothed, near_smoothed, exists
+        info, values, exists, mode_block, near_modes, smoothed, near_smoothed
     )
 
     pushed = apply_flex(moved)
@@ -330,37 +353,49 @@
     image_high = lax.reduce_precision(image, 8, 7)
     image_low = (image - image_high).astype(jnp.bfloat16)
     image_weights = weigh(image_high.astype(jnp.bfloat16)) + weigh(image_low)
-    blocks = gather_with_sum(pack(image_weights.astype(jnp.bfloat16)), partials)
-    second_sums = swapped_sum(coarse_product(padded, blocks))
+    payload = with_sum(pack(image_weights.astype(jnp.bfloat16)), partials)
+    payload, late_image = lax.optimization_barrier((payload, image))
+    stage = summed_along_z(payload)
+    image_smoothed = smooth(late_image.astype(jnp.bfloat16))
+    residual_jump, image_jump = residual * factor, late_image * factor
+    energies = (
+        load_dot(residual_jump, smoothed),
+        load_dot(residual_jump, image_smoothed) + load_dot(image_jump, smoothed),
+        load_dot(image_jump, image_smoothed),
+    )
+    stage, energies = lax.optimization_barrier((stage, energies))
+    second_sums = swapped_sum(coarse_product(padded, across(stage)))
     totals = jnp.sum(second_sums[2 * half_slots :], axis=0)
     energy = totals[:64]
     size = energy / totals[64:]
+    local_energy = energies[0] - size * (energies[1] - size * energies[2])
+
+    packed = first_sums - jnp.tile(size, 2)[None, :] * second_sums[: 2 * half_slots]
+    coarse_values = lax.reduce_precision(packed[:half_slots], 8, 7)
+    coarse_energy = jnp.sum(coarse_values * packed[half_slots:], axis=0)
+    partial = local_energy + 0.5 * (coarse_energy[:64] + coarse_energy[64:])
+    partial = jnp.concatenate([partial, jnp.zeros_like(partial)])[None, :]
+    payload = with_sum(coarse_values.astype(jnp.bfloat16), partial)
+    payload, size = lax.optimization_barrier((payload, size))
     multipliers = size[:, None] * direction
     residual = residual - size[:, None] * image
-
-    packed = first_sums - jnp.tile(size, 2)[None, :] * second_sums[: 2 * half_slots]
-    rounded = residual.astype(jnp.bfloat16)
-    smoothed = smooth(rounded)
-    coarse_values = lax.reduce_precision(packed[:half_slots], 8, 7)
-    coarse_energy = jnp.sum(coarse_values * packed[half_slots:], axis=0)
-    local_energy = load_dot(residual * factor, smoothed)
-    partial = local_energy + 0.5 * (coarse_energy[:64] + coarse_energy[64:])
-    partial = jnp.concatenate([partial, jnp.zeros_like(partial)])[None, :]
+    smoothed = smooth(residual.astype(jnp.bfloat16))
     near_smoothed = neighbours(smoothed)
-    values = gather_with_sum(coarse_values.astype(jnp.bfloat16), partial)
+    stage = summed_along_z(payload)
+    stage, smoothed = lax.optimization_barrier((stage, smoothed))
+    values = across(stage)
     sums = jnp.sum(values[:, nz * half_slots :, :].astype(jnp.float32), axis=(0, 1))[None, :]
     fresh = swapped_sum(sums)[0, :64]
     direction, near_direction, moved = next_direction(
         info,
         values,
+        exists,
         mode_block,
         near_modes,
         smoothed,
         near_smoothed,
-        exists,
         (fresh / energy)[:, None],
-        direction,
-        near_direction,
+        (direction, near_direction),
     )
 
     pushed = apply_flex(moved)

time: 280 us -> 290 us (1.036)
  blocking collectives: 87.3 us -> 31.3 us
  waiting for transfers between devices: 29 us -> 56.3 us
  starting transfers between devices: 105 us -> 130 us
  local copies, waits for them, and re-layouts: 19.2 us -> 24.7 us
  other arithmetic: 12.1 us -> 16.6 us
  matrix products: 8.06 us -> 11 us
    all_to_all x5 -> x2, blocking collectives: 87.3 us -> 31.3 us  [spread(): return lax.all_to_all(copies, axes, 0, 0, tiled=False)]
    all_to_all x5 -> x8, waiting for transfers between devices: 10.6 us -> 44.4 us  [spread(): return lax.all_to_all(copies, axes, 0, 0, tiled=False)]
    all_to_all x5 -> x8, starting transfers between devices: 36.7 us -> 59.2 us  [spread(): return lax.all_to_all(copies, axes, 0, 0, tiled=False)]
    ppermute x6, waiting for transfers between devices: 14.5 us -> 11 us  [neighbours(): from_below = lax.ppermute(north, WIDE, up)]
    dot_general x2 -> x3, matrix products: 5.02 us -> 8.05 us  [smooth(): jnp.dot(inner, precond_block, preferred_element_type=jnp.float32)]
    unnamed x78 -> x100, local copies, waits for them, and re-layouts: 12.1 us -> 11.6 us
  transfers between devices with their start and end apart: 26 -> 29, of which waited for: 10 -> 11; matrix products, arithmetic and copies ran while one was open for 4% -> 6% of each run, Pallas kernels for 2% -> 3%
where the time goes in v5:
time: 290 us; the launch traced here: 285 us
  starting transfers between devices  130 us (45%)
  waiting for transfers between devices  56.3 us (19%)
  blocking collectives  31.3 us (11%)
  local copies, waits for them, and re-layouts  24.7 us (9%)
  other arithmetic  16.6 us (6%)
  Pallas kernels  13.7 us (5%)
  matrix products  11 us (4%)
    all_to_all x8, starting transfers between devices, spread(): return lax.all_to_all(copies, axes, 0, 0, tiled=False)  59.2 us
    all_to_all x8, waiting for transfers between devices, spread(): return lax.all_to_all(copies, axes, 0, 0, tiled=False)  44.4 us
    all_to_all x2, blocking collectives, spread(): return lax.all_to_all(copies, axes, 0, 0, tiled=False)  31.3 us
    ppermute x6, starting transfers between devices, neighbours(): lax.ppermute(jnp.where(column == 0, east, west), 'c', [(0, 1), (1, 0)])  25.3 us
    ppermute x6, starting transfers between devices, neighbours(): from_above = lax.ppermute(south, WIDE, down)  20.6 us
    ppermute x3, starting transfers between devices, swapped_sum(): return partial + lax.ppermute(partial, 'c', [(0, 1), (1, 0)])  17.3 us
    unnamed x100, local copies, waits for them, and re-layouts  11.6 us
    ppermute x6, waiting for transfers between devices, neighbours(): from_below = lax.ppermute(north, WIDE, up)  11 us
  transfers between devices with their start and end apart: 29, of which 11 were waited for; matrix products, arithmetic and copies ran while one was open for 6% of the time, Pallas kernels for 3%

profile of v5, /device:TPU:1, one launch (start us, length us, event | category | flops | bytes accessed | tf_op | source)
XLA Modules:
  0.0 285.5 jit_solution(7926004564299728947)
XLA Ops:
  7.7 6.0 %collective-permute-start.2 = (bf16[64,256]{1,0:T(8,128)(2,1)S(1)}, bf16[64,256]{1,0:T(8,128)(2,1)S(1)}, u32[]{:S(2)}, u32[]{:S(2)}) collective-permute-start(bf16[64,256]{1,0:T(8,128)(2,1)S(1)} %get-tuple-element.78), channel_id=1, source_target_pairs={{0,1},{1,0},{2,3},{3,2},{4,5},{5,4},{6,7},{7,6},{8,9},{9,8},{10,11... | collective-permute-start | bytes 98312 | tf_op jit(solution)/shard_map/ppermute | solution.py:54
  21.3 13.5 %all-to-all-start = ((bf16[16,16,128]{2,1,0:T(8,128)(2,1)}), bf16[16,16,128]{2,1,0:T(8,128)(2,1)S(1)}, u32[]{:S(2)}, u32[]{:S(2)}) async-start(bf16[16,16,128]{2,1,0:T(8,128)(2,1)} %broadcast_in_dim.66), calls=%async_computation | async-start | bytes 131072 | tf_op jit(solution)/shard_map/all_to_all | solution.py:17
  36.9 6.5 %pad_inverse.1.padded_ref = bf16[128,4096]{1,0:T(8,128)(2,1)S(1)} custom-call(s32[33]{0:T(128)S(1)} %pad_add_fusion.1.first_ref, s32[2,32,1,128]{3,2,1,0:T(1,128)S(1)} %compare_select_fusion.source_ref, bf16[32,4096]{1,0:T(8,128)(2,1)S(1)} %copy-done.10), custom_call_target="tpu_custom_call" | custom-call | tf_op jit(solution)/shard_map/pad_inverse/pallas_call | solution.py:106
  47.7 6.8 %all-to-all-start.1 = ((bf16[16,256,128]{2,1,0:T(8,128)(2,1)}), bf16[16,256,128]{2,1,0:T(8,128)(2,1)}, u32[]{:S(2)}, u32[]{:S(2)}) async-start(bf16[16,256,128]{2,1,0:T(8,128)(2,1)} %broadcast_in_dim.72), calls=%async_computation.1 | async-start | bytes 2097152 | tf_op jit(solution)/shard_map/all_to_all | solution.py:17
  56.8 4.9 %collective-permute-start.6 = (bf16[64,256]{1,0:T(8,128)(2,1)S(1)}, bf16[64,256]{1,0:T(8,128)(2,1)}, u32[]{:S(2)}, u32[]{:S(2)}) collective-permute-start(bf16[64,256]{1,0:T(8,128)(2,1)S(1)} %get-tuple-element.75), channel_id=1, source_target_pairs={{0,1},{1,0},{2,3},{3,2},{4,5},{5,4},{6,7},{7,6},{8,9},{9,8},{10,11... | collective-permute-start | bytes 98312 | tf_op jit(solution)/shard_map/ppermute | solution.py:54
  61.7 7.2 %all-to-all-done.1.blocks_ref = bf16[16,256,128]{2,1,0:T(8,128)(2,1)} async-done(((bf16[16,256,128]{2,1,0:T(8,128)(2,1)}), bf16[16,256,128]{2,1,0:T(8,128)(2,1)}, u32[]{:S(2)}, u32[]{:S(2)}) %all-to-all-start.1) | async-done | bytes 1048608 | tf_op jit(solution)/shard_map/all_to_all | solution.py:17
  70.6 5.7 %collective-permute-start.3 = (f32[32,128]{1,0:T(8,128)S(1)}, f32[32,128]{1,0:T(8,128)S(1)}, u32[]{:S(2)}, u32[]{:S(2)}) collective-permute-start(f32[32,128]{1,0:T(8,128)S(1)} %coarse_product.2), channel_id=1, source_target_pairs={{0,1},{1,0},{2,3},{3,2},{4,5},{5,4},{6,7},{7,6},{8,9},{9,8},{10,11... | collective-permute-start | bytes 49160 | tf_op jit(solution)/shard_map/ppermute | solution.py:171
  81.1 12.9 %all-to-all-start.2 = ((bf16[16,16,128]{2,1,0:T(8,128)(2,1)}), bf16[16,16,128]{2,1,0:T(8,128)(2,1)S(1)}, u32[]{:S(2)}, u32[]{:S(2)}) async-start(bf16[16,16,128]{2,1,0:T(8,128)(2,1)} %broadcast_in_dim.73), calls=%async_computation.2 | async-start | bytes 131072 | tf_op jit(solution)/shard_map/all_to_all | solution.py:17
  96.3 9.3 %all-to-all-done.2 = bf16[16,16,128]{2,1,0:T(8,128)(2,1)S(1)} async-done(((bf16[16,16,128]{2,1,0:T(8,128)(2,1)}), bf16[16,16,128]{2,1,0:T(8,128)(2,1)S(1)}, u32[]{:S(2)}, u32[]{:S(2)}) %all-to-all-start.2) | async-done | bytes 65568 | tf_op jit(solution)/shard_map/all_to_all | solution.py:17
  106.8 4.3 %all-to-all-start.3 = ((bf16[16,256,128]{2,1,0:T(8,128)(2,1)}), bf16[16,256,128]{2,1,0:T(8,128)(2,1)}, u32[]{:S(2)}, u32[]{:S(2)}) async-start(bf16[16,256,128]{2,1,0:T(8,128)(2,1)} %broadcast_in_dim.77), calls=%async_computation.3 | async-start | bytes 2097152 | tf_op jit(solution)/shard_map/all_to_all | solution.py:17
  111.2 4.1 %collective-permute-start.9 = (bf16[32,256]{1,0:T(8,128)(2,1)S(1)}, bf16[32,256]{1,0:T(8,128)(2,1)S(1)}, u32[]{:S(2)}, u32[]{:S(2)}) collective-permute-start(bf16[32,256]{1,0:T(8,128)(2,1)S(1)} %get-tuple-element.81), channel_id=1, source_target_pairs={{0,1},{1,0},{2,3},{3,2},{4,5},{5,4},{6,7},{7,6},{8,9},{9,8},{10,11... | collective-permute-start | bytes 49160 | tf_op jit(solution)/shard_map/ppermute | solution.py:54
  120.0 5.9 %collective-permute-done.8 = bf16[32,256]{1,0:T(8,128)(2,1)S(1)} collective-permute-done((bf16[32,256]{1,0:T(8,128)(2,1)S(1)}, bf16[32,256]{1,0:T(8,128)(2,1)S(1)}, u32[]{:S(2)}, u32[]{:S(2)}) %collective-permute-start.8) | collective-permute-done | bytes 16416 | tf_op jit(solution)/shard_map/ppermute | solution.py:53
  132.8 4.2 %collective-permute-start.10 = (bf16[64,256]{1,0:T(8,128)(2,1)S(1)}, bf16[64,256]{1,0:T(8,128)(2,1)S(1)}, u32[]{:S(2)}, u32[]{:S(2)}) collective-permute-start(bf16[64,256]{1,0:T(8,128)(2,1)S(1)} %get-tuple-element.71), channel_id=1, source_target_pairs={{0,2},{2,4},{4,6},{6,8},{8,10},{10,12},{12,14},{14,16},{16,18},{18... | collective-permute-start | bytes 98312 | tf_op jit(solution)/shard_map/ppermute | solution.py:52
  151.3 7.6 %all-to-all-start.4 = ((bf16[16,24,128]{2,1,0:T(8,128)(2,1)}), bf16[16,24,128]{2,1,0:T(8,128)(2,1)}, u32[]{:S(2)}, u32[]{:S(2)}) async-start(bf16[16,24,128]{2,1,0:T(8,128)(2,1)} %broadcast_in_dim.144), calls=%async_computation.4 | async-start | bytes 196608 | tf_op jit(solution)/shard_map/all_to_all | solution.py:17
  162.4 8.4 %all-to-all-done.4 = bf16[16,24,128]{2,1,0:T(8,128)(2,1)} async-done(((bf16[16,24,128]{2,1,0:T(8,128)(2,1)}), bf16[16,24,128]{2,1,0:T(8,128)(2,1)}, u32[]{:S(2)}, u32[]{:S(2)}) %all-to-all-start.4) | async-done | bytes 98336 | tf_op jit(solution)/shard_map/all_to_all | solution.py:17
  174.0 20.5 %all_to_all.50.blocks_ref = bf16[16,264,128]{2,1,0:T(8,128)(2,1)S(1)} all-to-all(bf16[16,264,128]{2,1,0:T(8,128)(2,1)S(1)} %broadcast_in_dim.145), channel_id=1, replica_groups=mesh['x'=4,'z'=16,'y'=4,'c'=2] {'x','y'}, dimensions={0} | all-to-all | bytes 2162688 | tf_op jit(solution)/shard_map/all_to_all | solution.py:17
  195.1 6.2 %collective-permute-start.13 = (f32[40,128]{1,0:T(8,128)S(1)}, f32[40,128]{1,0:T(8,128)S(1)}, u32[]{:S(2)}, u32[]{:S(2)}) collective-permute-start(f32[40,128]{1,0:T(8,128)S(1)} %coarse_product.3), channel_id=1, source_target_pairs={{0,1},{1,0},{2,3},{3,2},{4,5},{5,4},{6,7},{7,6},{8,9},{9,8},{10,11... | collective-permute-start | bytes 61448 | tf_op jit(solution)/shard_map/ppermute | solution.py:171
  204.5 4.6 %all-to-all-start.6 = ((bf16[16,24,128]{2,1,0:T(8,128)(2,1)}), bf16[16,24,128]{2,1,0:T(8,128)(2,1)S(1)}, u32[]{:S(2)}, u32[]{:S(2)}) async-start(bf16[16,24,128]{2,1,0:T(8,128)(2,1)} %broadcast_in_dim.146), calls=%async_computation.6 | async-start | bytes 196608 | tf_op jit(solution)/shard_map/all_to_all | solution.py:17
  212.1 8.8 %all-to-all-done.6 = bf16[16,24,128]{2,1,0:T(8,128)(2,1)S(1)} async-done(((bf16[16,24,128]{2,1,0:T(8,128)(2,1)}), bf16[16,24,128]{2,1,0:T(8,128)(2,1)S(1)}, u32[]{:S(2)}, u32[]{:S(2)}) %all-to-all-start.6) | async-done | bytes 98336 | tf_op jit(solution)/shard_map/all_to_all | solution.py:17
  227.4 4.6 %collective-permute-start.17 = (bf16[64,256]{1,0:T(8,128)(2,1)S(1)}, bf16[64,256]{1,0:T(8,128)(2,1)S(1)}, u32[]{:S(2)}, u32[]{:S(2)}) collective-permute-start(bf16[64,256]{1,0:T(8,128)(2,1)S(1)} %get-tuple-element.67), channel_id=1, source_target_pairs={{0,1},{1,0},{2,3},{3,2},{4,5},{5,4},{6,7},{7,6},{8,9},{9,8},{10,11... | collective-permute-start | bytes 98312 | tf_op jit(solution)/shard_map/ppermute | solution.py:54
  240.8 5.4 %collective-permute-start.14 = (f32[1,128]{1,0:T(1,128)S(1)}, f32[1,128]{1,0:T(1,128)S(1)}, u32[]{:S(2)}, u32[]{:S(2)}) collective-permute-start(f32[1,128]{1,0:T(1,128)S(1)} %bitcast.143), channel_id=1, source_target_pairs={{0,1},{1,0},{2,3},{3,2},{4,5},{5,4},{6,7},{7,6},{8,9},{9,8},{10,11... | collective-permute-start | bytes 1544 | tf_op jit(solution)/shard_map/ppermute | solution.py:171
  255.9 10.8 %all_to_all.51 = f32[32,1,64]{2,1,0:T(1,128)S(1)} all-to-all(f32[32,1,64]{2,1,0:T(1,128)S(1)} %broadcast_in_dim.150), channel_id=1, replica_groups=mesh['x'=4,'z'=16,'y'=4,'c'=2] {'x','y','c'}, dimensions={0} | all-to-all | bytes 16384 | tf_op jit(solution)/shard_map/all_to_all | solution.py:17
  267.3 5.8 %all-to-all-start.9 = ((f32[16,1,64]{2,1,0:T(1,128)}), f32[16,1,64]{2,1,0:T(1,128)S(1)}, u32[]{:S(2)}, u32[]{:S(2)}) async-start(f32[16,1,64]{2,1,0:T(1,128)} %broadcast_in_dim.151), calls=%async_computation.9 | async-start | bytes 16384 | tf_op jit(solution)/shard_map/all_to_all | solution.py:17
  279.8 4.6 %all-to-all-done.9 = f32[16,1,64]{2,1,0:T(1,128)S(1)} async-done(((f32[16,1,64]{2,1,0:T(1,128)}), f32[16,1,64]{2,1,0:T(1,128)S(1)}, u32[]{:S(2)}, u32[]{:S(2)}) %all-to-all-start.9) | async-done | bytes 4128 | tf_op jit(solution)/shard_map/all_to_all | solution.py:17
  (249 shorter events, 105.1 us)
Async XLA Ops:
  3.6 11.8 %collective-permute-start = (bf16[64,256]{1,0:T(8,128)(2,1)S(1)}, bf16[64,256]{1,0:T(8,128)(2,1)S(1)}, u32[]{:S(2)}, u32[]{:S(2)}) collective-permute-start(bf16[64,256]{1,0:T(8,128)(2,1)S(1)} %get-tuple-element.77), channel_id=1, source_target_pairs={{0,2},{2,4},{4,6},{6,8},{8,10},{10,12},{12,14},{14,16},{16,18},{18... | collective-permute-start | bytes 98312 | tf_op jit(solution)/shard_map/ppermute | solution.py:52
  7.7 7.8 %collective-permute-start.2 = (bf16[64,256]{1,0:T(8,128)(2,1)S(1)}, bf16[64,256]{1,0:T(8,128)(2,1)S(1)}, u32[]{:S(2)}, u32[]{:S(2)}) collective-permute-start(bf16[64,256]{1,0:T(8,128)(2,1)S(1)} %get-tuple-element.78), channel_id=1, source_target_pairs={{0,1},{1,0},{2,3},{3,2},{4,5},{5,4},{6,7},{7,6},{8,9},{9,8},{10,11... | collective-permute-start | bytes 98312 | tf_op jit(solution)/shard_map/ppermute | solution.py:54
  21.3 25.1 %all-to-all-start = ((bf16[16,16,128]{2,1,0:T(8,128)(2,1)}), bf16[16,16,128]{2,1,0:T(8,128)(2,1)S(1)}, u32[]{:S(2)}, u32[]{:S(2)}) async-start(bf16[16,16,128]{2,1,0:T(8,128)(2,1)} %broadcast_in_dim.66), calls=%async_computation | async-start | bytes 131072 | tf_op jit(solution)/shard_map/all_to_all | solution.py:17
  47.7 21.2 %all-to-all-start.1 = ((bf16[16,256,128]{2,1,0:T(8,128)(2,1)}), bf16[16,256,128]{2,1,0:T(8,128)(2,1)}, u32[]{:S(2)}, u32[]{:S(2)}) async-start(bf16[16,256,128]{2,1,0:T(8,128)(2,1)} %broadcast_in_dim.72), calls=%async_computation.1 | async-start | bytes 2097152 | tf_op jit(solution)/shard_map/all_to_all | solution.py:17
  56.8 37.2 %collective-permute-start.6 = (bf16[64,256]{1,0:T(8,128)(2,1)S(1)}, bf16[64,256]{1,0:T(8,128)(2,1)}, u32[]{:S(2)}, u32[]{:S(2)}) collective-permute-start(bf16[64,256]{1,0:T(8,128)(2,1)S(1)} %get-tuple-element.75), channel_id=1, source_target_pairs={{0,1},{1,0},{2,3},{3,2},{4,5},{5,4},{6,7},{7,6},{8,9},{9,8},{10,11... | collective-permute-start | bytes 98312 | tf_op jit(solution)/shard_map/ppermute | solution.py:54
  70.6 9.8 %collective-permute-start.3 = (f32[32,128]{1,0:T(8,128)S(1)}, f32[32,128]{1,0:T(8,128)S(1)}, u32[]{:S(2)}, u32[]{:S(2)}) collective-permute-start(f32[32,128]{1,0:T(8,128)S(1)} %coarse_product.2), channel_id=1, source_target_pairs={{0,1},{1,0},{2,3},{3,2},{4,5},{5,4},{6,7},{7,6},{8,9},{9,8},{10,11... | collective-permute-start | bytes 49160 | tf_op jit(solution)/shard_map/ppermute | solution.py:171
  76.3 18.5 %collective-permute-start.4 = (bf16[64,256]{1,0:T(8,128)(2,1)S(1)}, bf16[64,256]{1,0:T(8,128)(2,1)}, u32[]{:S(2)}, u32[]{:S(2)}) collective-permute-start(bf16[64,256]{1,0:T(8,128)(2,1)S(1)} %get-tuple-element.74), channel_id=1, source_target_pairs={{0,2},{2,4},{4,6},{6,8},{8,10},{10,12},{12,14},{14,16},{16,18},{18... | collective-permute-start | bytes 98312 | tf_op jit(solution)/shard_map/ppermute | solution.py:52
  79.1 15.7 %collective-permute-start.5 = (bf16[64,256]{1,0:T(8,128)(2,1)S(1)}, bf16[64,256]{1,0:T(8,128)(2,1)}, u32[]{:S(2)}, u32[]{:S(2)}) collective-permute-start(bf16[64,256]{1,0:T(8,128)(2,1)S(1)} %get-tuple-element.76), channel_id=1, source_target_pairs={{2,0},{4,2},{6,4},{8,6},{10,8},{12,10},{14,12},{16,14},{18,16},{20... | collective-permute-start | bytes 98312 | tf_op jit(solution)/shard_map/ppermute | solution.py:53
  81.1 24.5 %all-to-all-start.2 = ((bf16[16,16,128]{2,1,0:T(8,128)(2,1)}), bf16[16,16,128]{2,1,0:T(8,128)(2,1)S(1)}, u32[]{:S(2)}, u32[]{:S(2)}) async-start(bf16[16,16,128]{2,1,0:T(8,128)(2,1)} %broadcast_in_dim.73), calls=%async_computation.2 | async-start | bytes 131072 | tf_op jit(solution)/shard_map/all_to_all | solution.py:17
  106.8 19.7 %all-to-all-start.3 = ((bf16[16,256,128]{2,1,0:T(8,128)(2,1)}), bf16[16,256,128]{2,1,0:T(8,128)(2,1)}, u32[]{:S(2)}, u32[]{:S(2)}) async-start(bf16[16,256,128]{2,1,0:T(8,128)(2,1)} %broadcast_in_dim.77), calls=%async_computation.3 | async-start | bytes 2097152 | tf_op jit(solution)/shard_map/all_to_all | solution.py:17
  111.2 8.8 %collective-permute-start.9 = (bf16[32,256]{1,0:T(8,128)(2,1)S(1)}, bf16[32,256]{1,0:T(8,128)(2,1)S(1)}, u32[]{:S(2)}, u32[]{:S(2)}) collective-permute-start(bf16[32,256]{1,0:T(8,128)(2,1)S(1)} %get-tuple-element.81), channel_id=1, source_target_pairs={{0,1},{1,0},{2,3},{3,2},{4,5},{5,4},{6,7},{7,6},{8,9},{9,8},{10,11... | collective-permute-start | bytes 49160 | tf_op jit(solution)/shard_map/ppermute | solution.py:54
  118.7 7.2 %collective-permute-start.8 = (bf16[32,256]{1,0:T(8,128)(2,1)S(1)}, bf16[32,256]{1,0:T(8,128)(2,1)S(1)}, u32[]{:S(2)}, u32[]{:S(2)}) collective-permute-start(bf16[32,256]{1,0:T(8,128)(2,1)S(1)} %get-tuple-element.82), channel_id=1, source_target_pairs={{2,0},{4,2},{6,4},{8,6},{10,8},{12,10},{14,12},{16,14},{18,16},{20... | collective-permute-start | bytes 49160 | tf_op jit(solution)/shard_map/ppermute | solution.py:53
  132.8 9.3 %collective-permute-start.10 = (bf16[64,256]{1,0:T(8,128)(2,1)S(1)}, bf16[64,256]{1,0:T(8,128)(2,1)S(1)}, u32[]{:S(2)}, u32[]{:S(2)}) collective-permute-start(bf16[64,256]{1,0:T(8,128)(2,1)S(1)} %get-tuple-element.71), channel_id=1, source_target_pairs={{0,2},{2,4},{4,6},{6,8},{8,10},{10,12},{12,14},{14,16},{16,18},{18... | collective-permute-start | bytes 98312 | tf_op jit(solution)/shard_map/ppermute | solution.py:52
  151.3 19.5 %all-to-all-start.4 = ((bf16[16,24,128]{2,1,0:T(8,128)(2,1)}), bf16[16,24,128]{2,1,0:T(8,128)(2,1)}, u32[]{:S(2)}, u32[]{:S(2)}) async-start(bf16[16,24,128]{2,1,0:T(8,128)(2,1)} %broadcast_in_dim.144), calls=%async_computation.4 | async-start | bytes 196608 | tf_op jit(solution)/shard_map/all_to_all | solution.py:17
  195.1 7.0 %collective-permute-start.13 = (f32[40,128]{1,0:T(8,128)S(1)}, f32[40,128]{1,0:T(8,128)S(1)}, u32[]{:S(2)}, u32[]{:S(2)}) collective-permute-start(f32[40,128]{1,0:T(8,128)S(1)} %coarse_product.3), channel_id=1, source_target_pairs={{0,1},{1,0},{2,3},{3,2},{4,5},{5,4},{6,7},{7,6},{8,9},{9,8},{10,11... | collective-permute-start | bytes 61448 | tf_op jit(solution)/shard_map/ppermute | solution.py:171
  204.5 16.5 %all-to-all-start.6 = ((bf16[16,24,128]{2,1,0:T(8,128)(2,1)}), bf16[16,24,128]{2,1,0:T(8,128)(2,1)S(1)}, u32[]{:S(2)}, u32[]{:S(2)}) async-start(bf16[16,24,128]{2,1,0:T(8,128)(2,1)} %broadcast_in_dim.146), calls=%async_computation.6 | async-start | bytes 196608 | tf_op jit(solution)/shard_map/all_to_all | solution.py:17
  222.2 18.6 %all-to-all-start.7 = ((bf16[16,264,128]{2,1,0:T(8,128)(2,1)}), bf16[16,264,128]{2,1,0:T(8,128)(2,1)S(1)}, u32[]{:S(2)}, u32[]{:S(2)}) async-start(bf16[16,264,128]{2,1,0:T(8,128)(2,1)} %broadcast_in_dim.147), calls=%async_computation.7 | async-start | bytes 2162688 | tf_op jit(solution)/shard_map/all_to_all | solution.py:17
  227.4 9.9 %collective-permute-start.17 = (bf16[64,256]{1,0:T(8,128)(2,1)S(1)}, bf16[64,256]{1,0:T(8,128)(2,1)S(1)}, u32[]{:S(2)}, u32[]{:S(2)}) collective-permute-start(bf16[64,256]{1,0:T(8,128)(2,1)S(1)} %get-tuple-element.67), channel_id=1, source_target_pairs={{0,1},{1,0},{2,3},{3,2},{4,5},{5,4},{6,7},{7,6},{8,9},{9,8},{10,11... | collective-permute-start | bytes 98312 | tf_op jit(solution)/shard_map/ppermute | solution.py:54
  232.0 14.3 %collective-permute-start.15 = (bf16[64,256]{1,0:T(8,128)(2,1)}, bf16[64,256]{1,0:T(8,128)(2,1)}, u32[]{:S(2)}, u32[]{:S(2)}) collective-permute-start(bf16[64,256]{1,0:T(8,128)(2,1)} %get-tuple-element.66), channel_id=1, source_target_pairs={{0,2},{2,4},{4,6},{6,8},{8,10},{10,12},{12,14},{14,16},{16,18},{18... | collective-permute-start | bytes 98312 | tf_op jit(solution)/shard_map/ppermute | solution.py:52
  236.0 10.3 %collective-permute-start.16 = (bf16[64,256]{1,0:T(8,128)(2,1)}, bf16[64,256]{1,0:T(8,128)(2,1)}, u32[]{:S(2)}, u32[]{:S(2)}) collective-permute-start(bf16[64,256]{1,0:T(8,128)(2,1)} %get-tuple-element.68), channel_id=1, source_target_pairs={{2,0},{4,2},{6,4},{8,6},{10,8},{12,10},{14,12},{16,14},{18,16},{20... | collective-permute-start | bytes 98312 | tf_op jit(solution)/shard_map/ppermute | solution.py:53
  240.8 6.9 %collective-permute-start.14 = (f32[1,128]{1,0:T(1,128)S(1)}, f32[1,128]{1,0:T(1,128)S(1)}, u32[]{:S(2)}, u32[]{:S(2)}) collective-permute-start(f32[1,128]{1,0:T(1,128)S(1)} %bitcast.143), channel_id=1, source_target_pairs={{0,1},{1,0},{2,3},{3,2},{4,5},{5,4},{6,7},{7,6},{8,9},{9,8},{10,11... | collective-permute-start | bytes 1544 | tf_op jit(solution)/shard_map/ppermute | solution.py:171
  267.3 17.1 %all-to-all-start.9 = ((f32[16,1,64]{2,1,0:T(1,128)}), f32[16,1,64]{2,1,0:T(1,128)S(1)}, u32[]{:S(2)}, u32[]{:S(2)}) async-start(f32[16,1,64]{2,1,0:T(1,128)} %broadcast_in_dim.151), calls=%async_computation.9 | async-start | bytes 16384 | tf_op jit(solution)/shard_map/all_to_all | solution.py:17
  273.2 11.3 %collective-permute-start.18 = (bf16[64,256]{1,0:T(8,128)(2,1)S(1)}, bf16[64,256]{1,0:T(8,128)(2,1)S(1)}, u32[]{:S(2)}, u32[]{:S(2)}) collective-permute-start(bf16[64,256]{1,0:T(8,128)(2,1)S(1)} %get-tuple-element.63), channel_id=1, source_target_pairs={{0,2},{2,4},{4,6},{6,8},{8,10},{10,12},{12,14},{14,16},{16,18},{18... | collective-permute-start | bytes 98312 | tf_op jit(solution)/shard_map/ppermute | solution.py:52
  275.4 9.1 %collective-permute-start.20 = (bf16[64,256]{1,0:T(8,128)(2,1)S(1)}, bf16[64,256]{1,0:T(8,128)(2,1)S(1)}, u32[]{:S(2)}, u32[]{:S(2)}) collective-permute-start(bf16[64,256]{1,0:T(8,128)(2,1)S(1)} %get-tuple-element.64), channel_id=1, source_target_pairs={{0,1},{1,0},{2,3},{3,2},{4,5},{5,4},{6,7},{7,6},{8,9},{9,8},{10,11... | collective-permute-start | bytes 98312 | tf_op jit(solution)/shard_map/ppermute | solution.py:54
  (53 other events, 838.2 us)

commit v6 on v4

--- a/solution.py
+++ b/solution.py
@@ -5,6 +5,7 @@
 from jax.experimental.pallas import tpu as pltpu
 from jax.sharding import Mesh, PartitionSpec as P
 
+
 XYZ = (4, 16, 4)
 WIDE = ("x", "z", "y")
 INTERPRET = False
@@ -24,12 +25,15 @@
     return spread(block, ("x", "y"))
 
 
-def gather_with_sum(block, partial):
-    rows = block.shape[0]
-    stage = spread(jnp.concatenate([block, in_pieces(partial)], axis=0), "z")
+def with_sum(block, partial):
+    return jnp.concatenate([block, in_pieces(partial)], axis=0)
+
+
+def summed_along_z(payload):
+    stage = spread(payload, "z")
+    rows = payload.shape[0] - 8
     sums = jnp.sum(stage[:, rows:, :].astype(jnp.float32), axis=(0, 1))[None, :]
-    rest = stage[:, :rows, :].reshape(-1, block.shape[1])
-    return across(jnp.concatenate([rest, in_pieces(sums)], axis=0))
+    return with_sum(stage[:, :rows, :].reshape(-1, payload.shape[1]), sums)
 
 
 def total(partial):
@@ -38,7 +42,7 @@
 
 
 def neighbours(values):
-    load_count, width = values.shape
+    _, width = values.shape
     face = width // 4
     rows = lax.axis_size(WIDE)
     column = lax.axis_index("c")
@@ -252,7 +256,7 @@
     flex_block = flexibility[0, 0]
     precond_block = dirichlet[0, 0]
     mode_block = modes[0, 0]
-    nx, nz, ny = XYZ
+    _, nz, ny = XYZ
     rows = lax.axis_size(WIDE)
     row = lax.axis_index(WIDE)
     column = lax.axis_index("c")
@@ -280,7 +284,11 @@
     def load_dot(left, right):
         return jnp.sum(left.astype(jnp.float32) * right.astype(jnp.float32), axis=1)
 
-    residual = jump(apply_flex(local_loads))
+    load_count = local_loads.shape[0]
+    displaced = apply_flex(local_loads)
+    near = neighbours(jnp.concatenate([displaced, mode_block], axis=0))
+    near_modes = near[load_count:]
+    residual = displaced.astype(jnp.float32) - near[:load_count].astype(jnp.float32)
     rounded = residual.astype(jnp.bfloat16)
     payload = pack(weigh(rounded).astype(jnp.bfloat16))
     payload, mode_counts = lax.optimization_barrier((payload, mode_counts))
@@ -313,10 +321,7 @@
     stage, padded, info, rounded = lax.optimization_barrier((stage, padded, info, rounded))
     smoothed = smooth(rounded)
     near_smoothed = neighbours(smoothed)
-    blocks, near_smoothed, late_modes = lax.optimization_barrier(
-        (across(stage), near_smoothed, mode_block)
-    )
-    near_modes = neighbours(late_modes)
+    blocks, near_smoothed = lax.optimization_barrier((across(stage), near_smoothed))
     first_sums = swapped_sum(coarse_product(padded, blocks))
     half_slots = first_sums.shape[0] // 2
     values = across(along_z(first_sums[:half_slots].astype(jnp.bfloat16)))
@@ -325,29 +330,51 @@
     )
 
     pushed = apply_flex(moved)
-    partials = jnp.concatenate([load_dot(residual, direction), load_dot(moved, pushed)])[None, :]
-    image = jump(pushed)
+    curvature = load_dot(moved, pushed)
+    partials = jnp.concatenate([load_dot(residual, direction), curvature])[None, :]
+    pieces = in_pieces(partials)
+    near_pushed = neighbours(pushed)
+    near_pushed, pieces = lax.optimization_barrier((near_pushed, pieces))
+
+    def difference(own, near):
+        return own.astype(jnp.float32) - near.astype(jnp.float32)
+
+    image = difference(pushed, near_pushed)
     image_high = lax.reduce_precision(image, 8, 7)
     image_low = (image - image_high).astype(jnp.bfloat16)
     image_weights = weigh(image_high.astype(jnp.bfloat16)) + weigh(image_low)
-    blocks = gather_with_sum(pack(image_weights.astype(jnp.bfloat16)), partials)
+    payload = jnp.concatenate([pack(image_weights.astype(jnp.bfloat16)), pieces], axis=0)
+    stage, late_pushed, late_near = lax.optimization_barrier(
+        (summed_along_z(payload), pushed, near_pushed)
+    )
+    late_image = difference(late_pushed, late_near)
+    image_smoothed = smooth(late_image.astype(jnp.bfloat16))
+    residual_jump, image_jump = residual * factor, late_image * factor
+    energies = (
+        load_dot(residual_jump, smoothed),
+        load_dot(residual_jump, image_smoothed) + load_dot(image_jump, smoothed),
+        load_dot(image_jump, image_smoothed),
+    )
+    blocks, energies = lax.optimization_barrier((across(stage), energies))
     second_sums = swapped_sum(coarse_product(padded, blocks))
     totals = jnp.sum(second_sums[2 * half_slots :], axis=0)
     energy = totals[:64]
     size = energy / totals[64:]
+    local_energy = energies[0] - size * (energies[1] - size * energies[2])
+
+    packed = first_sums - jnp.tile(size, 2)[None, :] * second_sums[: 2 * half_slots]
+    coarse_values = lax.reduce_precision(packed[:half_slots], 8, 7)
+    coarse_energy = jnp.sum(coarse_values * packed[half_slots:], axis=0)
+    partial = local_energy + 0.5 * (coarse_energy[:64] + coarse_energy[64:])
+    partial = jnp.concatenate([partial, jnp.zeros_like(partial)])[None, :]
+    payload = with_sum(coarse_values.astype(jnp.bfloat16), partial)
+    payload, size = lax.optimization_barrier((payload, size))
     multipliers = size[:, None] * direction
     residual = residual - size[:, None] * image
-
-    packed = first_sums - jnp.tile(size, 2)[None, :] * second_sums[: 2 * half_slots]
-    rounded = residual.astype(jnp.bfloat16)
-    smoothed = smooth(rounded)
-    coarse_values = lax.reduce_precision(packed[:half_slots], 8, 7)
-    coarse_energy = jnp.sum(coarse_values * packed[half_slots:], axis=0)
-    local_energy = load_dot(residual * factor, smoothed)
-    partial = local_energy + 0.5 * (coarse_energy[:64] + coarse_energy[64:])
-    partial = jnp.concatenate([partial, jnp.zeros_like(partial)])[None, :]
+    smoothed = smooth(residual.astype(jnp.bfloat16))
+    stage, smoothed = lax.optimization_barrier((summed_along_z(payload), smoothed))
     near_smoothed = neighbours(smoothed)
-    values = gather_with_sum(coarse_values.astype(jnp.bfloat16), partial)
+    values = across(stage)
     sums = jnp.sum(values[:, nz * half_slots :, :].astype(jnp.float32), axis=(0, 1))[None, :]
     fresh = swapped_sum(sums)[0, :64]
     direction, near_direction, moved = next_direction(

time: 280 us -> 281 us (level)
  blocking collectives: 87.3 us -> 49.4 us
  waiting for transfers between devices: 29 us -> 52.7 us
  starting transfers between devices: 105 us -> 110 us
  local copies, waits for them, and re-layouts: 19.2 us -> 23.9 us
  matrix products: 8.06 us -> 11.3 us
    all_to_all x5 -> x3, blocking collectives: 87.3 us -> 49.4 us  [spread(): return lax.all_to_all(copies, axes, 0, 0, tiled=False)]
    all_to_all x5 -> x7, waiting for transfers between devices: 10.6 us -> 43.6 us  [spread(): return lax.all_to_all(copies, axes, 0, 0, tiled=False)]
    all_to_all x5 -> x7, starting transfers between devices: 36.7 us -> 48.4 us  [spread(): return lax.all_to_all(copies, axes, 0, 0, tiled=False)]
    ppermute x6 -> x5, waiting for transfers between devices: 14.5 us -> 7.05 us  [neighbours(): from_below = lax.ppermute(north, WIDE, up)]
    dot_general x2 -> x3, matrix products: 5.02 us -> 8.25 us  [smooth(): jnp.dot(inner, precond_block, preferred_element_type=jnp.float32)]
    ppermute x6 -> x5, starting transfers between devices: 27.3 us -> 24.5 us  [neighbours(): lax.ppermute(jnp.where(column == 0, east, west), 'c', [(0, 1), (1, 0)])]
    ppermute x6 -> x5, starting transfers between devices: 18.8 us -> 16.1 us  [neighbours(): from_above = lax.ppermute(south, WIDE, down)]
    ppermute x6 -> x5, starting transfers between devices: 7.74 us -> 6.45 us  [neighbours(): from_below = lax.ppermute(north, WIDE, up)]
  transfers between devices with their start and end apart: 26 -> 25, of which waited for: 10 -> 11; matrix products, arithmetic and copies ran while one was open for 4% -> 6% of each run, Pallas kernels for 2% -> 2%
where the time goes in v6:
time: 281 us; the launch traced here: 277 us
  starting transfers between devices  110 us (39%)
  waiting for transfers between devices  52.7 us (19%)
  blocking collectives  49.4 us (18%)
  local copies, waits for them, and re-layouts  23.9 us (9%)
  Pallas kernels  14.6 us (5%)
  other arithmetic  13.7 us (5%)
  matrix products  11.3 us (4%)
    all_to_all x3, blocking collectives, spread(): return lax.all_to_all(copies, axes, 0, 0, tiled=False)  49.4 us
    all_to_all x7, starting transfers between devices, spread(): return lax.all_to_all(copies, axes, 0, 0, tiled=False)  48.4 us
    all_to_all x7, waiting for transfers between devices, spread(): return lax.all_to_all(copies, axes, 0, 0, tiled=False)  43.6 us
    ppermute x5, starting transfers between devices, neighbours(): lax.ppermute(jnp.where(column == 0, east, west), 'c', [(0, 1), (1, 0)])  24.5 us
    ppermute x5, starting transfers between devices, neighbours(): from_above = lax.ppermute(south, WIDE, down)  16.1 us
    ppermute x3, starting transfers between devices, swapped_sum(): return partial + lax.ppermute(partial, 'c', [(0, 1), (1, 0)])  14.9 us
    unnamed x76, local copies, waits for them, and re-layouts  11.7 us
    dot_general x3, matrix products, smooth(): jnp.dot(inner, precond_block, preferred_element_type=jnp.float32)  8.25 us
  transfers between devices with their start and end apart: 25, of which 11 were waited for; matrix products, arithmetic and copies ran while one was open for 6% of the time, Pallas kernels for 2%

profile of v6, /device:TPU:1, one launch (start us, length us, event | category | flops | bytes accessed | tf_op | source)
XLA Modules:
  0.0 277.4 jit_solution(1632620131140486179)
XLA Ops:
  3.7 4.0 %collective-permute-start = (bf16[96,256]{1,0:T(8,128)(2,1)S(1)}, bf16[96,256]{1,0:T(8,128)(2,1)S(1)}, u32[]{:S(2)}, u32[]{:S(2)}) collective-permute-start(bf16[96,256]{1,0:T(8,128)(2,1)S(1)} %get-tuple-element.69), channel_id=1, source_target_pairs={{0,2},{2,4},{4,6},{6,8},{8,10},{10,12},{12,14},{14,16},{16,18},{18... | collective-permute-start | bytes 147464 | tf_op jit(solution)/shard_map/ppermute | solution.py:52
  9.0 6.0 %collective-permute-start.2 = (bf16[96,256]{1,0:T(8,128)(2,1)S(1)}, bf16[96,256]{1,0:T(8,128)(2,1)S(1)}, u32[]{:S(2)}, u32[]{:S(2)}) collective-permute-start(bf16[96,256]{1,0:T(8,128)(2,1)S(1)} %get-tuple-element.71), channel_id=1, source_target_pairs={{0,1},{1,0},{2,3},{3,2},{4,5},{5,4},{6,7},{7,6},{8,9},{9,8},{10,11... | collective-permute-start | bytes 147464 | tf_op jit(solution)/shard_map/ppermute | solution.py:54
  18.8 16.1 %all-to-all-start = ((bf16[16,16,128]{2,1,0:T(8,128)(2,1)}), bf16[16,16,128]{2,1,0:T(8,128)(2,1)S(1)}, u32[]{:S(2)}, u32[]{:S(2)}) async-start(bf16[16,16,128]{2,1,0:T(8,128)(2,1)} %broadcast_in_dim.69), calls=%async_computation | async-start | bytes 131072 | tf_op jit(solution)/shard_map/all_to_all | solution.py:17
  37.0 6.4 %pad_inverse.1.padded_ref = bf16[128,4096]{1,0:T(8,128)(2,1)S(1)} custom-call(s32[33]{0:T(128)S(1)} %pad_add_fusion.1.first_ref, s32[2,32,1,128]{3,2,1,0:T(1,128)S(1)} %compare_select_fusion.source_ref, bf16[32,4096]{1,0:T(8,128)(2,1)S(1)} %copy-done.10), custom_call_target="tpu_custom_call" | custom-call | tf_op jit(solution)/shard_map/pad_inverse/pallas_call | solution.py:106
  47.8 4.3 %all-to-all-start.1 = ((bf16[16,256,128]{2,1,0:T(8,128)(2,1)}), bf16[16,256,128]{2,1,0:T(8,128)(2,1)}, u32[]{:S(2)}, u32[]{:S(2)}) async-start(bf16[16,256,128]{2,1,0:T(8,128)(2,1)} %broadcast_in_dim.75), calls=%async_computation.1 | async-start | bytes 2097152 | tf_op jit(solution)/shard_map/all_to_all | solution.py:17
  54.4 5.3 %collective-permute-start.5 = (bf16[64,256]{1,0:T(8,128)(2,1)S(1)}, bf16[64,256]{1,0:T(8,128)(2,1)S(1)}, u32[]{:S(2)}, u32[]{:S(2)}) collective-permute-start(bf16[64,256]{1,0:T(8,128)(2,1)S(1)} %get-tuple-element.82), channel_id=1, source_target_pairs={{0,1},{1,0},{2,3},{3,2},{4,5},{5,4},{6,7},{7,6},{8,9},{9,8},{10,11... | collective-permute-start | bytes 98312 | tf_op jit(solution)/shard_map/ppermute | solution.py:54
  64.6 3.8 %collective-permute-done.4 = bf16[64,256]{1,0:T(8,128)(2,1)S(1)} collective-permute-done((bf16[64,256]{1,0:T(8,128)(2,1)S(1)}, bf16[64,256]{1,0:T(8,128)(2,1)S(1)}, u32[]{:S(2)}, u32[]{:S(2)}) %collective-permute-start.4) | collective-permute-done | bytes 32800 | tf_op jit(solution)/shard_map/ppermute | solution.py:53
  75.0 19.8 %all_to_all.50 = bf16[16,16,128]{2,1,0:T(8,128)(2,1)S(1)} all-to-all(bf16[16,16,128]{2,1,0:T(8,128)(2,1)S(1)} %broadcast_in_dim.142), channel_id=1, replica_groups=mesh['x'=4,'z'=16,'y'=4,'c'=2] {'z'}, dimensions={0} | all-to-all | bytes 131072 | tf_op jit(solution)/shard_map/all_to_all | solution.py:17
  96.0 7.5 %all-to-all-start.3 = ((bf16[16,256,128]{2,1,0:T(8,128)(2,1)}), bf16[16,256,128]{2,1,0:T(8,128)(2,1)}, u32[]{:S(2)}, u32[]{:S(2)}) async-start(bf16[16,256,128]{2,1,0:T(8,128)(2,1)} %broadcast_in_dim.144), calls=%async_computation.3 | async-start | bytes 2097152 | tf_op jit(solution)/shard_map/all_to_all | solution.py:17
  104.9 13.2 %all-to-all-done.3.blocks_ref = bf16[16,256,128]{2,1,0:T(8,128)(2,1)} async-done(((bf16[16,256,128]{2,1,0:T(8,128)(2,1)}), bf16[16,256,128]{2,1,0:T(8,128)(2,1)}, u32[]{:S(2)}, u32[]{:S(2)}) %all-to-all-start.3) | async-done | bytes 1048608 | tf_op jit(solution)/shard_map/all_to_all | solution.py:17
  128.0 5.4 %collective-permute-start.9 = (bf16[64,256]{1,0:T(8,128)(2,1)S(1)}, bf16[64,256]{1,0:T(8,128)(2,1)S(1)}, u32[]{:S(2)}, u32[]{:S(2)}) collective-permute-start(bf16[64,256]{1,0:T(8,128)(2,1)S(1)} %get-tuple-element.79), channel_id=1, source_target_pairs={{0,1},{1,0},{2,3},{3,2},{4,5},{5,4},{6,7},{7,6},{8,9},{9,8},{10,11... | collective-permute-start | bytes 98312 | tf_op jit(solution)/shard_map/ppermute | solution.py:54
  138.9 18.8 %all_to_all.51 = bf16[16,24,128]{2,1,0:T(8,128)(2,1)S(1)} all-to-all(bf16[16,24,128]{2,1,0:T(8,128)(2,1)S(1)} %broadcast_in_dim.146), channel_id=1, replica_groups=mesh['x'=4,'z'=16,'y'=4,'c'=2] {'z'}, dimensions={0} | all-to-all | bytes 196608 | tf_op jit(solution)/shard_map/all_to_all | solution.py:17
  163.7 6.2 %all-to-all-start.5 = ((bf16[16,264,128]{2,1,0:T(8,128)(2,1)}), bf16[16,264,128]{2,1,0:T(8,128)(2,1)}, u32[]{:S(2)}, u32[]{:S(2)}) async-start(bf16[16,264,128]{2,1,0:T(8,128)(2,1)} %broadcast_in_dim.147), calls=%async_computation.5 | async-start | bytes 2162688 | tf_op jit(solution)/shard_map/all_to_all | solution.py:17
  173.5 10.9 %all-to-all-done.5.blocks_ref = bf16[16,264,128]{2,1,0:T(8,128)(2,1)} async-done(((bf16[16,264,128]{2,1,0:T(8,128)(2,1)}), bf16[16,264,128]{2,1,0:T(8,128)(2,1)}, u32[]{:S(2)}, u32[]{:S(2)}) %all-to-all-start.5) | async-done | bytes 1081376 | tf_op jit(solution)/shard_map/all_to_all | solution.py:17
  186.2 6.2 %collective-permute-start.10 = (f32[40,128]{1,0:T(8,128)S(1)}, f32[40,128]{1,0:T(8,128)S(1)}, u32[]{:S(2)}, u32[]{:S(2)}) collective-permute-start(f32[40,128]{1,0:T(8,128)S(1)} %coarse_product.3), channel_id=1, source_target_pairs={{0,1},{1,0},{2,3},{3,2},{4,5},{5,4},{6,7},{7,6},{8,9},{9,8},{10,11... | collective-permute-start | bytes 61448 | tf_op jit(solution)/shard_map/ppermute | solution.py:171
  195.7 4.6 %all-to-all-start.6 = ((bf16[16,24,128]{2,1,0:T(8,128)(2,1)}), bf16[16,24,128]{2,1,0:T(8,128)(2,1)S(1)}, u32[]{:S(2)}, u32[]{:S(2)}) async-start(bf16[16,24,128]{2,1,0:T(8,128)(2,1)} %broadcast_in_dim.148), calls=%async_computation.6 | async-start | bytes 196608 | tf_op jit(solution)/shard_map/all_to_all | solution.py:17
  203.3 8.9 %all-to-all-done.6 = bf16[16,24,128]{2,1,0:T(8,128)(2,1)S(1)} async-done(((bf16[16,24,128]{2,1,0:T(8,128)(2,1)}), bf16[16,24,128]{2,1,0:T(8,128)(2,1)S(1)}, u32[]{:S(2)}, u32[]{:S(2)}) %all-to-all-start.6) | async-done | bytes 98336 | tf_op jit(solution)/shard_map/all_to_all | solution.py:17
  213.5 3.7 %all-to-all-start.7 = ((bf16[16,264,128]{2,1,0:T(8,128)(2,1)}), bf16[16,264,128]{2,1,0:T(8,128)(2,1)S(1)}, u32[]{:S(2)}, u32[]{:S(2)}) async-start(bf16[16,264,128]{2,1,0:T(8,128)(2,1)} %broadcast_in_dim.149), calls=%async_computation.7 | async-start | bytes 2162688 | tf_op jit(solution)/shard_map/all_to_all | solution.py:17
  218.6 4.6 %collective-permute-start.14 = (bf16[64,256]{1,0:T(8,128)(2,1)S(1)}, bf16[64,256]{1,0:T(8,128)(2,1)S(1)}, u32[]{:S(2)}, u32[]{:S(2)}) collective-permute-start(bf16[64,256]{1,0:T(8,128)(2,1)S(1)} %get-tuple-element.76), channel_id=1, source_target_pairs={{0,1},{1,0},{2,3},{3,2},{4,5},{5,4},{6,7},{7,6},{8,9},{9,8},{10,11... | collective-permute-start | bytes 98312 | tf_op jit(solution)/shard_map/ppermute | solution.py:54
  223.2 4.0 %collective-permute-start.12 = (bf16[64,256]{1,0:T(8,128)(2,1)}, bf16[64,256]{1,0:T(8,128)(2,1)}, u32[]{:S(2)}, u32[]{:S(2)}) collective-permute-start(bf16[64,256]{1,0:T(8,128)(2,1)} %get-tuple-element.75), channel_id=1, source_target_pairs={{0,2},{2,4},{4,6},{6,8},{8,10},{10,12},{12,14},{14,16},{16,18},{18... | collective-permute-start | bytes 98312 | tf_op jit(solution)/shard_map/ppermute | solution.py:52
  232.1 5.4 %collective-permute-start.11 = (f32[1,128]{1,0:T(1,128)S(1)}, f32[1,128]{1,0:T(1,128)S(1)}, u32[]{:S(2)}, u32[]{:S(2)}) collective-permute-start(f32[1,128]{1,0:T(1,128)S(1)} %bitcast.145), channel_id=1, source_target_pairs={{0,1},{1,0},{2,3},{3,2},{4,5},{5,4},{6,7},{7,6},{8,9},{9,8},{10,11... | collective-permute-start | bytes 1544 | tf_op jit(solution)/shard_map/ppermute | solution.py:171
  246.8 10.8 %all_to_all.52 = f32[32,1,64]{2,1,0:T(1,128)S(1)} all-to-all(f32[32,1,64]{2,1,0:T(1,128)S(1)} %broadcast_in_dim.152), channel_id=1, replica_groups=mesh['x'=4,'z'=16,'y'=4,'c'=2] {'x','y','c'}, dimensions={0} | all-to-all | bytes 16384 | tf_op jit(solution)/shard_map/all_to_all | solution.py:17
  258.3 5.8 %all-to-all-start.9 = ((f32[16,1,64]{2,1,0:T(1,128)}), f32[16,1,64]{2,1,0:T(1,128)S(1)}, u32[]{:S(2)}, u32[]{:S(2)}) async-start(f32[16,1,64]{2,1,0:T(1,128)} %broadcast_in_dim.153), calls=%async_computation.9 | async-start | bytes 16384 | tf_op jit(solution)/shard_map/all_to_all | solution.py:17
  270.7 4.6 %all-to-all-done.9 = f32[16,1,64]{2,1,0:T(1,128)S(1)} async-done(((f32[16,1,64]{2,1,0:T(1,128)}), f32[16,1,64]{2,1,0:T(1,128)S(1)}, u32[]{:S(2)}, u32[]{:S(2)}) %all-to-all-start.9) | async-done | bytes 4128 | tf_op jit(solution)/shard_map/all_to_all | solution.py:17
  (217 shorter events, 89.5 us)
Async XLA Ops:
  3.7 12.2 %collective-permute-start = (bf16[96,256]{1,0:T(8,128)(2,1)S(1)}, bf16[96,256]{1,0:T(8,128)(2,1)S(1)}, u32[]{:S(2)}, u32[]{:S(2)}) collective-permute-start(bf16[96,256]{1,0:T(8,128)(2,1)S(1)} %get-tuple-element.69), channel_id=1, source_target_pairs={{0,2},{2,4},{4,6},{6,8},{8,10},{10,12},{12,14},{14,16},{16,18},{18... | collective-permute-start | bytes 147464 | tf_op jit(solution)/shard_map/ppermute | solution.py:52
  7.7 8.2 %collective-permute-start.1 = (bf16[96,256]{1,0:T(8,128)(2,1)S(1)}, bf16[96,256]{1,0:T(8,128)(2,1)S(1)}, u32[]{:S(2)}, u32[]{:S(2)}) collective-permute-start(bf16[96,256]{1,0:T(8,128)(2,1)S(1)} %get-tuple-element.70), channel_id=1, source_target_pairs={{2,0},{4,2},{6,4},{8,6},{10,8},{12,10},{14,12},{16,14},{18,16},{20... | collective-permute-start | bytes 147464 | tf_op jit(solution)/shard_map/ppermute | solution.py:53
  9.0 6.9 %collective-permute-start.2 = (bf16[96,256]{1,0:T(8,128)(2,1)S(1)}, bf16[96,256]{1,0:T(8,128)(2,1)S(1)}, u32[]{:S(2)}, u32[]{:S(2)}) collective-permute-start(bf16[96,256]{1,0:T(8,128)(2,1)S(1)} %get-tuple-element.71), channel_id=1, source_target_pairs={{0,1},{1,0},{2,3},{3,2},{4,5},{5,4},{6,7},{7,6},{8,9},{9,8},{10,11... | collective-permute-start | bytes 147464 | tf_op jit(solution)/shard_map/ppermute | solution.py:54
  18.8 27.8 %all-to-all-start = ((bf16[16,16,128]{2,1,0:T(8,128)(2,1)}), bf16[16,16,128]{2,1,0:T(8,128)(2,1)S(1)}, u32[]{:S(2)}, u32[]{:S(2)}) async-start(bf16[16,16,128]{2,1,0:T(8,128)(2,1)} %broadcast_in_dim.69), calls=%async_computation | async-start | bytes 131072 | tf_op jit(solution)/shard_map/all_to_all | solution.py:17
  47.8 21.2 %all-to-all-start.1 = ((bf16[16,256,128]{2,1,0:T(8,128)(2,1)}), bf16[16,256,128]{2,1,0:T(8,128)(2,1)}, u32[]{:S(2)}, u32[]{:S(2)}) async-start(bf16[16,256,128]{2,1,0:T(8,128)(2,1)} %broadcast_in_dim.75), calls=%async_computation.1 | async-start | bytes 2097152 | tf_op jit(solution)/shard_map/all_to_all | solution.py:17
  54.4 10.1 %collective-permute-start.5 = (bf16[64,256]{1,0:T(8,128)(2,1)S(1)}, bf16[64,256]{1,0:T(8,128)(2,1)S(1)}, u32[]{:S(2)}, u32[]{:S(2)}) collective-permute-start(bf16[64,256]{1,0:T(8,128)(2,1)S(1)} %get-tuple-element.82), channel_id=1, source_target_pairs={{0,1},{1,0},{2,3},{3,2},{4,5},{5,4},{6,7},{7,6},{8,9},{9,8},{10,11... | collective-permute-start | bytes 98312 | tf_op jit(solution)/shard_map/ppermute | solution.py:54
  59.8 4.8 %collective-permute-start.3 = (bf16[64,256]{1,0:T(8,128)(2,1)S(1)}, bf16[64,256]{1,0:T(8,128)(2,1)S(1)}, u32[]{:S(2)}, u32[]{:S(2)}) collective-permute-start(bf16[64,256]{1,0:T(8,128)(2,1)S(1)} %get-tuple-element.81), channel_id=1, source_target_pairs={{0,2},{2,4},{4,6},{6,8},{8,10},{10,12},{12,14},{14,16},{16,18},{18... | collective-permute-start | bytes 98312 | tf_op jit(solution)/shard_map/ppermute | solution.py:52
  63.3 5.1 %collective-permute-start.4 = (bf16[64,256]{1,0:T(8,128)(2,1)S(1)}, bf16[64,256]{1,0:T(8,128)(2,1)S(1)}, u32[]{:S(2)}, u32[]{:S(2)}) collective-permute-start(bf16[64,256]{1,0:T(8,128)(2,1)S(1)} %get-tuple-element.83), channel_id=1, source_target_pairs={{2,0},{4,2},{6,4},{8,6},{10,8},{12,10},{14,12},{16,14},{18,16},{20... | collective-permute-start | bytes 98312 | tf_op jit(solution)/shard_map/ppermute | solution.py:53
  96.0 22.2 %all-to-all-start.3 = ((bf16[16,256,128]{2,1,0:T(8,128)(2,1)}), bf16[16,256,128]{2,1,0:T(8,128)(2,1)}, u32[]{:S(2)}, u32[]{:S(2)}) async-start(bf16[16,256,128]{2,1,0:T(8,128)(2,1)} %broadcast_in_dim.144), calls=%async_computation.3 | async-start | bytes 2097152 | tf_op jit(solution)/shard_map/all_to_all | solution.py:17
  125.6 9.2 %collective-permute-start.7 = (bf16[64,256]{1,0:T(8,128)(2,1)S(1)}, bf16[64,256]{1,0:T(8,128)(2,1)S(1)}, u32[]{:S(2)}, u32[]{:S(2)}) collective-permute-start(bf16[64,256]{1,0:T(8,128)(2,1)S(1)} %get-tuple-element.78), channel_id=1, source_target_pairs={{0,2},{2,4},{4,6},{6,8},{8,10},{10,12},{12,14},{14,16},{16,18},{18... | collective-permute-start | bytes 98312 | tf_op jit(solution)/shard_map/ppermute | solution.py:52
  128.0 6.8 %collective-permute-start.9 = (bf16[64,256]{1,0:T(8,128)(2,1)S(1)}, bf16[64,256]{1,0:T(8,128)(2,1)S(1)}, u32[]{:S(2)}, u32[]{:S(2)}) collective-permute-start(bf16[64,256]{1,0:T(8,128)(2,1)S(1)} %get-tuple-element.79), channel_id=1, source_target_pairs={{0,1},{1,0},{2,3},{3,2},{4,5},{5,4},{6,7},{7,6},{8,9},{9,8},{10,11... | collective-permute-start | bytes 98312 | tf_op jit(solution)/shard_map/ppermute | solution.py:54
  133.4 4.7 %collective-permute-start.8 = (bf16[64,256]{1,0:T(8,128)(2,1)S(1)}, bf16[64,256]{1,0:T(8,128)(2,1)S(1)}, u32[]{:S(2)}, u32[]{:S(2)}) collective-permute-start(bf16[64,256]{1,0:T(8,128)(2,1)S(1)} %get-tuple-element.80), channel_id=1, source_target_pairs={{2,0},{4,2},{6,4},{8,6},{10,8},{12,10},{14,12},{16,14},{18,16},{20... | collective-permute-start | bytes 98312 | tf_op jit(solution)/shard_map/ppermute | solution.py:53
  163.7 20.7 %all-to-all-start.5 = ((bf16[16,264,128]{2,1,0:T(8,128)(2,1)}), bf16[16,264,128]{2,1,0:T(8,128)(2,1)}, u32[]{:S(2)}, u32[]{:S(2)}) async-start(bf16[16,264,128]{2,1,0:T(8,128)(2,1)} %broadcast_in_dim.147), calls=%async_computation.5 | async-start | bytes 2162688 | tf_op jit(solution)/shard_map/all_to_all | solution.py:17
  186.2 7.0 %collective-permute-start.10 = (f32[40,128]{1,0:T(8,128)S(1)}, f32[40,128]{1,0:T(8,128)S(1)}, u32[]{:S(2)}, u32[]{:S(2)}) collective-permute-start(f32[40,128]{1,0:T(8,128)S(1)} %coarse_product.3), channel_id=1, source_target_pairs={{0,1},{1,0},{2,3},{3,2},{4,5},{5,4},{6,7},{7,6},{8,9},{9,8},{10,11... | collective-permute-start | bytes 61448 | tf_op jit(solution)/shard_map/ppermute | solution.py:171
  195.7 16.5 %all-to-all-start.6 = ((bf16[16,24,128]{2,1,0:T(8,128)(2,1)}), bf16[16,24,128]{2,1,0:T(8,128)(2,1)S(1)}, u32[]{:S(2)}, u32[]{:S(2)}) async-start(bf16[16,24,128]{2,1,0:T(8,128)(2,1)} %broadcast_in_dim.148), calls=%async_computation.6 | async-start | bytes 196608 | tf_op jit(solution)/shard_map/all_to_all | solution.py:17
  213.5 18.6 %all-to-all-start.7 = ((bf16[16,264,128]{2,1,0:T(8,128)(2,1)}), bf16[16,264,128]{2,1,0:T(8,128)(2,1)S(1)}, u32[]{:S(2)}, u32[]{:S(2)}) async-start(bf16[16,264,128]{2,1,0:T(8,128)(2,1)} %broadcast_in_dim.149), calls=%async_computation.7 | async-start | bytes 2162688 | tf_op jit(solution)/shard_map/all_to_all | solution.py:17
  218.6 9.9 %collective-permute-start.14 = (bf16[64,256]{1,0:T(8,128)(2,1)S(1)}, bf16[64,256]{1,0:T(8,128)(2,1)S(1)}, u32[]{:S(2)}, u32[]{:S(2)}) collective-permute-start(bf16[64,256]{1,0:T(8,128)(2,1)S(1)} %get-tuple-element.76), channel_id=1, source_target_pairs={{0,1},{1,0},{2,3},{3,2},{4,5},{5,4},{6,7},{7,6},{8,9},{9,8},{10,11... | collective-permute-start | bytes 98312 | tf_op jit(solution)/shard_map/ppermute | solution.py:54
  223.2 14.3 %collective-permute-start.12 = (bf16[64,256]{1,0:T(8,128)(2,1)}, bf16[64,256]{1,0:T(8,128)(2,1)}, u32[]{:S(2)}, u32[]{:S(2)}) collective-permute-start(bf16[64,256]{1,0:T(8,128)(2,1)} %get-tuple-element.75), channel_id=1, source_target_pairs={{0,2},{2,4},{4,6},{6,8},{8,10},{10,12},{12,14},{14,16},{16,18},{18... | collective-permute-start | bytes 98312 | tf_op jit(solution)/shard_map/ppermute | solution.py:52
  227.3 10.3 %collective-permute-start.13 = (bf16[64,256]{1,0:T(8,128)(2,1)}, bf16[64,256]{1,0:T(8,128)(2,1)}, u32[]{:S(2)}, u32[]{:S(2)}) collective-permute-start(bf16[64,256]{1,0:T(8,128)(2,1)} %get-tuple-element.77), channel_id=1, source_target_pairs={{2,0},{4,2},{6,4},{8,6},{10,8},{12,10},{14,12},{16,14},{18,16},{20... | collective-permute-start | bytes 98312 | tf_op jit(solution)/shard_map/ppermute | solution.py:53
  232.1 6.9 %collective-permute-start.11 = (f32[1,128]{1,0:T(1,128)S(1)}, f32[1,128]{1,0:T(1,128)S(1)}, u32[]{:S(2)}, u32[]{:S(2)}) collective-permute-start(f32[1,128]{1,0:T(1,128)S(1)} %bitcast.145), channel_id=1, source_target_pairs={{0,1},{1,0},{2,3},{3,2},{4,5},{5,4},{6,7},{7,6},{8,9},{9,8},{10,11... | collective-permute-start | bytes 1544 | tf_op jit(solution)/shard_map/ppermute | solution.py:171
  258.3 17.1 %all-to-all-start.9 = ((f32[16,1,64]{2,1,0:T(1,128)}), f32[16,1,64]{2,1,0:T(1,128)S(1)}, u32[]{:S(2)}, u32[]{:S(2)}) async-start(f32[16,1,64]{2,1,0:T(1,128)} %broadcast_in_dim.153), calls=%async_computation.9 | async-start | bytes 16384 | tf_op jit(solution)/shard_map/all_to_all | solution.py:17
  264.1 12.4 %collective-permute-start.15 = (bf16[64,256]{1,0:T(8,128)(2,1)S(1)}, bf16[64,256]{1,0:T(8,128)(2,1)S(1)}, u32[]{:S(2)}, u32[]{:S(2)}) collective-permute-start(bf16[64,256]{1,0:T(8,128)(2,1)S(1)} %get-tuple-element.72), channel_id=1, source_target_pairs={{0,2},{2,4},{4,6},{6,8},{8,10},{10,12},{12,14},{14,16},{16,18},{18... | collective-permute-start | bytes 98312 | tf_op jit(solution)/shard_map/ppermute | solution.py:52
  266.3 10.2 %collective-permute-start.17 = (bf16[64,256]{1,0:T(8,128)(2,1)S(1)}, bf16[64,256]{1,0:T(8,128)(2,1)S(1)}, u32[]{:S(2)}, u32[]{:S(2)}) collective-permute-start(bf16[64,256]{1,0:T(8,128)(2,1)S(1)} %get-tuple-element.73), channel_id=1, source_target_pairs={{0,1},{1,0},{2,3},{3,2},{4,5},{5,4},{6,7},{7,6},{8,9},{9,8},{10,11... | collective-permute-start | bytes 98312 | tf_op jit(solution)/shard_map/ppermute | solution.py:54
  269.4 7.1 %collective-permute-start.16 = (bf16[64,256]{1,0:T(8,128)(2,1)S(1)}, bf16[64,256]{1,0:T(8,128)(2,1)S(1)}, u32[]{:S(2)}, u32[]{:S(2)}) collective-permute-start(bf16[64,256]{1,0:T(8,128)(2,1)S(1)} %get-tuple-element.74), channel_id=1, source_target_pairs={{2,0},{4,2},{6,4},{8,6},{10,8},{12,10},{14,12},{16,14},{18,16},{20... | collective-permute-start | bytes 98312 | tf_op jit(solution)/shard_map/ppermute | solution.py:53
  (37 other events, 506.6 us)

commit v7 on v6

--- a/solution.py
+++ b/solution.py
@@ -246,7 +246,7 @@
         in_specs=[pl.BlockSpec(memory_space=pltpu.SMEM)] + [in_vmem] * (1 + len(rest)),
         out_specs=(in_vmem,) * 3,
         interpret=INTERPRET,
-        compiler_params=pltpu.CompilerParams(vmem_limit_bytes=8 << 20),
+        compiler_params=pltpu.CompilerParams(vmem_limit_bytes=(56 if previous else 8) << 20),
         name="next_direction",
     )(info, blocks, *rest)
 
@@ -318,15 +318,15 @@
     info = jnp.stack([place(owner), place(owner + 1), base - 32 * owner, count_of], axis=1)
     info = info.reshape(-1).astype(jnp.int32)
 
-    stage, padded, info, rounded = lax.optimization_barrier((stage, padded, info, rounded))
+    stage, padded, info = lax.optimization_barrier((stage, padded, info))
+    first_sums = swapped_sum(coarse_product(padded, across(stage)))
+    half_slots = first_sums.shape[0] // 2
+    stage = along_z(first_sums[:half_slots].astype(jnp.bfloat16))
+    stage, rounded = lax.optimization_barrier((stage, rounded))
     smoothed = smooth(rounded)
     near_smoothed = neighbours(smoothed)
-    blocks, near_smoothed = lax.optimization_barrier((across(stage), near_smoothed))
-    first_sums = swapped_sum(coarse_product(padded, blocks))
-    half_slots = first_sums.shape[0] // 2
-    values = across(along_z(first_sums[:half_slots].astype(jnp.bfloat16)))
     direction, near_direction, moved = next_direction(
-        info, values, mode_block, near_modes, smoothed, near_smoothed, exists
+        info, across(stage), mode_block, near_modes, smoothed, near_smoothed, exists
     )
 
     pushed = apply_flex(moved)
@@ -344,9 +344,8 @@
     image_low = (image - image_high).astype(jnp.bfloat16)
     image_weights = weigh(image_high.astype(jnp.bfloat16)) + weigh(image_low)
     payload = jnp.concatenate([pack(image_weights.astype(jnp.bfloat16)), pieces], axis=0)
-    stage, late_pushed, late_near = lax.optimization_barrier(
-        (summed_along_z(payload), pushed, near_pushed)
-    )
+    products = coarse_product(padded, across(summed_along_z(payload)))
+    products, late_pushed, late_near = lax.optimization_barrier((products, pushed, near_pushed))
     late_image = difference(late_pushed, late_near)
     image_smoothed = smooth(late_image.astype(jnp.bfloat16))
     residual_jump, image_jump = residual * factor, late_image * factor
@@ -355,8 +354,7 @@
         load_dot(residual_jump, image_smoothed) + load_dot(image_jump, smoothed),
         load_dot(image_jump, image_smoothed),
     )
-    blocks, energies = lax.optimization_barrier((across(stage), energies))
-    second_sums = swapped_sum(coarse_product(padded, blocks))
+    second_sums = swapped_sum(products)
     totals = jnp.sum(second_sums[2 * half_slots :], axis=0)
     energy = totals[:64]
     size = energy / totals[64:]

time: 281 us -> 273 us (0.972)
  blocking collectives: 49.4 us -> 69.8 us
  waiting for transfers between devices: 52.7 us -> 42.1 us
  starting transfers between devices: 110 us -> 104 us
  local copies, waits for them, and re-layouts: 23.9 us -> 18.3 us
  other arithmetic: 13.7 us -> 10.7 us
    all_to_all x3 -> x4, blocking collectives: 49.4 us -> 69.8 us  [spread(): return lax.all_to_all(copies, axes, 0, 0, tiled=False)]
    all_to_all x7 -> x6, waiting for transfers between devices: 43.6 us -> 32.9 us  [spread(): return lax.all_to_all(copies, axes, 0, 0, tiled=False)]
    all_to_all x7 -> x6, starting transfers between devices: 48.4 us -> 42 us  [spread(): return lax.all_to_all(copies, axes, 0, 0, tiled=False)]
    unnamed x76, local copies, waits for them, and re-layouts: 11.7 us -> 6.02 us
    ppermute x5, starting transfers between devices: 24.5 us -> 20.2 us  [neighbours(): lax.ppermute(jnp.where(column == 0, east, west), 'c', [(0, 1), (1, 0)])]
    ppermute x3, starting transfers between devices: 14.9 us -> 18.5 us  [swapped_sum(): return partial + lax.ppermute(partial, 'c', [(0, 1), (1, 0)])]
  transfers between devices with their start and end apart: 25 -> 24, of which waited for: 11 -> 10; matrix products, arithmetic and copies ran while one was open for 6% -> 5% of each run, Pallas kernels for 2% -> 2%
where the time goes in v7:
time: 273 us; the launch traced here: 270 us
  starting transfers between devices  104 us (38%)
  blocking collectives  69.8 us (26%)
  waiting for transfers between devices  42.1 us (15%)
  local copies, waits for them, and re-layouts  18.3 us (7%)
  Pallas kernels  13.3 us (5%)
  other arithmetic  10.7 us (4%)
  matrix products  9.78 us (4%)
    all_to_all x4, blocking collectives, spread(): return lax.all_to_all(copies, axes, 0, 0, tiled=False)  69.8 us
    all_to_all x6, starting transfers between devices, spread(): return lax.all_to_all(copies, axes, 0, 0, tiled=False)  42 us
    all_to_all x6, waiting for transfers between devices, spread(): return lax.all_to_all(copies, axes, 0, 0, tiled=False)  32.9 us
    ppermute x5, starting transfers between devices, neighbours(): lax.ppermute(jnp.where(column == 0, east, west), 'c', [(0, 1), (1, 0)])  20.2 us
    ppermute x3, starting transfers between devices, swapped_sum(): return partial + lax.ppermute(partial, 'c', [(0, 1), (1, 0)])  18.5 us
    ppermute x5, starting transfers between devices, neighbours(): from_above = lax.ppermute(south, WIDE, down)  17 us
    broadcast_in_dim x10, local copies, waits for them, and re-layouts, spread(): copies = jnp.broadcast_to(values[None], (count,) + values.shape)  6.95 us
    pallas_call x1, Pallas kernels, padded_inverse(): pl.pallas_call(pad_kernel, out_shape=jax.ShapeDtypeStruct((4 * rows, subd...  6.45 us
  transfers between devices with their start and end apart: 24, of which 10 were waited for; matrix products, arithmetic and copies ran while one was open for 5% of the time, Pallas kernels for 2%

profile of v7, /device:TPU:1, one launch (start us, length us, event | category | flops | bytes accessed | tf_op | source)
XLA Modules:
  0.0 269.6 jit_solution(13636095676717924054)
XLA Ops:
  3.7 4.0 %collective-permute-start = (bf16[96,256]{1,0:T(8,128)(2,1)S(1)}, bf16[96,256]{1,0:T(8,128)(2,1)S(1)}, u32[]{:S(2)}, u32[]{:S(2)}) collective-permute-start(bf16[96,256]{1,0:T(8,128)(2,1)S(1)} %get-tuple-element.59), channel_id=1, source_target_pairs={{0,2},{2,4},{4,6},{6,8},{8,10},{10,12},{12,14},{14,16},{16,18},{18... | collective-permute-start | bytes 147464 | tf_op jit(solution)/shard_map/ppermute | solution.py:52
  9.0 6.0 %collective-permute-start.2 = (bf16[96,256]{1,0:T(8,128)(2,1)S(1)}, bf16[96,256]{1,0:T(8,128)(2,1)S(1)}, u32[]{:S(2)}, u32[]{:S(2)}) collective-permute-start(bf16[96,256]{1,0:T(8,128)(2,1)S(1)} %get-tuple-element.61), channel_id=1, source_target_pairs={{0,1},{1,0},{2,3},{3,2},{4,5},{5,4},{6,7},{7,6},{8,9},{9,8},{10,11... | collective-permute-start | bytes 147464 | tf_op jit(solution)/shard_map/ppermute | solution.py:54
  19.0 16.2 %all-to-all-start = ((bf16[16,16,128]{2,1,0:T(8,128)(2,1)}), bf16[16,16,128]{2,1,0:T(8,128)(2,1)}, u32[]{:S(2)}, u32[]{:S(2)}) async-start(bf16[16,16,128]{2,1,0:T(8,128)(2,1)} %broadcast_in_dim.67), calls=%async_computation | async-start | bytes 131072 | tf_op jit(solution)/shard_map/all_to_all | solution.py:17
  36.3 6.5 %pad_inverse.1.padded_ref = bf16[128,4096]{1,0:T(8,128)(2,1)S(1)} custom-call(s32[33]{0:T(128)S(1)} %pad_add_fusion.1.first_ref, s32[2,32,1,128]{3,2,1,0:T(1,128)S(1)} %compare_select_fusion.source_ref, bf16[32,4096]{1,0:T(8,128)(2,1)S(1)} %copy-done.8), custom_call_target="tpu_custom_call" | custom-call | tf_op jit(solution)/shard_map/pad_inverse/pallas_call | solution.py:106
  42.7 4.2 %all-to-all-done = bf16[16,16,128]{2,1,0:T(8,128)(2,1)} async-done(((bf16[16,16,128]{2,1,0:T(8,128)(2,1)}), bf16[16,16,128]{2,1,0:T(8,128)(2,1)}, u32[]{:S(2)}, u32[]{:S(2)}) %all-to-all-start) | async-done | bytes 65568 | tf_op jit(solution)/shard_map/all_to_all | solution.py:17
  47.9 17.1 %all_to_all.50.blocks_ref = bf16[16,256,128]{2,1,0:T(8,128)(2,1)S(1)} all-to-all(bf16[16,256,128]{2,1,0:T(8,128)(2,1)S(1)} %broadcast_in_dim.73), channel_id=1, replica_groups=mesh['x'=4,'z'=16,'y'=4,'c'=2] {'x','y'}, dimensions={0} | all-to-all | bytes 2097152 | tf_op jit(solution)/shard_map/all_to_all | solution.py:17
  65.6 6.8 %collective-permute-start.3 = (f32[32,128]{1,0:T(8,128)S(1)}, f32[32,128]{1,0:T(8,128)S(1)}, u32[]{:S(2)}, u32[]{:S(2)}) collective-permute-start(f32[32,128]{1,0:T(8,128)S(1)} %coarse_product.2), channel_id=1, source_target_pairs={{0,1},{1,0},{2,3},{3,2},{4,5},{5,4},{6,7},{7,6},{8,9},{9,8},{10,11... | collective-permute-start | bytes 49160 | tf_op jit(solution)/shard_map/ppermute | solution.py:171
  73.9 7.3 %all-to-all-start.2 = ((bf16[16,16,128]{2,1,0:T(8,128)(2,1)}), bf16[16,16,128]{2,1,0:T(8,128)(2,1)S(1)}, u32[]{:S(2)}, u32[]{:S(2)}) async-start(bf16[16,16,128]{2,1,0:T(8,128)(2,1)} %broadcast_in_dim.74), calls=%async_computation.2 | async-start | bytes 131072 | tf_op jit(solution)/shard_map/all_to_all | solution.py:17
  81.3 11.5 %all-to-all-done.2 = bf16[16,16,128]{2,1,0:T(8,128)(2,1)S(1)} async-done(((bf16[16,16,128]{2,1,0:T(8,128)(2,1)}), bf16[16,16,128]{2,1,0:T(8,128)(2,1)S(1)}, u32[]{:S(2)}, u32[]{:S(2)}) %all-to-all-start.2) | async-done | bytes 65568 | tf_op jit(solution)/shard_map/all_to_all | solution.py:17
  94.0 4.5 %all-to-all-start.3 = ((bf16[16,256,128]{2,1,0:T(8,128)(2,1)}), bf16[16,256,128]{2,1,0:T(8,128)(2,1)}, u32[]{:S(2)}, u32[]{:S(2)}) async-start(bf16[16,256,128]{2,1,0:T(8,128)(2,1)} %broadcast_in_dim.75), calls=%async_computation.3 | async-start | bytes 2097152 | tf_op jit(solution)/shard_map/all_to_all | solution.py:17
  100.7 3.9 %collective-permute-start.6 = (bf16[64,256]{1,0:T(8,128)(2,1)S(1)}, bf16[64,256]{1,0:T(8,128)(2,1)S(1)}, u32[]{:S(2)}, u32[]{:S(2)}) collective-permute-start(bf16[64,256]{1,0:T(8,128)(2,1)S(1)} %get-tuple-element.72), channel_id=1, source_target_pairs={{0,1},{1,0},{2,3},{3,2},{4,5},{5,4},{6,7},{7,6},{8,9},{9,8},{10,11... | collective-permute-start | bytes 98312 | tf_op jit(solution)/shard_map/ppermute | solution.py:54
  134.1 18.7 %all_to_all.51 = bf16[16,24,128]{2,1,0:T(8,128)(2,1)S(1)} all-to-all(bf16[16,24,128]{2,1,0:T(8,128)(2,1)S(1)} %broadcast_in_dim.144), channel_id=1, replica_groups=mesh['x'=4,'z'=16,'y'=4,'c'=2] {'z'}, dimensions={0} | all-to-all | bytes 196608 | tf_op jit(solution)/shard_map/all_to_all | solution.py:17
  157.7 23.5 %all_to_all.52.blocks_ref = bf16[16,264,128]{2,1,0:T(8,128)(2,1)S(1)} all-to-all(bf16[16,264,128]{2,1,0:T(8,128)(2,1)S(1)} %broadcast_in_dim.145), channel_id=1, replica_groups=mesh['x'=4,'z'=16,'y'=4,'c'=2] {'x','y'}, dimensions={0} | all-to-all | bytes 2162688 | tf_op jit(solution)/shard_map/all_to_all | solution.py:17
  181.8 6.3 %collective-permute-start.10 = (f32[40,128]{1,0:T(8,128)S(1)}, f32[40,128]{1,0:T(8,128)S(1)}, u32[]{:S(2)}, u32[]{:S(2)}) collective-permute-start(f32[40,128]{1,0:T(8,128)S(1)} %coarse_product.3), channel_id=1, source_target_pairs={{0,1},{1,0},{2,3},{3,2},{4,5},{5,4},{6,7},{7,6},{8,9},{9,8},{10,11... | collective-permute-start | bytes 61448 | tf_op jit(solution)/shard_map/ppermute | solution.py:171
  190.0 4.6 %all-to-all-start.6 = ((bf16[16,24,128]{2,1,0:T(8,128)(2,1)}), bf16[16,24,128]{2,1,0:T(8,128)(2,1)S(1)}, u32[]{:S(2)}, u32[]{:S(2)}) async-start(bf16[16,24,128]{2,1,0:T(8,128)(2,1)} %broadcast_in_dim.146), calls=%async_computation.6 | async-start | bytes 196608 | tf_op jit(solution)/shard_map/all_to_all | solution.py:17
  197.4 9.1 %all-to-all-done.6 = bf16[16,24,128]{2,1,0:T(8,128)(2,1)S(1)} async-done(((bf16[16,24,128]{2,1,0:T(8,128)(2,1)}), bf16[16,24,128]{2,1,0:T(8,128)(2,1)S(1)}, u32[]{:S(2)}, u32[]{:S(2)}) %all-to-all-start.6) | async-done | bytes 98336 | tf_op jit(solution)/shard_map/all_to_all | solution.py:17
  207.7 3.7 %all-to-all-start.7 = ((bf16[16,264,128]{2,1,0:T(8,128)(2,1)}), bf16[16,264,128]{2,1,0:T(8,128)(2,1)S(1)}, u32[]{:S(2)}, u32[]{:S(2)}) async-start(bf16[16,264,128]{2,1,0:T(8,128)(2,1)} %broadcast_in_dim.147), calls=%async_computation.7 | async-start | bytes 2162688 | tf_op jit(solution)/shard_map/all_to_all | solution.py:17
  212.8 4.6 %collective-permute-start.14 = (bf16[64,256]{1,0:T(8,128)(2,1)S(1)}, bf16[64,256]{1,0:T(8,128)(2,1)S(1)}, u32[]{:S(2)}, u32[]{:S(2)}) collective-permute-start(bf16[64,256]{1,0:T(8,128)(2,1)S(1)} %get-tuple-element.66), channel_id=1, source_target_pairs={{0,1},{1,0},{2,3},{3,2},{4,5},{5,4},{6,7},{7,6},{8,9},{9,8},{10,11... | collective-permute-start | bytes 98312 | tf_op jit(solution)/shard_map/ppermute | solution.py:54
  217.4 4.0 %collective-permute-start.12 = (bf16[64,256]{1,0:T(8,128)(2,1)}, bf16[64,256]{1,0:T(8,128)(2,1)}, u32[]{:S(2)}, u32[]{:S(2)}) collective-permute-start(bf16[64,256]{1,0:T(8,128)(2,1)} %get-tuple-element.65), channel_id=1, source_target_pairs={{0,2},{2,4},{4,6},{6,8},{8,10},{10,12},{12,14},{14,16},{16,18},{18... | collective-permute-start | bytes 98312 | tf_op jit(solution)/shard_map/ppermute | solution.py:52
  222.8 3.5 %all-to-all-done.7.blocks_ref = bf16[16,264,128]{2,1,0:T(8,128)(2,1)S(1)} async-done(((bf16[16,264,128]{2,1,0:T(8,128)(2,1)}), bf16[16,264,128]{2,1,0:T(8,128)(2,1)S(1)}, u32[]{:S(2)}, u32[]{:S(2)}) %all-to-all-start.7) | async-done | bytes 1081376 | tf_op jit(solution)/shard_map/all_to_all | solution.py:17
  226.3 5.4 %collective-permute-start.11 = (f32[1,128]{1,0:T(1,128)S(1)}, f32[1,128]{1,0:T(1,128)S(1)}, u32[]{:S(2)}, u32[]{:S(2)}) collective-permute-start(f32[1,128]{1,0:T(1,128)S(1)} %bitcast.144), channel_id=1, source_target_pairs={{0,1},{1,0},{2,3},{3,2},{4,5},{5,4},{6,7},{7,6},{8,9},{9,8},{10,11... | collective-permute-start | bytes 1544 | tf_op jit(solution)/shard_map/ppermute | solution.py:171
  239.0 10.6 %all_to_all.53 = f32[32,1,64]{2,1,0:T(1,128)S(1)} all-to-all(f32[32,1,64]{2,1,0:T(1,128)S(1)} %broadcast_in_dim.150), channel_id=1, replica_groups=mesh['x'=4,'z'=16,'y'=4,'c'=2] {'x','y','c'}, dimensions={0} | all-to-all | bytes 16384 | tf_op jit(solution)/shard_map/all_to_all | solution.py:17
  250.2 5.8 %all-to-all-start.9 = ((f32[16,1,64]{2,1,0:T(1,128)}), f32[16,1,64]{2,1,0:T(1,128)S(1)}, u32[]{:S(2)}, u32[]{:S(2)}) async-start(f32[16,1,64]{2,1,0:T(1,128)} %broadcast_in_dim.151), calls=%async_computation.9 | async-start | bytes 16384 | tf_op jit(solution)/shard_map/all_to_all | solution.py:17
  262.6 4.6 %all-to-all-done.9 = f32[16,1,64]{2,1,0:T(1,128)S(1)} async-done(((f32[16,1,64]{2,1,0:T(1,128)}), f32[16,1,64]{2,1,0:T(1,128)S(1)}, u32[]{:S(2)}, u32[]{:S(2)}) %all-to-all-start.9) | async-done | bytes 4128 | tf_op jit(solution)/shard_map/all_to_all | solution.py:17
  (215 shorter events, 75.8 us)
Async XLA Ops:
  3.7 12.3 %collective-permute-start = (bf16[96,256]{1,0:T(8,128)(2,1)S(1)}, bf16[96,256]{1,0:T(8,128)(2,1)S(1)}, u32[]{:S(2)}, u32[]{:S(2)}) collective-permute-start(bf16[96,256]{1,0:T(8,128)(2,1)S(1)} %get-tuple-element.59), channel_id=1, source_target_pairs={{0,2},{2,4},{4,6},{6,8},{8,10},{10,12},{12,14},{14,16},{16,18},{18... | collective-permute-start | bytes 147464 | tf_op jit(solution)/shard_map/ppermute | solution.py:52
  7.7 8.2 %collective-permute-start.1 = (bf16[96,256]{1,0:T(8,128)(2,1)S(1)}, bf16[96,256]{1,0:T(8,128)(2,1)S(1)}, u32[]{:S(2)}, u32[]{:S(2)}) collective-permute-start(bf16[96,256]{1,0:T(8,128)(2,1)S(1)} %get-tuple-element.60), channel_id=1, source_target_pairs={{2,0},{4,2},{6,4},{8,6},{10,8},{12,10},{14,12},{16,14},{18,16},{20... | collective-permute-start | bytes 147464 | tf_op jit(solution)/shard_map/ppermute | solution.py:53
  9.0 6.9 %collective-permute-start.2 = (bf16[96,256]{1,0:T(8,128)(2,1)S(1)}, bf16[96,256]{1,0:T(8,128)(2,1)S(1)}, u32[]{:S(2)}, u32[]{:S(2)}) collective-permute-start(bf16[96,256]{1,0:T(8,128)(2,1)S(1)} %get-tuple-element.61), channel_id=1, source_target_pairs={{0,1},{1,0},{2,3},{3,2},{4,5},{5,4},{6,7},{7,6},{8,9},{9,8},{10,11... | collective-permute-start | bytes 147464 | tf_op jit(solution)/shard_map/ppermute | solution.py:54
  19.0 27.9 %all-to-all-start = ((bf16[16,16,128]{2,1,0:T(8,128)(2,1)}), bf16[16,16,128]{2,1,0:T(8,128)(2,1)}, u32[]{:S(2)}, u32[]{:S(2)}) async-start(bf16[16,16,128]{2,1,0:T(8,128)(2,1)} %broadcast_in_dim.67), calls=%async_computation | async-start | bytes 131072 | tf_op jit(solution)/shard_map/all_to_all | solution.py:17
  65.6 7.7 %collective-permute-start.3 = (f32[32,128]{1,0:T(8,128)S(1)}, f32[32,128]{1,0:T(8,128)S(1)}, u32[]{:S(2)}, u32[]{:S(2)}) collective-permute-start(f32[32,128]{1,0:T(8,128)S(1)} %coarse_product.2), channel_id=1, source_target_pairs={{0,1},{1,0},{2,3},{3,2},{4,5},{5,4},{6,7},{7,6},{8,9},{9,8},{10,11... | collective-permute-start | bytes 49160 | tf_op jit(solution)/shard_map/ppermute | solution.py:171
  73.9 18.9 %all-to-all-start.2 = ((bf16[16,16,128]{2,1,0:T(8,128)(2,1)}), bf16[16,16,128]{2,1,0:T(8,128)(2,1)S(1)}, u32[]{:S(2)}, u32[]{:S(2)}) async-start(bf16[16,16,128]{2,1,0:T(8,128)(2,1)} %broadcast_in_dim.74), calls=%async_computation.2 | async-start | bytes 131072 | tf_op jit(solution)/shard_map/all_to_all | solution.py:17
  94.0 21.3 %all-to-all-start.3 = ((bf16[16,256,128]{2,1,0:T(8,128)(2,1)}), bf16[16,256,128]{2,1,0:T(8,128)(2,1)}, u32[]{:S(2)}, u32[]{:S(2)}) async-start(bf16[16,256,128]{2,1,0:T(8,128)(2,1)} %broadcast_in_dim.75), calls=%async_computation.3 | async-start | bytes 2097152 | tf_op jit(solution)/shard_map/all_to_all | solution.py:17
  100.7 9.3 %collective-permute-start.6 = (bf16[64,256]{1,0:T(8,128)(2,1)S(1)}, bf16[64,256]{1,0:T(8,128)(2,1)S(1)}, u32[]{:S(2)}, u32[]{:S(2)}) collective-permute-start(bf16[64,256]{1,0:T(8,128)(2,1)S(1)} %get-tuple-element.72), channel_id=1, source_target_pairs={{0,1},{1,0},{2,3},{3,2},{4,5},{5,4},{6,7},{7,6},{8,9},{9,8},{10,11... | collective-permute-start | bytes 98312 | tf_op jit(solution)/shard_map/ppermute | solution.py:54
  105.4 6.1 %collective-permute-start.4 = (bf16[64,256]{1,0:T(8,128)(2,1)S(1)}, bf16[64,256]{1,0:T(8,128)(2,1)S(1)}, u32[]{:S(2)}, u32[]{:S(2)}) collective-permute-start(bf16[64,256]{1,0:T(8,128)(2,1)S(1)} %get-tuple-element.71), channel_id=1, source_target_pairs={{0,2},{2,4},{4,6},{6,8},{8,10},{10,12},{12,14},{14,16},{16,18},{18... | collective-permute-start | bytes 98312 | tf_op jit(solution)/shard_map/ppermute | solution.py:52
  108.7 5.9 %collective-permute-start.5 = (bf16[64,256]{1,0:T(8,128)(2,1)S(1)}, bf16[64,256]{1,0:T(8,128)(2,1)S(1)}, u32[]{:S(2)}, u32[]{:S(2)}) collective-permute-start(bf16[64,256]{1,0:T(8,128)(2,1)S(1)} %get-tuple-element.73), channel_id=1, source_target_pairs={{2,0},{4,2},{6,4},{8,6},{10,8},{12,10},{14,12},{16,14},{18,16},{20... | collective-permute-start | bytes 98312 | tf_op jit(solution)/shard_map/ppermute | solution.py:53
  122.7 7.3 %collective-permute-start.7 = (bf16[64,256]{1,0:T(8,128)(2,1)S(1)}, bf16[64,256]{1,0:T(8,128)(2,1)S(1)}, u32[]{:S(2)}, u32[]{:S(2)}) collective-permute-start(bf16[64,256]{1,0:T(8,128)(2,1)S(1)} %get-tuple-element.68), channel_id=1, source_target_pairs={{0,2},{2,4},{4,6},{6,8},{8,10},{10,12},{12,14},{14,16},{16,18},{18... | collective-permute-start | bytes 98312 | tf_op jit(solution)/shard_map/ppermute | solution.py:52
  126.2 3.8 %collective-permute-start.9 = (bf16[64,256]{1,0:T(8,128)(2,1)S(1)}, bf16[64,256]{1,0:T(8,128)(2,1)S(1)}, u32[]{:S(2)}, u32[]{:S(2)}) collective-permute-start(bf16[64,256]{1,0:T(8,128)(2,1)S(1)} %get-tuple-element.69), channel_id=1, source_target_pairs={{0,1},{1,0},{2,3},{3,2},{4,5},{5,4},{6,7},{7,6},{8,9},{9,8},{10,11... | collective-permute-start | bytes 98312 | tf_op jit(solution)/shard_map/ppermute | solution.py:54
  128.7 4.7 %collective-permute-start.8 = (bf16[64,256]{1,0:T(8,128)(2,1)S(1)}, bf16[64,256]{1,0:T(8,128)(2,1)S(1)}, u32[]{:S(2)}, u32[]{:S(2)}) collective-permute-start(bf16[64,256]{1,0:T(8,128)(2,1)S(1)} %get-tuple-element.70), channel_id=1, source_target_pairs={{2,0},{4,2},{6,4},{8,6},{10,8},{12,10},{14,12},{16,14},{18,16},{20... | collective-permute-start | bytes 98312 | tf_op jit(solution)/shard_map/ppermute | solution.py:53
  181.8 7.2 %collective-permute-start.10 = (f32[40,128]{1,0:T(8,128)S(1)}, f32[40,128]{1,0:T(8,128)S(1)}, u32[]{:S(2)}, u32[]{:S(2)}) collective-permute-start(f32[40,128]{1,0:T(8,128)S(1)} %coarse_product.3), channel_id=1, source_target_pairs={{0,1},{1,0},{2,3},{3,2},{4,5},{5,4},{6,7},{7,6},{8,9},{9,8},{10,11... | collective-permute-start | bytes 61448 | tf_op jit(solution)/shard_map/ppermute | solution.py:171
  190.0 16.5 %all-to-all-start.6 = ((bf16[16,24,128]{2,1,0:T(8,128)(2,1)}), bf16[16,24,128]{2,1,0:T(8,128)(2,1)S(1)}, u32[]{:S(2)}, u32[]{:S(2)}) async-start(bf16[16,24,128]{2,1,0:T(8,128)(2,1)} %broadcast_in_dim.146), calls=%async_computation.6 | async-start | bytes 196608 | tf_op jit(solution)/shard_map/all_to_all | solution.py:17
  207.7 18.6 %all-to-all-start.7 = ((bf16[16,264,128]{2,1,0:T(8,128)(2,1)}), bf16[16,264,128]{2,1,0:T(8,128)(2,1)S(1)}, u32[]{:S(2)}, u32[]{:S(2)}) async-start(bf16[16,264,128]{2,1,0:T(8,128)(2,1)} %broadcast_in_dim.147), calls=%async_computation.7 | async-start | bytes 2162688 | tf_op jit(solution)/shard_map/all_to_all | solution.py:17
  212.8 9.9 %collective-permute-start.14 = (bf16[64,256]{1,0:T(8,128)(2,1)S(1)}, bf16[64,256]{1,0:T(8,128)(2,1)S(1)}, u32[]{:S(2)}, u32[]{:S(2)}) collective-permute-start(bf16[64,256]{1,0:T(8,128)(2,1)S(1)} %get-tuple-element.66), channel_id=1, source_target_pairs={{0,1},{1,0},{2,3},{3,2},{4,5},{5,4},{6,7},{7,6},{8,9},{9,8},{10,11... | collective-permute-start | bytes 98312 | tf_op jit(solution)/shard_map/ppermute | solution.py:54
  217.4 14.3 %collective-permute-start.12 = (bf16[64,256]{1,0:T(8,128)(2,1)}, bf16[64,256]{1,0:T(8,128)(2,1)}, u32[]{:S(2)}, u32[]{:S(2)}) collective-permute-start(bf16[64,256]{1,0:T(8,128)(2,1)} %get-tuple-element.65), channel_id=1, source_target_pairs={{0,2},{2,4},{4,6},{6,8},{8,10},{10,12},{12,14},{14,16},{16,18},{18... | collective-permute-start | bytes 98312 | tf_op jit(solution)/shard_map/ppermute | solution.py:52
  221.4 10.3 %collective-permute-start.13 = (bf16[64,256]{1,0:T(8,128)(2,1)S(1)}, bf16[64,256]{1,0:T(8,128)(2,1)}, u32[]{:S(2)}, u32[]{:S(2)}) collective-permute-start(bf16[64,256]{1,0:T(8,128)(2,1)S(1)} %get-tuple-element.67), channel_id=1, source_target_pairs={{2,0},{4,2},{6,4},{8,6},{10,8},{12,10},{14,12},{16,14},{18,16},{20... | collective-permute-start | bytes 98312 | tf_op jit(solution)/shard_map/ppermute | solution.py:53
  226.3 6.9 %collective-permute-start.11 = (f32[1,128]{1,0:T(1,128)S(1)}, f32[1,128]{1,0:T(1,128)S(1)}, u32[]{:S(2)}, u32[]{:S(2)}) collective-permute-start(f32[1,128]{1,0:T(1,128)S(1)} %bitcast.144), channel_id=1, source_target_pairs={{0,1},{1,0},{2,3},{3,2},{4,5},{5,4},{6,7},{7,6},{8,9},{9,8},{10,11... | collective-permute-start | bytes 1544 | tf_op jit(solution)/shard_map/ppermute | solution.py:171
  250.2 17.1 %all-to-all-start.9 = ((f32[16,1,64]{2,1,0:T(1,128)}), f32[16,1,64]{2,1,0:T(1,128)S(1)}, u32[]{:S(2)}, u32[]{:S(2)}) async-start(f32[16,1,64]{2,1,0:T(1,128)} %broadcast_in_dim.151), calls=%async_computation.9 | async-start | bytes 16384 | tf_op jit(solution)/shard_map/all_to_all | solution.py:17
  256.0 12.7 %collective-permute-start.15 = (bf16[64,256]{1,0:T(8,128)(2,1)S(1)}, bf16[64,256]{1,0:T(8,128)(2,1)S(1)}, u32[]{:S(2)}, u32[]{:S(2)}) collective-permute-start(bf16[64,256]{1,0:T(8,128)(2,1)S(1)} %get-tuple-element.62), channel_id=1, source_target_pairs={{0,2},{2,4},{4,6},{6,8},{8,10},{10,12},{12,14},{14,16},{16,18},{18... | collective-permute-start | bytes 98312 | tf_op jit(solution)/shard_map/ppermute | solution.py:52
  258.2 9.7 %collective-permute-start.17 = (bf16[64,256]{1,0:T(8,128)(2,1)S(1)}, bf16[64,256]{1,0:T(8,128)(2,1)}, u32[]{:S(2)}, u32[]{:S(2)}) collective-permute-start(bf16[64,256]{1,0:T(8,128)(2,1)S(1)} %get-tuple-element.63), channel_id=1, source_target_pairs={{0,1},{1,0},{2,3},{3,2},{4,5},{5,4},{6,7},{7,6},{8,9},{9,8},{10,11... | collective-permute-start | bytes 98312 | tf_op jit(solution)/shard_map/ppermute | solution.py:54
  261.3 7.4 %collective-permute-start.16 = (bf16[64,256]{1,0:T(8,128)(2,1)S(1)}, bf16[64,256]{1,0:T(8,128)(2,1)S(1)}, u32[]{:S(2)}, u32[]{:S(2)}) collective-permute-start(bf16[64,256]{1,0:T(8,128)(2,1)S(1)} %get-tuple-element.64), channel_id=1, source_target_pairs={{2,0},{4,2},{6,4},{8,6},{10,8},{12,10},{14,12},{16,14},{18,16},{20... | collective-permute-start | bytes 98312 | tf_op jit(solution)/shard_map/ppermute | solution.py:53
  (36 other events, 553.0 us)
